TPU v7x, 32 devices: a whole 2x2x4 slice. The times are simulated.
32 devices in a mesh: seq: 4 (over x, core), dp: 8 (over z, y).
Axes of the slice: x: 2, y: 2, z: 4, core: 2. Of those that a mesh axis runs over, the one named last changes fastest.
Arguments:
- tokens: bfloat16 [8, 2048, 768], P('dp', 'seq'), may hold values from -6 to 6
- qkv_weight: bfloat16 [768, 2304], P('dp'), may hold values from -0.21875 to 0.21875
- out_weight: bfloat16 [768, 768], P('dp'), may hold values from -0.625 to 0.625
- up_weight: bfloat16 [768, 3072], P('dp'), may hold values from -0.21875 to 0.21875
- down_weight: bfloat16 [3072, 768], P('dp'), may hold values from -0.109375 to 0.109375
- norm_gain: bfloat16 [768], P('dp'), may hold values from 0.5 to 1.5
- mlp_gain: bfloat16 [768], P('dp'), may hold values from 0.5 to 1.5
- pass_embed: bfloat16 [768], P('dp'), may hold values from -6 to 6
- cotangent: bfloat16 [8, 2048, 768], P('dp', 'seq'), may hold values from -6 to 6
Outputs:
- mixed_out: bfloat16 [8, 2048, 768], P('dp', 'seq')
- input_grad: float32 [8, 2048, 768], P('dp', 'seq')
- qkv_grad: float32 [768, 2304], P('dp')
- output_grad: float32 [768, 768], P('dp')
- up_weight_grad: float32 [768, 3072], P('dp')
- down_weight_grad: float32 [3072, 768], P('dp')
- norm_gain_grad: float32 [768], P('dp')
- mlp_gain_grad: float32 [768], P('dp')
- embed_grad: float32 [768], P('dp')
All inputs are finite; a program needn't handle non-finite values.
Results may differ from a plain program's by a relative error of at most 0.019.
Values may be sent and summed in bfloat16 or wider, within the bound.
A program may use at most 256 MiB of HBM per device.

v0:
```python
import jax
import jax.numpy as jnp
from jax import lax
from jax.sharding import PartitionSpec as P

HEAD_DIM = 64


epsilon = 1e-05


def layer_norm(vector, gain_vec):
    centre = vector - jnp.mean(vector, axis=-1, keepdims=True)
    spread = jnp.mean(centre * centre, axis=-1, keepdims=True)
    return centre * lax.rsqrt(spread + epsilon) * gain_vec


def gelu_value(vector):
    return jax.nn.gelu(vector, approximate=True)


def contract_rows(left_side, right_side):
    return lax.dot_general(
        left_side, right_side, (((0,), (0,)), ((), ())), preferred_element_type=jnp.float32
    )


def contract_cols(left_side, right_side):
    return lax.dot_general(
        left_side, right_side, (((1,), (1,)), ((), ())), preferred_element_type=jnp.float32
    )


def attend_forward(queries, key_rows, value_rows):
    length, local_heads, head_width = queries.shape
    block_size = min(512, length)
    block_count = length // block_size
    score_scale = head_width ** (-0.5)
    key_place = jnp.arange(key_rows.shape[0]) % length

    def one_block(block_index):
        row_start = block_index * block_size
        query_rows = lax.dynamic_slice_in_dim(queries, row_start, block_size, 0)
        positions = row_start + jnp.arange(block_size)
        scores = (
            jnp.einsum("qhd,khd->hqk", query_rows, key_rows, preferred_element_type=jnp.float32)
            * score_scale
        )
        allowed = key_place[None, :] <= positions[:, None]
        scores = jnp.where(allowed[None], scores, -1e30)
        row_max = jnp.max(scores, axis=-1, keepdims=True)
        weights = jnp.exp(scores - row_max)
        row_sum = jnp.sum(weights, axis=-1, keepdims=True)
        chances = (weights / row_sum).astype(jnp.bfloat16)
        result = jnp.einsum("hqk,khd->qhd", chances, value_rows, preferred_element_type=jnp.float32)
        return (result, (row_max + jnp.log(row_sum))[..., 0])

    results, totals = lax.map(one_block, jnp.arange(block_count))
    return (results.reshape(length, local_heads, head_width), totals)


def attend_backward(queries, key_rows, value_rows, upstream, totals):
    length, local_heads, head_width = queries.shape
    block_size = min(512, length)
    block_count = length // block_size
    score_scale = head_width ** (-0.5)
    key_place = jnp.arange(key_rows.shape[0]) % length

    def one_block(sums_now, block_index):
        key_sum, value_sum = sums_now
        row_start = block_index * block_size
        query_rows = lax.dynamic_slice_in_dim(queries, row_start, block_size, 0)
        grad_rows = lax.dynamic_slice_in_dim(upstream, row_start, block_size, 0)
        positions = row_start + jnp.arange(block_size)
        scores = (
            jnp.einsum("qhd,khd->hqk", query_rows, key_rows, preferred_element_type=jnp.float32)
            * score_scale
        )
        allowed = key_place[None, :] <= positions[:, None]
        scores = jnp.where(allowed[None], scores, -1e30)
        chances = jnp.exp(scores - totals[block_index][..., None])
        d_chance = jnp.einsum(
            "qhd,khd->hqk", grad_rows, value_rows, preferred_element_type=jnp.float32
        )
        centre = jnp.sum(chances * d_chance, axis=-1, keepdims=True)
        d_score = (chances * (d_chance - centre)).astype(jnp.bfloat16)
        query_grad = (
            jnp.einsum("hqk,khd->qhd", d_score, key_rows, preferred_element_type=jnp.float32)
            * score_scale
        )
        key_sum = (
            key_sum
            + jnp.einsum("hqk,qhd->khd", d_score, query_rows, preferred_element_type=jnp.float32)
            * score_scale
        )
        value_sum = value_sum + jnp.einsum(
            "hqk,qhd->khd",
            chances.astype(jnp.bfloat16),
            grad_rows,
            preferred_element_type=jnp.float32,
        )
        return ((key_sum, value_sum), query_grad)

    zero_keys = jnp.zeros(key_rows.shape, jnp.float32)
    (key_grad, value_grad), query_grad = lax.scan(
        one_block, (zero_keys, zero_keys), jnp.arange(block_count)
    )
    return (query_grad.reshape(length, local_heads, head_width), key_grad, value_grad)


def block_forward(stream, weights, earlier):
    qkv_w, out_w, up_w, down_w, gain_a, gain_b = weights
    normed = layer_norm(stream, gain_a).astype(jnp.bfloat16)
    packed = jnp.dot(normed, qkv_w, preferred_element_type=jnp.float32).astype(jnp.bfloat16)
    heads = lax.all_to_all(packed, "seq", split_axis=1, concat_axis=0, tiled=True)
    length = heads.shape[0]
    local_heads = heads.shape[1] // (3 * HEAD_DIM)
    heads = heads.reshape(length, local_heads, 3, HEAD_DIM)
    queries = heads[:, :, 0]
    key_rows = heads[:, :, 1]
    value_rows = heads[:, :, 2]
    if earlier is None:
        all_keys, all_values = (key_rows, value_rows)
    else:
        all_keys = jnp.concatenate([earlier[0], key_rows], axis=0)
        all_values = jnp.concatenate([earlier[1], value_rows], axis=0)
    attended, totals = attend_forward(queries, all_keys, all_values)
    mixed = attended.reshape(length, local_heads * HEAD_DIM).astype(jnp.bfloat16)
    mixed_rows = lax.all_to_all(mixed, "seq", split_axis=0, concat_axis=1, tiled=True)
    middle = stream + jnp.dot(mixed_rows, out_w, preferred_element_type=jnp.float32)
    normed_b = layer_norm(middle, gain_b).astype(jnp.bfloat16)
    hidden = jnp.dot(normed_b, up_w, preferred_element_type=jnp.float32)
    active = gelu_value(hidden).astype(jnp.bfloat16)
    result = middle + jnp.dot(active, down_w, preferred_element_type=jnp.float32)
    stored = (
        stream,
        normed,
        queries,
        all_keys,
        all_values,
        totals,
        mixed_rows,
        middle,
        normed_b,
        hidden,
        active,
    )
    return (result, stored, (key_rows, value_rows))


def block_backward(upstream, stored, weights, carried):
    qkv_w, out_w, up_w, down_w, gain_a, gain_b = weights
    (
        stream,
        normed,
        queries,
        all_keys,
        all_values,
        totals,
        mixed_rows,
        middle,
        normed_b,
        hidden,
        active,
    ) = stored
    out_bf = upstream.astype(jnp.bfloat16)
    down_grad = contract_rows(active, out_bf)
    d_active = contract_cols(out_bf, down_w)
    d_hidden = jax.vjp(gelu_value, hidden)[1](d_active)[0].astype(jnp.bfloat16)
    up_grad = contract_rows(normed_b, d_hidden)
    d_normed_b = contract_cols(d_hidden, up_w)
    d_middle_norm, gain_b_grad = jax.vjp(layer_norm, middle, gain_b)[1](d_normed_b)
    d_middle = upstream + d_middle_norm
    middle_bf = d_middle.astype(jnp.bfloat16)
    out_grad = contract_rows(mixed_rows, middle_bf)
    d_mixed = contract_cols(middle_bf, out_w).astype(jnp.bfloat16)
    d_heads = lax.all_to_all(d_mixed, "seq", split_axis=1, concat_axis=0, tiled=True)
    length, local_heads = (queries.shape[0], queries.shape[1])
    d_heads = d_heads.reshape(length, local_heads, HEAD_DIM)
    query_grad, key_grad, value_grad = attend_backward(
        queries, all_keys, all_values, d_heads, totals
    )
    earlier_len = key_grad.shape[0] - length
    own_keys = key_grad[earlier_len:]
    own_values = value_grad[earlier_len:]
    passed = None
    if earlier_len > 0:
        passed = (key_grad[:earlier_len], value_grad[:earlier_len])
    if carried is not None:
        own_keys = own_keys + carried[0]
        own_values = own_values + carried[1]
    d_packed = jnp.stack([query_grad, own_keys, own_values], axis=2).astype(jnp.bfloat16)
    d_packed = d_packed.reshape(length, local_heads * 3 * HEAD_DIM)
    d_rows = lax.all_to_all(d_packed, "seq", split_axis=0, concat_axis=1, tiled=True)
    qkv_grad = contract_rows(normed, d_rows)
    d_normed = contract_cols(d_rows, qkv_w)
    d_stream_norm, gain_a_grad = jax.vjp(layer_norm, stream, gain_a)[1](d_normed)
    grads = (qkv_grad, out_grad, up_grad, down_grad, gain_a_grad, gain_b_grad)
    return (d_middle + d_stream_norm, grads, passed)


def local(
    tokens,
    qkv_weight,
    out_weight,
    up_weight,
    down_weight,
    norm_gain,
    mlp_gain,
    pass_embed,
    cotangent,
):
    gathered = (
        lax.all_gather(qkv_weight, "dp", axis=0, tiled=True),
        lax.all_gather(out_weight, "dp", axis=0, tiled=True),
        lax.all_gather(up_weight, "dp", axis=0, tiled=True),
        lax.all_gather(down_weight, "dp", axis=0, tiled=True),
        lax.all_gather(norm_gain, "dp", axis=0, tiled=True),
        lax.all_gather(mlp_gain, "dp", axis=0, tiled=True),
        lax.all_gather(pass_embed, "dp", axis=0, tiled=True),
    )
    weights = (
        gathered[0],
        gathered[1],
        gathered[2],
        gathered[3],
        gathered[4].astype(jnp.float32),
        gathered[5].astype(jnp.float32),
    )
    embedding = gathered[6].astype(jnp.float32)
    first_out, first_kept, first_keys = block_forward(tokens[0].astype(jnp.float32), weights, None)
    second_out, second_kept, unused_keys = block_forward(first_out + embedding, weights, first_keys)
    d_second, second_grads, passed = block_backward(
        cotangent[0].astype(jnp.float32), second_kept, weights, None
    )
    embed_grad = jnp.sum(d_second, axis=0)
    d_first, first_grads, unused = block_backward(d_second, first_kept, weights, passed)
    summed = jax.tree.map(jnp.add, first_grads, second_grads) + (embed_grad,)
    shards = (
        lax.psum_scatter(
            summed[0].astype(jnp.bfloat16), "dp", scatter_dimension=0, tiled=True
        ).astype(jnp.float32),
        lax.psum_scatter(
            summed[1].astype(jnp.bfloat16), "dp", scatter_dimension=0, tiled=True
        ).astype(jnp.float32),
        lax.psum_scatter(
            summed[2].astype(jnp.bfloat16), "dp", scatter_dimension=0, tiled=True
        ).astype(jnp.float32),
        lax.psum_scatter(
            summed[3].astype(jnp.bfloat16), "dp", scatter_dimension=0, tiled=True
        ).astype(jnp.float32),
        lax.psum_scatter(
            summed[4].astype(jnp.bfloat16), "dp", scatter_dimension=0, tiled=True
        ).astype(jnp.float32),
        lax.psum_scatter(
            summed[5].astype(jnp.bfloat16), "dp", scatter_dimension=0, tiled=True
        ).astype(jnp.float32),
        lax.psum_scatter(
            summed[6].astype(jnp.bfloat16), "dp", scatter_dimension=0, tiled=True
        ).astype(jnp.float32),
    )
    final = (
        lax.psum(shards[0].astype(jnp.bfloat16), "seq").astype(jnp.float32),
        lax.psum(shards[1].astype(jnp.bfloat16), "seq").astype(jnp.float32),
        lax.psum(shards[2].astype(jnp.bfloat16), "seq").astype(jnp.float32),
        lax.psum(shards[3].astype(jnp.bfloat16), "seq").astype(jnp.float32),
        lax.psum(shards[4].astype(jnp.bfloat16), "seq").astype(jnp.float32),
        lax.psum(shards[5].astype(jnp.bfloat16), "seq").astype(jnp.float32),
        lax.psum(shards[6].astype(jnp.bfloat16), "seq").astype(jnp.float32),
    )
    return (
        second_out.astype(jnp.bfloat16)[None],
        d_first[None],
        final[0],
        final[1],
        final[2],
        final[3],
        final[4],
        final[5],
        final[6],
    )


def solution(mesh):
    in_specs = (
        P("dp", "seq", None),
        P("dp", None),
        P("dp", None),
        P("dp", None),
        P("dp", None),
        P("dp"),
        P("dp"),
        P("dp"),
        P("dp", "seq", None),
    )
    out_specs = (
        P("dp", "seq", None),
        P("dp", "seq", None),
        P("dp", None),
        P("dp", None),
        P("dp", None),
        P("dp", None),
        P("dp"),
        P("dp"),
        P("dp"),
    )
    return jax.shard_map(local, mesh=mesh, in_specs=in_specs, out_specs=out_specs, check_vma=False)
```

profile of v0, /device:TPU:0, one launch (start us, length us, event | category | flops | bytes accessed | tf_op | source)
XLA Modules:
  0.0 1605.7 jit_solution(13835982464477941416)
XLA Ops:
  13.9 23.9 %all-reduce.7 = (bf16[768]{0:T(1024)(128)(2,1)S(1)}, bf16[768]{0:T(1024)(128)(2,1)S(1)}, bf16[768]{0:T(1024)(128)(2,1)S(1)}) all-reduce(bf16[768]{0:T(1024)(128)(2,1)S(1)} %dynamic-update-slice, bf16[768]{0:T(1024)(128)(2,1)S(1)} %dynamic-update-slice.2, bf16[768]{0:T(1024)(128)(2,1)S(1)} %dynamic-update-slice.1), channel_id=1, replica_groups=mesh['seq'=4,'dp'=8] {'dp'}, use_global_device_ids=true, to_apply=%add | all-reduce | flops 2304 | bytes 9216
  41.3 37.4 %all-gather.5.cloned.1.call-done = bf16[768,2304]{1,0:T(8,128)(2,1)} async-done(((bf16[96,2304]{1,0:T(8,128)(2,1)}), bf16[768,2304]{1,0:T(8,128)(2,1)}) %all-gather.5.cloned.1.call-update) | async-done | bytes 3538960 | tf_op jit(solution)/shard_map/all_gather | solution.py:214
  89.8 27.9 %all-to-all-done = bf16[512,4,576]{0,2,1:T(8,128)(2,1)S(1)} async-done(((bf16[512,4,576]{0,2,1:T(8,128)(2,1)}), bf16[512,4,576]{0,2,1:T(8,128)(2,1)S(1)}, u32[]{:S(2)}, u32[]{:S(2)}) %all-to-all-start) | async-done | bytes 2359328 | tf_op jit(solution)/shard_map/all_to_all | solution.py:115
  128.6 86.6 %while.56 = (s32[]{:T(128)}, bf16[4,512,3,64]{1,3,2,0:T(8,128)(2,1)S(1)}, f32[4,3,512]{2,1,0:T(4,128)S(1)}, s32[4]{0:T(128)S(1)}, bf16[2048,3,64]{0,2,1:T(8,128)...) while((s32[]{:T(128)}, ...), condition=%wide.region_5.6_spmd.clone, body=%wide.region_2.5_spmd.clone.sunk | while | flops 844114944 | bytes 44185780 | solution.py:58
  244.0 37.5 %all-gather.11.cloned.1.call-done = bf16[3072,768]{1,0:T(8,128)(2,1)} async-done(((bf16[384,768]{1,0:T(8,128)(2,1)}), bf16[3072,768]{1,0:T(8,128)(2,1)}) %all-gather.11.cloned.1.call-update) | async-done | bytes 4718608 | tf_op jit(solution)/shard_map/all_gather | solution.py:217
  302.5 28.6 %all-to-all-done.2 = bf16[512,4,576]{0,2,1:T(8,128)(2,1)} async-done(((bf16[512,4,576]{0,2,1:T(8,128)(2,1)}), bf16[512,4,576]{0,2,1:T(8,128)(2,1)}, u32[]{:S(2)}, u32[]{:S(2)}) %all-to-all-start.2) | async-done | bytes 2359328 | tf_op jit(solution)/shard_map/all_to_all | solution.py:115
  346.6 160.2 %while.57 = (s32[]{:T(128)}, bf16[4,512,3,64]{1,3,2,0:T(8,128)(2,1)}, f32[4,3,512]{2,1,0:T(4,128)S(1)}, s32[4]{0:T(128)S(1)}, bf16[2048,3,64]{0,2,1:T(8,128)(2,1...) while((s32[]{:T(128)}, ...), condition=%wide.region_13.14_spmd.clone, body=%wide.region_10.13_spmd.clone.sunk | while | flops 1688230912 | bytes 87714480 | solution.py:58
  560.7 356.0 %while.58 = (s32[]{:T(128)}, f32[4096,3,64]{0,2,1:T(8,128)}, f32[4096,3,64]{0,2,1:T(8,128)}, bf16[4,512,3,64]{1,3,2,0:T(8,128)(2,1)}, s32[4]{0:T(128)S(1)}, /*in...) while((s32[]{:T(128)}, f32[4096,3,64]{0,2,1:T(8,128)}, ...), condition=%wide.region_20.21_spmd.clone, body=%wide.region_18.20_spmd.clone.sunk | while | flops 4127054848 | bytes 215694096 | solution.py:105
  577.3 18.2 %multiply_reduce_fusion.13 = (f32[3,512]{1,0:T(4,128)S(1)}, f32[3,512,4096]{2,1,0:T(8,128)}) fusion(f32[3,512,4096]{2,1,0:T(8,128)} %fusion.266, f32[3,512]{1,0:T(4,128)S(1)} %dynamic-slice_bitcast_fusion.4, pred[512,4096]{1,0:T(8,128)(4,1)S(1)} %broadcast_compare_fusion.10, bf16[4096,3,64]{0,2,1:T(8,128)(2,1)} %get-tuple-element.780, ...), kind=kOutput, calls=%fused_computation.47.clone.1 | convolution fusion | flops 836762112 | bytes 54210564 | tf_op jit(solution)/shard_map/while/body/eval_jaxpr/qhd,khd->hqk/dot_general | solution.py:82
  595.6 21.8 %multiply_convert_fusion.19 = bf16[3,512,4096]{2,1,0:T(8,128)(2,1)} fusion(f32[3,512,4096]{2,1,0:T(8,128)} %get-tuple-element.661, f32[3,512,4096]{2,1,0:T(8,128)} %fusion.266, f32[3,512]{1,0:T(4,128)S(1)} %get-tuple-element.662, f32[3,512]{1,0:T(4,128)S(1)} %dynamic-slice_bitcast_fusion.4, pred[512,4096]{1,0:T(8,128)(4,1)S(1)} %broadcast_compare_fusion.10), kind=kLoop, calls=%fused_computation.46.clone.1 | loop fusion | flops 37748736 | bytes 65024000 | tf_op jit(solution)/shard_map/while/body/eval_jaxpr/convert_element_type | solution.py:86
  664.7 18.2 %multiply_reduce_fusion.13 = (f32[3,512]{1,0:T(4,128)S(1)}, f32[3,512,4096]{2,1,0:T(8,128)}) fusion(f32[3,512,4096]{2,1,0:T(8,128)} %fusion.266, f32[3,512]{1,0:T(4,128)S(1)} %dynamic-slice_bitcast_fusion.4, pred[512,4096]{1,0:T(8,128)(4,1)S(1)} %broadcast_compare_fusion.10, bf16[4096,3,64]{0,2,1:T(8,128)(2,1)} %get-tuple-element.780, ...), kind=kOutput, calls=%fused_computation.47.clone.1 | convolution fusion | flops 836762112 | bytes 54210564 | tf_op jit(solution)/shard_map/while/body/eval_jaxpr/qhd,khd->hqk/dot_general | solution.py:82
  682.9 21.8 %multiply_convert_fusion.19 = bf16[3,512,4096]{2,1,0:T(8,128)(2,1)} fusion(f32[3,512,4096]{2,1,0:T(8,128)} %get-tuple-element.661, f32[3,512,4096]{2,1,0:T(8,128)} %fusion.266, f32[3,512]{1,0:T(4,128)S(1)} %get-tuple-element.662, f32[3,512]{1,0:T(4,128)S(1)} %dynamic-slice_bitcast_fusion.4, pred[512,4096]{1,0:T(8,128)(4,1)S(1)} %broadcast_compare_fusion.10), kind=kLoop, calls=%fused_computation.46.clone.1 | loop fusion | flops 37748736 | bytes 65024000 | tf_op jit(solution)/shard_map/while/body/eval_jaxpr/convert_element_type | solution.py:86
  754.1 18.3 %multiply_reduce_fusion.13 = (f32[3,512]{1,0:T(4,128)S(1)}, f32[3,512,4096]{2,1,0:T(8,128)}) fusion(f32[3,512,4096]{2,1,0:T(8,128)} %fusion.266, f32[3,512]{1,0:T(4,128)S(1)} %dynamic-slice_bitcast_fusion.4, pred[512,4096]{1,0:T(8,128)(4,1)S(1)} %broadcast_compare_fusion.10, bf16[4096,3,64]{0,2,1:T(8,128)(2,1)} %get-tuple-element.780, ...), kind=kOutput, calls=%fused_computation.47.clone.1 | convolution fusion | flops 836762112 | bytes 54210564 | tf_op jit(solution)/shard_map/while/body/eval_jaxpr/qhd,khd->hqk/dot_general | solution.py:82
  772.3 21.8 %multiply_convert_fusion.19 = bf16[3,512,4096]{2,1,0:T(8,128)(2,1)} fusion(f32[3,512,4096]{2,1,0:T(8,128)} %get-tuple-element.661, f32[3,512,4096]{2,1,0:T(8,128)} %fusion.266, f32[3,512]{1,0:T(4,128)S(1)} %get-tuple-element.662, f32[3,512]{1,0:T(4,128)S(1)} %dynamic-slice_bitcast_fusion.4, pred[512,4096]{1,0:T(8,128)(4,1)S(1)} %broadcast_compare_fusion.10), kind=kLoop, calls=%fused_computation.46.clone.1 | loop fusion | flops 37748736 | bytes 65024000 | tf_op jit(solution)/shard_map/while/body/eval_jaxpr/convert_element_type | solution.py:86
  843.4 18.2 %multiply_reduce_fusion.13 = (f32[3,512]{1,0:T(4,128)S(1)}, f32[3,512,4096]{2,1,0:T(8,128)}) fusion(f32[3,512,4096]{2,1,0:T(8,128)} %fusion.266, f32[3,512]{1,0:T(4,128)S(1)} %dynamic-slice_bitcast_fusion.4, pred[512,4096]{1,0:T(8,128)(4,1)S(1)} %broadcast_compare_fusion.10, bf16[4096,3,64]{0,2,1:T(8,128)(2,1)} %get-tuple-element.780, ...), kind=kOutput, calls=%fused_computation.47.clone.1 | convolution fusion | flops 836762112 | bytes 54210564 | tf_op jit(solution)/shard_map/while/body/eval_jaxpr/qhd,khd->hqk/dot_general | solution.py:82
  861.6 21.8 %multiply_convert_fusion.19 = bf16[3,512,4096]{2,1,0:T(8,128)(2,1)} fusion(f32[3,512,4096]{2,1,0:T(8,128)} %get-tuple-element.661, f32[3,512,4096]{2,1,0:T(8,128)} %fusion.266, f32[3,512]{1,0:T(4,128)S(1)} %get-tuple-element.662, f32[3,512]{1,0:T(4,128)S(1)} %dynamic-slice_bitcast_fusion.4, pred[512,4096]{1,0:T(8,128)(4,1)S(1)} %broadcast_compare_fusion.10), kind=kLoop, calls=%fused_computation.46.clone.1 | loop fusion | flops 37748736 | bytes 65024000 | tf_op jit(solution)/shard_map/while/body/eval_jaxpr/convert_element_type | solution.py:86
  927.9 31.5 %all_to_all.129 = bf16[4,512,576]{1,2,0:T(8,128)(2,1)S(1)} all-to-all(bf16[4,512,576]{1,2,0:T(8,128)(2,1)S(1)} %copy.60), channel_id=1, replica_groups=mesh['seq'=4,'dp'=8] {'seq'}, dimensions={0} | all-to-all | bytes 4718592 | tf_op jit(solution)/shard_map/all_to_all | solution.py:194
  997.3 183.4 %while.59 = (s32[]{:T(128)}, f32[2048,3,64]{0,2,1:T(8,128)}, f32[2048,3,64]{0,2,1:T(8,128)}, bf16[4,512,3,64]{1,3,2,0:T(8,128)(2,1)}, s32[4]{0:T(128)S(1)}, /*in...) while((s32[]{:T(128)}, f32[2048,3,64]{0,2,1:T(8,128)}, ...), condition=%wide.region_27.28_spmd.clone, body=%wide.region_25.27_spmd.clone.sunk | while | flops 2063576064 | bytes 185006576 | solution.py:105
  1201.1 25.3 %all-to-all-done.7 = bf16[4,512,576]{1,2,0:T(8,128)(2,1)} async-done(((bf16[4,512,576]{1,2,0:T(8,128)(2,1)}), bf16[4,512,576]{1,2,0:T(8,128)(2,1)}, u32[]{:S(2)}, u32[]{:S(2)}) %all-to-all-start.7) | async-done | bytes 2359328 | tf_op jit(solution)/shard_map/all_to_all | solution.py:194
  1276.6 70.0 %reduce-scatter.5.cloned.1.call-done = bf16[96,2304]{1,0:T(8,128)(2,1)} async-done(((bf16[768,2304]{1,0:T(8,128)(2,1)}), bf16[96,2304]{1,0:T(8,128)(2,1)}) %reduce-scatter.5.cloned.1.call-update) | async-done | bytes 442384 | tf_op jit(solution)/shard_map/reduce_scatter | solution.py:240
  1346.6 98.5 %reduce-scatter.11.cloned.1.call-done = bf16[384,768]{1,0:T(8,128)(2,1)} async-done(((bf16[3072,768]{1,0:T(8,128)(2,1)}), bf16[384,768]{1,0:T(8,128)(2,1)}) %reduce-scatter.11.cloned.1.call-update) | async-done | bytes 589840 | tf_op jit(solution)/shard_map/reduce_scatter | solution.py:249
  1445.1 98.7 %reduce-scatter.9.cloned.1.call-done = bf16[96,3072]{1,0:T(8,128)(2,1)} async-done(((bf16[768,3072]{1,0:T(8,128)(2,1)}), bf16[96,3072]{1,0:T(8,128)(2,1)}) %reduce-scatter.9.cloned.1.call-update) | async-done | bytes 589840 | tf_op jit(solution)/shard_map/reduce_scatter | solution.py:246
  1546.0 20.4 %all-reduce.6 = (bf16[768]{0:T(1024)(128)(2,1)S(1)}, bf16[768]{0:T(1024)(128)(2,1)S(1)}, bf16[768]{0:T(1024)(128)(2,1)S(1)}) all-reduce(bf16[768]{0:T(1024)(128)(2,1)S(1)} %add_convert_fusion.8, bf16[768]{0:T(1024)(128)(2,1)S(1)} %add_convert_fusion.7, bf16[768]{0:T(1024)(128)(2,1)S(1)} %copy-done.79), channel_id=6, replica_groups=mesh['seq'=4,'dp'=8] {'dp'}, use_global_device_ids=true, to_apply=%region_40.41.clone | all-reduce | flops 2304 | bytes 9216
  1577.0 15.9 all-reduce.12.cloned.1.call-done
  (558 shorter events, 885.1 us)
Async XLA Ops:
  7.2 71.5 %all-gather.5.cloned.1.call-start = ((), (), s32[]{:S(2)}) async-start(), calls=%async_computation.12 | async-start | bytes 3981312 | tf_op jit(solution)/shard_map/all_gather | solution.py:214
  7.9 212.3 %all-gather.7.cloned.1.call-start = ((), (), s32[]{:S(2)}) async-start(), calls=%async_computation.13 | async-start | bytes 1327104 | tf_op jit(solution)/shard_map/all_gather | solution.py:215
  8.7 227.7 %all-gather.9.cloned.1.call-start = ((), (), s32[]{:S(2)}) async-start(), calls=%async_computation.14 | async-start | bytes 5308416 | tf_op jit(solution)/shard_map/all_gather | solution.py:216
  37.8 45.2 %copy-start.49 = (f32[768]{0:T(1024)}, f32[768]{0:T(1024)S(1)}, u32[]{:S(2)}) copy-start(f32[768]{0:T(1024)S(1)} %convert_element_type.175) | copy-start | bytes 9220
  85.5 32.1 %all-to-all-start = ((bf16[512,4,576]{0,2,1:T(8,128)(2,1)}), bf16[512,4,576]{0,2,1:T(8,128)(2,1)S(1)}, u32[]{:S(2)}, u32[]{:S(2)}) async-start(bf16[512,4,576]{0,2,1:T(8,128)(2,1)} %bitcast.279), calls=%async_computation | async-start | bytes 4718592 | tf_op jit(solution)/shard_map/all_to_all | solution.py:115
  89.2 192.3 %all-gather.11.cloned.1.call-start = ((), (), s32[]{:S(2)}) async-start(), calls=%async_computation.15 | async-start | bytes 5308416 | tf_op jit(solution)/shard_map/all_gather | solution.py:217
  215.3 128.4 %copy-start.2 = (bf16[2048,3,64]{0,2,1:T(8,128)(2,1)}, bf16[2048,3,64]{0,2,1:T(8,128)(2,1)S(1)}, u32[]{:S(2)}) copy-start(bf16[2048,3,64]{0,2,1:T(8,128)(2,1)S(1)} %get-tuple-element.847) | copy-start | bytes 2359300
  215.3 128.4 %copy-start.5 = (bf16[2048,3,64]{0,2,1:T(8,128)(2,1)}, bf16[2048,3,64]{0,2,1:T(8,128)(2,1)S(1)}, u32[]{:S(2)}) copy-start(bf16[2048,3,64]{0,2,1:T(8,128)(2,1)S(1)} %get-tuple-element.864) | copy-start | bytes 2359300
  216.1 15.6 all-to-all-start.1
  235.2 46.2 %copy-start.16 = (f32[512,768]{1,0:T(8,128)}, f32[512,768]{1,0:T(8,128)S(1)}, u32[]{:S(2)}) copy-start(f32[512,768]{1,0:T(8,128)S(1)} %get-tuple-element.439) | copy-start | bytes 4718596
  244.0 46.2 %copy-start.50 = (f32[768]{0:T(1024)S(1)}, f32[768]{0:T(1024)}, u32[]{:S(2)}) copy-start(f32[768]{0:T(1024)} %copy-done.49) | copy-start | bytes 9220
  298.0 33.1 %all-to-all-start.2 = ((bf16[512,4,576]{0,2,1:T(8,128)(2,1)}), bf16[512,4,576]{0,2,1:T(8,128)(2,1)}, u32[]{:S(2)}, u32[]{:S(2)}) async-start(bf16[512,4,576]{0,2,1:T(8,128)(2,1)} %bitcast.280), calls=%async_computation.2 | async-start | bytes 4718592 | tf_op jit(solution)/shard_map/all_to_all | solution.py:115
  346.6 175.5 %copy-start.7 = (f32[512,768]{1,0:T(8,128)S(1)}, f32[512,768]{1,0:T(8,128)}, u32[]{:S(2)}) copy-start(f32[512,768]{1,0:T(8,128)} %copy-done.6) | copy-start | bytes 4718596
  542.5 15.1 all-to-all-start.4
  979.0 15.3 all-to-all-start.6
  1193.2 33.2 %all-to-all-start.7 = ((bf16[4,512,576]{1,2,0:T(8,128)(2,1)}), bf16[4,512,576]{1,2,0:T(8,128)(2,1)}, u32[]{:S(2)}, u32[]{:S(2)}) async-start(bf16[4,512,576]{1,2,0:T(8,128)(2,1)} %copy.65), calls=%async_computation.7 | async-start | bytes 4718592 | tf_op jit(solution)/shard_map/all_to_all | solution.py:194
  1197.9 78.7 %reduce-scatter.7.cloned.1.call-start = ((), (), s32[]{:S(2)}) async-start(), calls=%async_computation.17 | async-start | bytes 1327104 | tf_op jit(solution)/shard_map/reduce_scatter | solution.py:243
  1201.1 145.5 %reduce-scatter.5.cloned.1.call-start = ((), (), s32[]{:S(2)}) async-start(), calls=%async_computation.16 | async-start | bytes 3981312 | tf_op jit(solution)/shard_map/reduce_scatter | solution.py:240
  1234.8 210.3 %reduce-scatter.11.cloned.1.call-start = ((), (), s32[]{:S(2)}) async-start(), calls=%async_computation.19 | async-start | bytes 5308416 | tf_op jit(solution)/shard_map/reduce_scatter | solution.py:249
  1250.8 293.0 %reduce-scatter.9.cloned.1.call-start = ((), (), s32[]{:S(2)}) async-start(), calls=%async_computation.18 | async-start | bytes 5308416 | tf_op jit(solution)/shard_map/reduce_scatter | solution.py:246
  1261.5 331.4 %all-reduce.12.cloned.1.call-start = ((), (), s32[]{:S(2)}) async-start(), calls=%async_computation.20 | async-start | bytes 3538944 | tf_op jit(solution)/shard_map/psum | solution.py:263
  1271.5 272.3 %copy-start.20 = (bf16[1,512,768]{2,1,0:T(8,128)(2,1)S(1)}, bf16[1,512,768]{2,1,0:T(8,128)(2,1)}, u32[]{:S(2)}) copy-start(bf16[1,512,768]{2,1,0:T(8,128)(2,1)} %param.17) | copy-start | bytes 2359300
  1276.5 269.4 %copy-start.83 = (f32[768]{0:T(1024)S(1)}, f32[768]{0:T(1024)}, u32[]{:S(2)}) copy-start(f32[768]{0:T(1024)} %get-tuple-element.329) | copy-start | bytes 9220
  1276.5 269.5 %copy-start.79 = (bf16[768]{0:T(1024)(128)(2,1)S(1)}, bf16[768]{0:T(1024)(128)(2,1)}, u32[]{:S(2)}) copy-start(bf16[768]{0:T(1024)(128)(2,1)} %get-tuple-element.414) | copy-start | bytes 4612
  (118 other events, 1010.3 us)
Sparse Core Ops, SparseCore 0:
  10.2 68.3 all-gather.4
  80.8 39.6 all-gather.6
  122.7 78.6 all-gather.8
  203.4 78.0 all-gather.10
  1202.3 62.5 reduce-scatter.6
  1268.4 78.0 reduce-scatter.4
  1350.2 94.8 reduce-scatter.10
  1448.7 94.9 reduce-scatter.8
  1546.4 46.4 all-reduce.11
where the time goes:
time: 1610 us
  matrix products  640 us (40%)
  waiting for transfers between devices  477 us (30%)
  other arithmetic  233 us (14%)
  blocking collectives  96.8 us (6%)
  local copies, waits for them, and re-layouts  89.5 us (6%)
  loops' own time  28.1 us (2%)
  starting transfers between devices  24.8 us (2%)
  between operations  16.8 us (1%)
    dot_general x16, matrix products, one_block(): jnp.einsum('qhd,khd->hqk', query_rows, key_rows, preferred_element_type=j...  151 us
    convert_element_type x8, other arithmetic, one_block(): d_score = (chances * (d_chance - centre)).astype(jnp.bfloat16)  112 us
    dot_general x8, matrix products, one_block(): jnp.einsum('qhd,khd->hqk', grad_rows, value_rows, preferred_element_type=...  105 us
    reduce_scatter x1, waiting for transfers between devices, local(): lax.psum_scatter(summed[2].astype(jnp.bfloat16), 'dp', scatter_dimension=...  98.7 us
    reduce_scatter x1, waiting for transfers between devices, local(): lax.psum_scatter(summed[3].astype(jnp.bfloat16), 'dp', scatter_dimension=...  98.5 us
    dot_general x8, matrix products, one_block(): jnp.einsum('hqk,qhd->khd', chances.astype(jnp.bfloat16), grad_rows, prefe...  95.2 us
    dot_general x8, matrix products, one_block(): jnp.einsum('hqk,khd->qhd', chances, value_rows, preferred_element_type=jn...  79.4 us
    reduce_sum x8, other arithmetic, one_block(): row_sum = jnp.sum(weights, axis=-1, keepdims=True)  74.4 us
  transfers between devices with their start and end apart: 15, of which 12 were waited for; matrix products, arithmetic and copies ran while one was open for 11% of the time, Pallas kernels for 0%

commit v1 on v0

--- a/solution.py
+++ b/solution.py
@@ -1,6 +1,10 @@
+import functools
+
 import jax
 import jax.numpy as jnp
 from jax import lax
+from jax.experimental import pallas as pl
+from jax.experimental.pallas import tpu as pltpu
 from jax.sharding import PartitionSpec as P
 
 HEAD_DIM = 64
@@ -31,81 +35,187 @@
     )
 
 
-def attend_forward(queries, key_rows, value_rows):
-    length, local_heads, head_width = queries.shape
-    block_size = min(512, length)
-    block_count = length // block_size
-    score_scale = head_width ** (-0.5)
-    key_place = jnp.arange(key_rows.shape[0]) % length
-
-    def one_block(block_index):
-        row_start = block_index * block_size
-        query_rows = lax.dynamic_slice_in_dim(queries, row_start, block_size, 0)
-        positions = row_start + jnp.arange(block_size)
-        scores = (
-            jnp.einsum("qhd,khd->hqk", query_rows, key_rows, preferred_element_type=jnp.float32)
-            * score_scale
-        )
-        allowed = key_place[None, :] <= positions[:, None]
-        scores = jnp.where(allowed[None], scores, -1e30)
-        row_max = jnp.max(scores, axis=-1, keepdims=True)
-        weights = jnp.exp(scores - row_max)
-        row_sum = jnp.sum(weights, axis=-1, keepdims=True)
-        chances = (weights / row_sum).astype(jnp.bfloat16)
-        result = jnp.einsum("hqk,khd->qhd", chances, value_rows, preferred_element_type=jnp.float32)
-        return (result, (row_max + jnp.log(row_sum))[..., 0])
-
-    results, totals = lax.map(one_block, jnp.arange(block_count))
-    return (results.reshape(length, local_heads, head_width), totals)
-
-
-def attend_backward(queries, key_rows, value_rows, upstream, totals):
-    length, local_heads, head_width = queries.shape
-    block_size = min(512, length)
-    block_count = length // block_size
-    score_scale = head_width ** (-0.5)
-    key_place = jnp.arange(key_rows.shape[0]) % length
-
-    def one_block(sums_now, block_index):
-        key_sum, value_sum = sums_now
-        row_start = block_index * block_size
-        query_rows = lax.dynamic_slice_in_dim(queries, row_start, block_size, 0)
-        grad_rows = lax.dynamic_slice_in_dim(upstream, row_start, block_size, 0)
-        positions = row_start + jnp.arange(block_size)
-        scores = (
-            jnp.einsum("qhd,khd->hqk", query_rows, key_rows, preferred_element_type=jnp.float32)
-            * score_scale
-        )
-        allowed = key_place[None, :] <= positions[:, None]
-        scores = jnp.where(allowed[None], scores, -1e30)
-        chances = jnp.exp(scores - totals[block_index][..., None])
-        d_chance = jnp.einsum(
-            "qhd,khd->hqk", grad_rows, value_rows, preferred_element_type=jnp.float32
-        )
-        centre = jnp.sum(chances * d_chance, axis=-1, keepdims=True)
-        d_score = (chances * (d_chance - centre)).astype(jnp.bfloat16)
-        query_grad = (
-            jnp.einsum("hqk,khd->qhd", d_score, key_rows, preferred_element_type=jnp.float32)
-            * score_scale
-        )
-        key_sum = (
-            key_sum
-            + jnp.einsum("hqk,qhd->khd", d_score, query_rows, preferred_element_type=jnp.float32)
-            * score_scale
-        )
-        value_sum = value_sum + jnp.einsum(
-            "hqk,qhd->khd",
-            chances.astype(jnp.bfloat16),
-            grad_rows,
-            preferred_element_type=jnp.float32,
-        )
-        return ((key_sum, value_sum), query_grad)
-
-    zero_keys = jnp.zeros(key_rows.shape, jnp.float32)
-    (key_grad, value_grad), query_grad = lax.scan(
-        one_block, (zero_keys, zero_keys), jnp.arange(block_count)
-    )
-    return (query_grad.reshape(length, local_heads, head_width), key_grad, value_grad)
+HD = 64
+NEG = -1e30
+
+def nt(a, b):
+    return lax.dot_general(a, b, (((1,), (1,)), ((), ())), preferred_element_type=jnp.float32)
+
+def nn(a, b):
+    return lax.dot_general(a, b, (((1,), (0,)), ((), ())), preferred_element_type=jnp.float32)
+
+def fwd_kernel(nsets, heads, bq, bk, *refs):
+    qkv = refs[:nsets]
+    o_ref, lse_ref = refs[nsets:nsets + 2]
+    q_s, k_s, vt_s = refs[nsets + 2:]
+    length = o_ref.shape[0]
+    own = qkv[-1]
+    for h in range(heads):
+        c0 = 3 * HD * h
+        q_s[...] = own[:, c0:c0 + HD] * jnp.bfloat16(HD ** -0.5)
+        for s in range(nsets):
+            k_s[s] = qkv[s][:, c0 + HD:c0 + 2 * HD]
+            vt_s[s, :HD] = qkv[s][:, c0 + 2 * HD:c0 + 3 * HD].T
+            vt_s[s, HD:] = jnp.ones((16, length), jnp.bfloat16)
+
+        def q_block(i, _):
+            q0 = pl.multiple_of(i * bq, bq)
+            q = q_s[pl.ds(q0, bq), :]
+            per = bq // bk
+
+            def step(blocks, carry):
+                m, acc = carry
+                ss = []
+                for (s, k0, mask) in blocks:
+                    st = nt(k_s[s, pl.ds(k0, bk), :], q)
+                    if mask is not None:
+                        st = jnp.where(mask, st, NEG)
+                    ss.append(st)
+                m_new = m
+                for st in ss:
+                    m_new = jnp.maximum(m_new, jnp.max(st, axis=0, keepdims=True))
+                acc = acc * jnp.exp(m - m_new)
+                for (s, k0, _), st in zip(blocks, ss):
+                    p = jnp.exp(st - m_new).astype(jnp.bfloat16)
+                    acc = acc + nn(vt_s[s, :, pl.ds(k0, bk)], p)
+                return m_new, acc
+
+            carry = (jnp.full((1, bq), NEG, jnp.float32), jnp.zeros((HD + 16, bq), jnp.float32))
+            for t in range(per):
+                row = lax.broadcasted_iota(jnp.int32, (bk, bq), 0) + t * bk
+                col = lax.broadcasted_iota(jnp.int32, (bk, bq), 1)
+                mask = row <= col
+                carry = step([(s, pl.multiple_of(q0 + t * bk, bk), mask) for s in range(nsets)], carry)
+
+            def body(j, carry):
+                return step([(s, pl.multiple_of(j * bk, bk), None) for s in range(nsets)], carry)
+            m, acc = lax.fori_loop(0, i * per, body, carry)
+            l = acc[HD:HD + 1]
+            ot = acc[:HD] / l
+            o_ref[pl.ds(q0, bq), HD * h:HD * h + HD] = ot.T.astype(jnp.bfloat16)
+            lse_ref[h, :, pl.ds(q0, bq)] = m + jnp.log(l)
+            return 0
+        lax.fori_loop(0, length // bq, q_block, 0)
+
+def attn_fwd(packs, bq=512, bk=512):
+    nsets = len(packs)
+    length, cols = packs[0].shape
+    heads = cols // (3 * HD)
+    return pl.pallas_call(
+        functools.partial(fwd_kernel, nsets, heads, bq, bk),
+        out_shape=(jax.ShapeDtypeStruct((length, heads * HD), jnp.bfloat16),
+                   jax.ShapeDtypeStruct((heads, 1, length), jnp.float32)),
+        in_specs=[pl.BlockSpec(memory_space=pltpu.VMEM)] * nsets,
+        out_specs=(pl.BlockSpec(memory_space=pltpu.VMEM),) * 2,
+        scratch_shapes=[pltpu.VMEM((length, HD), jnp.bfloat16),
+                        pltpu.VMEM((nsets, length, HD), jnp.bfloat16),
+                        pltpu.VMEM((nsets, HD + 16, length), jnp.bfloat16)],
+        compiler_params=pltpu.CompilerParams(vmem_limit_bytes=56 << 20),
+        name=f"attn_fwd{nsets}",
+    )(*packs)
+
+def bwd_kernel(nsets, heads, bq, bk, has_add, *refs):
+    it = iter(refs)
+    qkv = [next(it) for _ in range(nsets)]
+    do_ref, o_ref, lse_ref = next(it), next(it), next(it)
+    add_ref = next(it) if has_add else None
+    dqkv_ref = next(it)
+    dprev_ref = next(it) if nsets == 2 else None
+    q_s, k_s, kt_s, v_s, doz_s, qz_s, do_s, delta_s, dqt_s, dkv_s = it
+    own = qkv[-1]
+    length = do_ref.shape[0]
+    nq, nk = length // bq, length // bk
+    scale = jnp.bfloat16(HD ** -0.5)
+    for h in range(heads):
+        c0 = 3 * HD * h
+        q = own[:, c0:c0 + HD]
+        q_s[...] = q * scale
+        do = do_ref[:, HD * h:HD * h + HD]
+        do_s[...] = do
+        zero = jnp.zeros((length, HD), jnp.bfloat16)
+        qz_s[:, :HD] = q * scale
+        qz_s[:, HD:] = zero
+        doz_s[:, :HD] = zero
+        doz_s[:, HD:] = do
+        prod = do.astype(jnp.float32) * o_ref[:, HD * h:HD * h + HD].astype(jnp.float32)
+        delta_s[...] = jnp.sum(prod.T, axis=0, keepdims=True)
+        for s in range(nsets):
+            k = qkv[s][:, c0 + HD:c0 + 2 * HD]
+            k_s[s] = k
+            kt_s[s] = (k * scale).T
+            v_s[s] = qkv[s][:, c0 + 2 * HD:c0 + 3 * HD]
+        dqt_s[...] = jnp.zeros_like(dqt_s)
+        if has_add:
+            dkv_s[0] = add_ref[h]
+        else:
+            for s in range(nsets):
+                dkv_s[s] = jnp.zeros_like(dkv_s[s])
+
+        def block(i, j, mask):
+            q0 = pl.multiple_of(i * bq, bq)
+            k0 = pl.multiple_of(j * bk, bk)
+            qb = q_s[pl.ds(q0, bq), :]
+            dob = do_s[pl.ds(q0, bq), :]
+            lse = lse_ref[h, :, pl.ds(q0, bq)]
+            delta = delta_s[:, pl.ds(q0, bq)]
+            dq = None
+            for s in range(nsets):
+                st = nt(k_s[s, pl.ds(k0, bk), :], qb)
+                p = jnp.exp(st - lse)
+                if mask is not None:
+                    p = jnp.where(mask, p, 0.0)
+                dpt = nt(v_s[s, pl.ds(k0, bk), :], dob)
+                ds = (p * (dpt - delta)).astype(jnp.bfloat16)
+                pb = p.astype(jnp.bfloat16)
+                dkv_s[s, pl.ds(k0, bk), :] += nn(pb, doz_s[pl.ds(q0, bq), :]) + nn(ds, qz_s[pl.ds(q0, bq), :])
+                t = nn(kt_s[s, :, pl.ds(k0, bk)], ds)
+                dq = t if dq is None else dq + t
+            dqt_s[:, pl.ds(q0, bq)] += dq
+
+        per = bq // bk
+        def q_loop(i, _):
+            for t in range(per):
+                row = lax.broadcasted_iota(jnp.int32, (bk, bq), 0) + t * bk
+                col = lax.broadcasted_iota(jnp.int32, (bk, bq), 1)
+                block(i, i * per + t, row <= col)
+            def k_loop(j, _):
+                block(i, j, None)
+                return 0
+            lax.fori_loop(0, i * per, k_loop, 0)
+            return 0
+        lax.fori_loop(0, nq, q_loop, 0)
+        dqkv_ref[:, c0:c0 + HD] = dqt_s[...].T.astype(jnp.bfloat16)
+        dqkv_ref[:, c0 + HD:c0 + 3 * HD] = dkv_s[nsets - 1].astype(jnp.bfloat16)
+        if nsets == 2:
+            dprev_ref[h] = dkv_s[0]
+
+def attn_bwd(packs, do, o, lse, add=None, bq=512, bk=512):
+    nsets = len(packs)
+    length, cols = packs[0].shape
+    heads = cols // (3 * HD)
+    outs = [jax.ShapeDtypeStruct((length, cols), jnp.bfloat16)]
+    if nsets == 2:
+        outs.append(jax.ShapeDtypeStruct((heads, length, 2 * HD), jnp.float32))
+    args = list(packs) + [do, o, lse] + ([add] if add is not None else [])
+    b = jnp.bfloat16
+    return pl.pallas_call(
+        functools.partial(bwd_kernel, nsets, heads, bq, bk, add is not None),
+        out_shape=tuple(outs),
+        in_specs=[pl.BlockSpec(memory_space=pltpu.VMEM)] * len(args),
+        out_specs=(pl.BlockSpec(memory_space=pltpu.VMEM),) * len(outs),
+        scratch_shapes=[pltpu.VMEM((length, HD), b),
+                        pltpu.VMEM((nsets, length, HD), b),
+                        pltpu.VMEM((nsets, HD, length), b),
+                        pltpu.VMEM((nsets, length, HD), b),
+                        pltpu.VMEM((length, 2 * HD), b),
+                        pltpu.VMEM((length, 2 * HD), b),
+                        pltpu.VMEM((length, HD), b),
+                        pltpu.VMEM((1, length), jnp.float32),
+                        pltpu.VMEM((HD, length), jnp.float32),
+                        pltpu.VMEM((nsets, length, 2 * HD), jnp.float32)],
+        compiler_params=pltpu.CompilerParams(vmem_limit_bytes=56 << 20),
+        name=f"attn_bwd{nsets}",
+    )(*args)
 
 
 def block_forward(stream, weights, earlier):
@@ -113,19 +223,8 @@
     normed = layer_norm(stream, gain_a).astype(jnp.bfloat16)
     packed = jnp.dot(normed, qkv_w, preferred_element_type=jnp.float32).astype(jnp.bfloat16)
     heads = lax.all_to_all(packed, "seq", split_axis=1, concat_axis=0, tiled=True)
-    length = heads.shape[0]
-    local_heads = heads.shape[1] // (3 * HEAD_DIM)
-    heads = heads.reshape(length, local_heads, 3, HEAD_DIM)
-    queries = heads[:, :, 0]
-    key_rows = heads[:, :, 1]
-    value_rows = heads[:, :, 2]
-    if earlier is None:
-        all_keys, all_values = (key_rows, value_rows)
-    else:
-        all_keys = jnp.concatenate([earlier[0], key_rows], axis=0)
-        all_values = jnp.concatenate([earlier[1], value_rows], axis=0)
-    attended, totals = attend_forward(queries, all_keys, all_values)
-    mixed = attended.reshape(length, local_heads * HEAD_DIM).astype(jnp.bfloat16)
+    packs = [heads] if earlier is None else [earlier, heads]
+    mixed, totals = attn_fwd(packs)
     mixed_rows = lax.all_to_all(mixed, "seq", split_axis=0, concat_axis=1, tiled=True)
     middle = stream + jnp.dot(mixed_rows, out_w, preferred_element_type=jnp.float32)
     normed_b = layer_norm(middle, gain_b).astype(jnp.bfloat16)
@@ -135,9 +234,8 @@
     stored = (
         stream,
         normed,
-        queries,
-        all_keys,
-        all_values,
+        packs,
+        mixed,
         totals,
         mixed_rows,
         middle,
@@ -145,7 +243,7 @@
         hidden,
         active,
     )
-    return (result, stored, (key_rows, value_rows))
+    return (result, stored, heads)
 
 
 def block_backward(upstream, stored, weights, carried):
@@ -153,9 +251,8 @@
     (
         stream,
         normed,
-        queries,
-        all_keys,
-        all_values,
+        packs,
+        mixed,
         totals,
         mixed_rows,
         middle,
@@ -175,22 +272,9 @@
     out_grad = contract_rows(mixed_rows, middle_bf)
     d_mixed = contract_cols(middle_bf, out_w).astype(jnp.bfloat16)
     d_heads = lax.all_to_all(d_mixed, "seq", split_axis=1, concat_axis=0, tiled=True)
-    length, local_heads = (queries.shape[0], queries.shape[1])
-    d_heads = d_heads.reshape(length, local_heads, HEAD_DIM)
-    query_grad, key_grad, value_grad = attend_backward(
-        queries, all_keys, all_values, d_heads, totals
-    )
-    earlier_len = key_grad.shape[0] - length
-    own_keys = key_grad[earlier_len:]
-    own_values = value_grad[earlier_len:]
-    passed = None
-    if earlier_len > 0:
-        passed = (key_grad[:earlier_len], value_grad[:earlier_len])
-    if carried is not None:
-        own_keys = own_keys + carried[0]
-        own_values = own_values + carried[1]
-    d_packed = jnp.stack([query_grad, own_keys, own_values], axis=2).astype(jnp.bfloat16)
-    d_packed = d_packed.reshape(length, local_heads * 3 * HEAD_DIM)
+    outs = attn_bwd(packs, d_heads, mixed, totals, carried)
+    d_packed = outs[0]
+    passed = outs[1] if len(outs) > 1 else None
     d_rows = lax.all_to_all(d_packed, "seq", split_axis=0, concat_axis=1, tiled=True)
     qkv_grad = contract_rows(normed, d_rows)
     d_normed = contract_cols(d_rows, qkv_w)

time: 1610 us -> 1020 us (0.63)
  matrix products: 640 us -> 109 us
  other arithmetic: 233 us -> 16.3 us
  Pallas kernels: 0 us -> 155 us
  blocking collectives: 96.8 us -> 196 us
  local copies, waits for them, and re-layouts: 89.5 us -> 47 us
  loops' own time: 28.1 us -> 0 us
    dot_general x56 -> x0, matrix products: 536 us -> none  [the longest x16 151 us: one_block(): jnp.einsum('qhd,khd->hqk', query_rows, key_rows, preferred_element_type=j...]
    pallas_call x0 -> x4, Pallas kernels: none -> 155 us  [the longest x2 92.9 us: attn_bwd(): pl.pallas_call(functools.partial(bwd_kernel, nsets, heads, bq, bk, add is...]
    convert_element_type x9 -> x0, other arithmetic: 112 us -> none  [the longest x8 112 us: one_block(): d_score = (chances * (d_chance - centre)).astype(jnp.bfloat16)]
    all_to_all x0 -> x4, blocking collectives: none -> 98.4 us  [the longest x2 66.3 us: block_forward(): lax.all_to_all(packed, 'seq', split_axis=1, concat_axis=0, tiled=True)]
    all_to_all x4 -> x0, waiting for transfers between devices: 79.7 us -> none  [the longest x2 56.5 us: block_forward(): lax.all_to_all(packed, 'seq', split_axis=1, concat_axis=0, tiled=True)]
    reduce_sum x8 -> x0, other arithmetic: 74.4 us -> none  [one_block(): row_sum = jnp.sum(weights, axis=-1, keepdims=True)]
    all_gather x1, waiting for transfers between devices: 37.5 us -> 73.1 us  [local(): lax.all_gather(down_weight, 'dp', axis=0, tiled=True)]
    all_gather x1, waiting for transfers between devices: 0.01 us -> 30.8 us  [local(): lax.all_gather(up_weight, 'dp', axis=0, tiled=True)]
  transfers between devices with their start and end apart: 15 -> 11, of which waited for: 12 -> 9; matrix products, arithmetic and copies ran while one was open for 11% -> 8% of each run, Pallas kernels for 0% -> 2%
where the time goes in v1:
time: 1020 us
  waiting for transfers between devices  468 us (46%)
  blocking collectives  196 us (19%)
  Pallas kernels  155 us (15%)
  matrix products  109 us (11%)
  local copies, waits for them, and re-layouts  47 us (5%)
  between operations  16.4 us (2%)
  other arithmetic  16.3 us (2%)
    reduce_scatter x1, waiting for transfers between devices, local(): lax.psum_scatter(summed[2].astype(jnp.bfloat16), 'dp', scatter_dimension=...  98.7 us
    reduce_scatter x1, waiting for transfers between devices, local(): lax.psum_scatter(summed[3].astype(jnp.bfloat16), 'dp', scatter_dimension=...  98.5 us
    pallas_call x2, Pallas kernels, attn_bwd(): pl.pallas_call(functools.partial(bwd_kernel, nsets, heads, bq, bk, add is...  92.9 us
    all_gather x1, waiting for transfers between devices, local(): lax.all_gather(down_weight, 'dp', axis=0, tiled=True)  73.1 us
    reduce_scatter x1, waiting for transfers between devices, local(): lax.psum_scatter(summed[0].astype(jnp.bfloat16), 'dp', scatter_dimension=...  70.3 us
    all_to_all x2, blocking collectives, block_forward(): lax.all_to_all(packed, 'seq', split_axis=1, concat_axis=0, tiled=True)  66.3 us
    pallas_call x2, Pallas kernels, attn_fwd(): pl.pallas_call(functools.partial(fwd_kernel, nsets, heads, bq, bk), out_s...  62.4 us
    unnamed x2, blocking collectives  44.1 us
  transfers between devices with their start and end apart: 11, of which 9 were waited for; matrix products, arithmetic and copies ran while one was open for 8% of the time, Pallas kernels for 2%

profile of v1, /device:TPU:0, one launch (start us, length us, event | category | flops | bytes accessed | tf_op | source)
XLA Modules:
  0.0 1016.7 jit_solution(10021808316945928993)
XLA Ops:
  12.0 23.7 %all-reduce.7 = (bf16[768]{0:T(1024)(128)(2,1)S(1)}, bf16[768]{0:T(1024)(128)(2,1)S(1)}, bf16[768]{0:T(1024)(128)(2,1)S(1)}) all-reduce(bf16[768]{0:T(1024)(128)(2,1)S(1)} %dynamic-update-slice, bf16[768]{0:T(1024)(128)(2,1)S(1)} %dynamic-update-slice.2, bf16[768]{0:T(1024)(128)(2,1)S(1)} %dynamic-update-slice.1), channel_id=1, replica_groups=mesh['seq'=4,'dp'=8] {'dp'}, use_global_device_ids=true, to_apply=%add | all-reduce | flops 2304 | bytes 9216
  36.3 42.2 %all-gather.5.cloned.1.call-done = bf16[768,2304]{1,0:T(8,128)(2,1)} async-done(((bf16[96,2304]{1,0:T(8,128)(2,1)}), bf16[768,2304]{1,0:T(8,128)(2,1)}) %all-gather.5.cloned.1.call-update) | async-done | bytes 3538960 | tf_op jit(solution)/shard_map/all_gather | solution.py:298
  88.5 33.0 %all_to_all.152 = bf16[512,4,576]{0,2,1:T(8,128)(2,1)} all-to-all(bf16[512,4,576]{0,2,1:T(8,128)(2,1)} %bitcast.119), channel_id=1, replica_groups=mesh['seq'=4,'dp'=8] {'seq'}, dimensions={1} | all-to-all | bytes 4718592 | tf_op jit(solution)/shard_map/all_to_all | solution.py:225
  125.9 24.1 %attn_fwd1.1 = (bf16[2048,192]{1,0:T(8,128)(2,1)}, f32[3,1,2048]{2,1,0:T(1,128)}) custom-call(bf16[2048,576]{1,0:T(8,128)(2,1)} %bitcast.110), custom_call_target="tpu_custom_call" | custom-call | tf_op jit(solution)/shard_map/attn_fwd1/pallas_call | solution.py:104
  156.0 11.6 %all-to-all-done.1 = bf16[4,512,192]{1,2,0:T(8,128)(2,1)S(1)} async-done(((bf16[4,512,192]{1,2,0:T(8,128)(2,1)}), bf16[4,512,192]{1,2,0:T(8,128)(2,1)S(1)}, u32[]{:S(2)}, u32[]{:S(2)}) %all-to-all-start.1) | async-done | bytes 786464 | tf_op jit(solution)/shard_map/all_to_all | solution.py:228
  170.3 30.8 %all-gather.9.cloned.1.call-done = bf16[768,3072]{1,0:T(8,128)(2,1)} async-done(((bf16[96,3072]{1,0:T(8,128)(2,1)}), bf16[768,3072]{1,0:T(8,128)(2,1)}) %all-gather.9.cloned.1.call-update) | async-done | bytes 4718608 | tf_op jit(solution)/shard_map/all_gather | solution.py:300
  208.1 73.1 %all-gather.11.cloned.1.call-done = bf16[3072,768]{1,0:T(8,128)(2,1)} async-done(((bf16[384,768]{1,0:T(8,128)(2,1)}), bf16[3072,768]{1,0:T(8,128)(2,1)}) %all-gather.11.cloned.1.call-update) | async-done | bytes 4718608 | tf_op jit(solution)/shard_map/all_gather | solution.py:301
  281.2 7.5 fusion.69
  297.0 33.2 %all_to_all.153 = bf16[512,4,576]{0,2,1:T(8,128)(2,1)} all-to-all(bf16[512,4,576]{0,2,1:T(8,128)(2,1)} %bitcast.121), channel_id=1, replica_groups=mesh['seq'=4,'dp'=8] {'seq'}, dimensions={1} | all-to-all | bytes 4718592 | tf_op jit(solution)/shard_map/all_to_all | solution.py:225
  334.6 38.3 %attn_fwd2.1 = (bf16[2048,192]{1,0:T(8,128)(2,1)}, f32[3,1,2048]{2,1,0:T(1,128)}) custom-call(bf16[2048,576]{1,0:T(8,128)(2,1)} %bitcast.111, bf16[2048,576]{1,0:T(8,128)(2,1)} %bitcast.114), custom_call_target="tpu_custom_call" | custom-call | tf_op jit(solution)/shard_map/attn_fwd2/pallas_call | solution.py:104
  374.4 14.7 %all_to_all.154 = bf16[4,512,192]{1,2,0:T(8,128)(2,1)S(1)} all-to-all(bf16[4,512,192]{1,2,0:T(8,128)(2,1)S(1)} %copy.39), channel_id=1, replica_groups=mesh['seq'=4,'dp'=8] {'seq'}, dimensions={0} | all-to-all | bytes 1572864 | tf_op jit(solution)/shard_map/all_to_all | solution.py:228
  410.9 16.1 %all_to_all.155 = bf16[512,4,192]{0,2,1:T(8,128)(2,1)} all-to-all(bf16[512,4,192]{0,2,1:T(8,128)(2,1)} %bitcast.133), channel_id=1, replica_groups=mesh['seq'=4,'dp'=8] {'seq'}, dimensions={1} | all-to-all | bytes 1572864 | tf_op jit(solution)/shard_map/all_to_all | solution.py:274
  429.2 57.8 %attn_bwd2.1 = (bf16[2048,576]{1,0:T(8,128)(2,1)}, f32[3,2048,128]{2,1,0:T(8,128)}) custom-call(bf16[2048,576]{1,0:T(8,128)(2,1)} %bitcast.112, bf16[2048,576]{1,0:T(8,128)(2,1)} %bitcast.115, bf16[2048,192]{1,0:T(8,128)(2,1)} %bitcast.128, bf16[2048,192]{1,0:T(8,128)(2,1)} %get-tuple-element.16.refs_3_, f32[3,1,2048]{2,1,0:T(1,128)} %get-tuple-element.17.refs_4_), custom_call_target="tpu_custom_call" | custom-call | tf_op jit(solution)/shard_map/attn_bwd2/pallas_call | solution.py:201
  491.4 33.1 %all_to_all.156 = bf16[4,512,576]{1,2,0:T(8,128)(2,1)S(1)} all-to-all(bf16[4,512,576]{1,2,0:T(8,128)(2,1)} %copy.42), channel_id=1, replica_groups=mesh['seq'=4,'dp'=8] {'seq'}, dimensions={0} | all-to-all | bytes 4718592 | tf_op jit(solution)/shard_map/all_to_all | solution.py:278
  547.2 16.1 %all_to_all.157 = bf16[512,4,192]{0,2,1:T(8,128)(2,1)} all-to-all(bf16[512,4,192]{0,2,1:T(8,128)(2,1)} %bitcast.134), channel_id=1, replica_groups=mesh['seq'=4,'dp'=8] {'seq'}, dimensions={1} | all-to-all | bytes 1572864 | tf_op jit(solution)/shard_map/all_to_all | solution.py:274
  565.5 35.1 %attn_bwd1.1 = bf16[2048,576]{1,0:T(8,128)(2,1)} custom-call(bf16[2048,576]{1,0:T(8,128)(2,1)} %bitcast.113, bf16[2048,192]{1,0:T(8,128)(2,1)} %bitcast.126, bf16[2048,192]{1,0:T(8,128)(2,1)} %get-tuple-element.15.refs_2_, f32[3,1,2048]{2,1,0:T(1,128)} %get-tuple-element.19.refs_3_, f32[3,2048,128]{2,1,0:T(8,128)} %get-tuple-element.20.refs_4_), custom_call_target="tpu_custom_call" | custom-call | tf_op jit(solution)/shard_map/attn_bwd1/pallas_call | solution.py:201
  614.1 23.9 %all-to-all-done.7 = bf16[4,512,576]{1,2,0:T(8,128)(2,1)} async-done(((bf16[4,512,576]{1,2,0:T(8,128)(2,1)}), bf16[4,512,576]{1,2,0:T(8,128)(2,1)}, u32[]{:S(2)}, u32[]{:S(2)}) %all-to-all-start.7) | async-done | bytes 2359328 | tf_op jit(solution)/shard_map/all_to_all | solution.py:278
  653.5 8.8 add_convert_fusion
  674.0 8.9 fusion.29
  688.0 70.3 %reduce-scatter.5.cloned.1.call-done = bf16[96,2304]{1,0:T(8,128)(2,1)} async-done(((bf16[768,2304]{1,0:T(8,128)(2,1)}), bf16[96,2304]{1,0:T(8,128)(2,1)}) %reduce-scatter.5.cloned.1.call-update) | async-done | bytes 442384 | tf_op jit(solution)/shard_map/reduce_scatter | solution.py:324
  758.4 98.5 %reduce-scatter.11.cloned.1.call-done = bf16[384,768]{1,0:T(8,128)(2,1)} async-done(((bf16[3072,768]{1,0:T(8,128)(2,1)}), bf16[384,768]{1,0:T(8,128)(2,1)}) %reduce-scatter.11.cloned.1.call-update) | async-done | bytes 589840 | tf_op jit(solution)/shard_map/reduce_scatter | solution.py:333
  856.9 98.7 %reduce-scatter.9.cloned.1.call-done = bf16[96,3072]{1,0:T(8,128)(2,1)} async-done(((bf16[768,3072]{1,0:T(8,128)(2,1)}), bf16[96,3072]{1,0:T(8,128)(2,1)}) %reduce-scatter.9.cloned.1.call-update) | async-done | bytes 589840 | tf_op jit(solution)/shard_map/reduce_scatter | solution.py:330
  957.9 20.4 %all-reduce.6 = (bf16[768]{0:T(1024)(128)(2,1)S(1)}, bf16[768]{0:T(1024)(128)(2,1)S(1)}, bf16[768]{0:T(1024)(128)(2,1)S(1)}) all-reduce(bf16[768]{0:T(1024)(128)(2,1)S(1)} %get-tuple-element.64, bf16[768]{0:T(1024)(128)(2,1)S(1)} %get-tuple-element.63, ...), channel_id=6, replica_groups=mesh['seq'=4,'dp'=8] {'dp'}, use_global_device_ids=true, to_apply=%region_26.0.clone | all-reduce | flops 2304 | bytes 9216
  988.9 15.8 %all-reduce.12.cloned.1.call-done = (bf16[96,2304]{1,0:T(8,128)(2,1)}, bf16[96,768]{1,0:T(8,128)(2,1)}, bf16[96,3072]{1,0:T(8,128)(2,1)}, bf16[384,768]{1,0:T(8,128)(2,1)}) async-done(((bf16[96,2304]{1,0:T(8,128)(2,1)}, bf16[96,768]{1,0:T(8,128)(2,1)}, bf16[96,3072]{1,0:T(8,128)(2,1)}, bf16[384,768]{1,0:T(8,128)(2,1)}), (bf16[96,2304]{1,0:T(8,128)(2,1)}, bf16[96,768]{1,0:T(8,128)(2,1)}, ...) | async-done | bytes 1769488 | tf_op jit(solution)/shard_map/psum | solution.py:347
  (207 shorter events, 164.6 us)
Async XLA Ops:
  7.2 28.5 %copy-start.7 = (bf16[1,512,768]{2,1,0:T(8,128)(2,1)S(1)}, bf16[1,512,768]{2,1,0:T(8,128)(2,1)}, u32[]{:S(2)}) copy-start(bf16[1,512,768]{2,1,0:T(8,128)(2,1)} %param.9) | copy-start | bytes 2359300
  7.2 71.3 %all-gather.5.cloned.1.call-start = ((), (), s32[]{:S(2)}) async-start(), calls=%async_computation.12 | async-start | bytes 3981312 | tf_op jit(solution)/shard_map/all_gather | solution.py:298
  8.0 148.0 %all-gather.7.cloned.1.call-start = ((), (), s32[]{:S(2)}) async-start(), calls=%async_computation.13 | async-start | bytes 1327104 | tf_op jit(solution)/shard_map/all_gather | solution.py:299
  8.7 192.4 %all-gather.9.cloned.1.call-start = ((), (), s32[]{:S(2)}) async-start(), calls=%async_computation.14 | async-start | bytes 5308416 | tf_op jit(solution)/shard_map/all_gather | solution.py:300
  9.4 271.8 %all-gather.11.cloned.1.call-start = ((), (), s32[]{:S(2)}) async-start(), calls=%async_computation.15 | async-start | bytes 5308416 | tf_op jit(solution)/shard_map/all_gather | solution.py:301
  36.3 47.9 %copy-start.27 = (f32[512]{0:T(512)}, f32[512]{0:T(512)S(1)}, u32[]{:S(2)}) copy-start(f32[512]{0:T(512)S(1)} %fusion.24) | copy-start | bytes 6148
  152.2 15.3 %all-to-all-start.1 = ((bf16[4,512,192]{1,2,0:T(8,128)(2,1)}), bf16[4,512,192]{1,2,0:T(8,128)(2,1)S(1)}, u32[]{:S(2)}, u32[]{:S(2)}) async-start(bf16[4,512,192]{1,2,0:T(8,128)(2,1)} %copy.36), calls=%async_computation.1 | async-start | bytes 1572864 | tf_op jit(solution)/shard_map/all_to_all | solution.py:228
  170.0 111.3 %copy-start.4 = (f32[512,768]{1,0:T(8,128)}, f32[512,768]{1,0:T(8,128)S(1)}, u32[]{:S(2)}) copy-start(f32[512,768]{1,0:T(8,128)S(1)} %get-tuple-element.53) | copy-start | bytes 4718596
  281.2 7.8 copy-start.30
  374.3 14.7 %copy-start.22 = (bf16[768,768]{1,0:T(8,128)(2,1)S(1)}, bf16[768,768]{1,0:T(8,128)(2,1)}, u32[]{:S(2)}) copy-start(bf16[768,768]{1,0:T(8,128)(2,1)} %all-gather.7.cloned.1.call-done) | copy-start | bytes 3538948
  390.3 11.1 %slice-start.4 = ((s8[4718592]{0:T(1024)(128)(4,1)}), s8[4194304]{0:T(1024)(128)(4,1)S(1)}, s32[]{:S(2)}) async-start(s8[4718592]{0:T(1024)(128)(4,1)} %bitcast.140), calls=%async_computation.25 | async-start | bytes 8388608
  491.4 40.4 %slice-start.2 = ((s8[4718592]{0:T(1024)(128)(4,1)}), s8[4194304]{0:T(1024)(128)(4,1)S(1)}, s32[]{:S(2)}) async-start(s8[4718592]{0:T(1024)(128)(4,1)} %bitcast.138), calls=%async_computation.23 | async-start | bytes 8388608
  491.4 40.4 %slice-start.8 = ((s8[6291456]{0:T(1024)(128)(4,1)}), s8[4194304]{0:T(1024)(128)(4,1)S(1)}, s32[]{:S(2)}) async-start(s8[6291456]{0:T(1024)(128)(4,1)} %bitcast.144), calls=%async_computation.29 | async-start | bytes 8388608
  524.4 7.4 slice-start.9
  531.8 9.9 copy-start.13
  604.9 33.1 %all-to-all-start.7 = ((bf16[4,512,576]{1,2,0:T(8,128)(2,1)}), bf16[4,512,576]{1,2,0:T(8,128)(2,1)}, u32[]{:S(2)}, u32[]{:S(2)}) async-start(bf16[4,512,576]{1,2,0:T(8,128)(2,1)} %copy.45), calls=%async_computation.7 | async-start | bytes 4718592 | tf_op jit(solution)/shard_map/all_to_all | solution.py:278
  609.4 78.6 %reduce-scatter.7.cloned.1.call-start = ((), (), s32[]{:S(2)}) async-start(), calls=%async_computation.17 | async-start | bytes 1327104 | tf_op jit(solution)/shard_map/reduce_scatter | solution.py:327
  614.1 144.3 %reduce-scatter.5.cloned.1.call-start = ((), (), s32[]{:S(2)}) async-start(), calls=%async_computation.16 | async-start | bytes 3981312 | tf_op jit(solution)/shard_map/reduce_scatter | solution.py:324
  646.5 210.4 %reduce-scatter.11.cloned.1.call-start = ((), (), s32[]{:S(2)}) async-start(), calls=%async_computation.19 | async-start | bytes 5308416 | tf_op jit(solution)/shard_map/reduce_scatter | solution.py:333
  662.4 293.2 %reduce-scatter.9.cloned.1.call-start = ((), (), s32[]{:S(2)}) async-start(), calls=%async_computation.18 | async-start | bytes 5308416 | tf_op jit(solution)/shard_map/reduce_scatter | solution.py:330
  673.3 331.4 %all-reduce.12.cloned.1.call-start = ((), (), s32[]{:S(2)}) async-start(), calls=%async_computation.20 | async-start | bytes 3538944 | tf_op jit(solution)/shard_map/psum | solution.py:347
  674.0 9.0 copy-start.8
  674.0 9.0 copy-start.31
  955.6 30.1 %copy-start.1 = (f32[512,768]{1,0:T(8,128)S(1)}, f32[512,768]{1,0:T(8,128)}, u32[]{:S(2)}) copy-start(f32[512,768]{1,0:T(8,128)} %copy-done) | copy-start | bytes 4718596
  (35 other events, 127.3 us)
Sparse Core Ops, SparseCore 0:
  10.2 68.2 all-gather.4
  80.7 39.5 all-gather.6
  122.5 78.6 all-gather.8
  203.2 78.0 all-gather.10
  614.2 62.5 reduce-scatter.6
  680.3 78.0 reduce-scatter.4
  762.0 94.8 reduce-scatter.10
  860.5 95.0 reduce-scatter.8
  958.2 46.4 all-reduce.11

commit v2 on v0

v2 whole, which is shorter than its diff:
```python
import functools

import jax
import jax.numpy as jnp
from jax import lax
from jax.experimental import pallas as pl
from jax.experimental.pallas import tpu as pltpu
from jax.sharding import PartitionSpec as P

HEAD_DIM = 64


epsilon = 1e-05


def layer_norm(vector, gain_vec):
    centre = vector - jnp.mean(vector, axis=-1, keepdims=True)
    spread = jnp.mean(centre * centre, axis=-1, keepdims=True)
    return centre * lax.rsqrt(spread + epsilon) * gain_vec


def gelu_value(vector):
    return jax.nn.gelu(vector, approximate=True)


def contract_rows(left_side, right_side):
    return lax.dot_general(
        left_side, right_side, (((0,), (0,)), ((), ())), preferred_element_type=jnp.float32
    )


def contract_cols(left_side, right_side):
    return lax.dot_general(
        left_side, right_side, (((1,), (1,)), ((), ())), preferred_element_type=jnp.float32
    )


def nt(left, right):
    return lax.dot_general(
        left, right, (((1,), (1,)), ((), ())), preferred_element_type=jnp.float32
    )


def nn(left, right):
    return lax.dot_general(
        left, right, (((1,), (0,)), ((), ())), preferred_element_type=jnp.float32
    )


def remote(src, dst, send_sem, recv_sem, device):
    return pltpu.make_async_remote_copy(
        src_ref=src,
        dst_ref=dst,
        send_sem=send_sem,
        recv_sem=recv_sem,
        device_id=device,
        device_id_type=pl.DeviceIdType.MESH,
    )


def greet(devices):
    barrier = pltpu.get_barrier_semaphore()
    for device in devices:
        pl.semaphore_signal(
            barrier, inc=1, device_id=device, device_id_type=pl.DeviceIdType.MESH
        )
    pl.semaphore_wait(barrier, len(devices))


def seq_peers(seq):
    me = lax.axis_index("seq")
    return [lax.rem(me + d, seq) for d in range(1, seq)]


class Gather:
    def __init__(self, seq, dp, shards, wholes, sems):
        self.line = dp // 2
        self.shards, self.wholes = shards, wholes
        self.z_send, self.z_recv, self.y_send, self.y_recv, self.c_send, self.c_recv, self.own = sems
        me = lax.axis_index("seq")
        self.core = lax.rem(me, 2)
        self.core_peer = {"seq": me + 1 - 2 * self.core}
        self.rank = lax.axis_index("dp")
        self.a, self.b = lax.div(self.rank, 2), lax.rem(self.rank, 2)
        self.y_peer = {"dp": self.a * 2 + 1 - self.b}
        self.sent = []

    @staticmethod
    def sems(units, dp):
        line = dp // 2
        dma = pltpu.SemaphoreType.DMA
        return [
            dma((units, line)),
            dma((units, line)),
            dma((units, line)),
            dma((units, line)),
            dma((units, 2 * line)),
            dma((units, 2 * line)),
            dma((units,)),
        ]

    def z_rank(self, offset):
        return lax.rem(self.a + offset, self.line) * 2 + self.b

    def peers(self):
        z = [{"dp": self.z_rank(d)} for d in range(1, self.line)]
        return z + [self.y_peer]

    def place(self, unit, rank):
        rows, columns = self.shards[unit].shape
        half = columns // 2
        return (
            pl.ds(pl.multiple_of(rank * rows, 8), rows),
            pl.ds(pl.multiple_of(self.core * half, 128), half),
        )

    def send(self, src, dst, send_sem, recv_sem, device):
        copy = remote(src, dst, send_sem, recv_sem, device)
        copy.start()
        self.sent.append(copy)
        return copy

    def start(self, unit):
        shard, whole = self.shards[unit], self.wholes[unit]
        where = self.place(unit, self.rank)
        mine = shard.at[:, where[1]]
        self.z_copies = getattr(self, "z_copies", {})
        self.y_copies = getattr(self, "y_copies", {})
        self.c_copies = getattr(self, "c_copies", {})
        for d in range(1, self.line):
            self.z_copies[unit, d] = self.send(
                mine,
                whole.at[where],
                self.z_send.at[unit, d],
                self.z_recv.at[unit, d],
                {"dp": self.z_rank(d)},
            )
        self.y_copies[unit, 0] = self.send(
            mine, whole.at[where], self.y_send.at[unit, 0], self.y_recv.at[unit, 0], self.y_peer
        )
        local_copy = pltpu.make_async_copy(
            shard, whole.at[where[0]], self.own.at[unit]
        )
        local_copy.start()
        self.c_copies[unit, 0] = local_copy

    def to_core(self, unit, slot, rank):
        block = self.wholes[unit].at[self.place(unit, rank)]
        self.c_copies[unit, slot] = self.send(
            block, block, self.c_send.at[unit, slot], self.c_recv.at[unit, slot], self.core_peer
        )

    def forward_z(self, unit):
        for d in range(1, self.line):
            self.z_copies[unit, d].wait_recv()
            rank = self.z_rank(self.line - d)
            block = self.wholes[unit].at[self.place(unit, rank)]
            self.y_copies[unit, d] = self.send(
                block, block, self.y_send.at[unit, d], self.y_recv.at[unit, d], self.y_peer
            )
            self.to_core(unit, d, rank)

    def forward_y(self, unit):
        for d in range(self.line):
            self.y_copies[unit, d].wait_recv()
            rank = lax.rem(self.a + self.line - d, self.line) * 2 + 1 - self.b
            self.to_core(unit, self.line + d, rank)

    def finish(self, unit):
        for slot in range(1, 2 * self.line):
            self.c_copies[unit, slot].wait_recv()
        self.c_copies[unit, 0].wait()

    def drain(self):
        for copy in self.sent:
            copy.wait_send()


def gather_kernel(seq, dp, units, *refs):
    shards, wholes, sems = refs[:units], refs[units : 2 * units], refs[2 * units :]
    gather = Gather(seq, dp, shards, wholes, sems)
    greet(gather.peers() + [gather.core_peer])
    for unit in range(units):
        gather.start(unit)
    for unit in range(units):
        gather.forward_z(unit)
    for unit in range(units):
        gather.forward_y(unit)
    for unit in range(units):
        gather.finish(unit)
    gather.drain()


def whole_shape(shard, dp):
    return jax.ShapeDtypeStruct((shard.shape[0] * dp, shard.shape[1]), shard.dtype)


def gather_now(seq, dp, shards):
    units = len(shards)
    hbm = pl.BlockSpec(memory_space=pl.ANY)
    return pl.pallas_call(
        functools.partial(gather_kernel, seq, dp, units),
        out_shape=tuple(whole_shape(shard, dp) for shard in shards),
        in_specs=[hbm] * units,
        out_specs=(hbm,) * units,
        scratch_shapes=Gather.sems(units, dp),
        compiler_params=pltpu.CompilerParams(
            collective_id=0, has_side_effects=True, vmem_limit_bytes=4 << 20
        ),
        name="gather_first",
    )(*shards)


def causal_mask(size):
    rows = lax.broadcasted_iota(jnp.int32, (size, size), 0)
    columns = lax.broadcasted_iota(jnp.int32, (size, size), 1)
    return rows <= columns


def forward_kernel(seq, dp, sets, units, heads, *refs):
    refs = list(refs)

    def take(count):
        taken = refs[:count]
        del refs[:count]
        return taken

    (packed,) = take(1)
    earlier = take(sets - 1)
    shards = take(units)
    heads_out, mixed_out, own_out, totals_out = take(4)
    wholes = take(units)
    arrived, mixed_in, q_s, k_s, v_s, in_send, in_recv, out_send, out_recv = take(9)
    gather = Gather(seq, dp, shards, wholes, refs) if units else None

    tokens = packed.shape[1]
    length = tokens * seq
    group = 3 * HEAD_DIM
    me = lax.axis_index("seq")
    peers = seq_peers(seq)
    greet([{"seq": peer} for peer in peers] + (gather.peers() if units else []))

    own_lanes = pl.ds(pl.multiple_of(me * tokens, tokens), tokens)
    copies = {}
    for h in range(heads):
        for d, peer in enumerate(peers):
            copy = remote(
                packed.at[pl.ds(pl.multiple_of((peer * heads + h) * group, group), group)],
                arrived.at[pl.ds(h * group, group), own_lanes],
                in_send.at[h, d],
                in_recv.at[h, d],
                {"seq": peer},
            )
            copy.start()
            copies[h, d] = copy
    for unit in range(units):
        gather.start(unit)
    for h in range(heads):
        arrived[h * group : (h + 1) * group, own_lanes] = packed[
            pl.ds(pl.multiple_of((me * heads + h) * group, group), group), :
        ]

    mask = causal_mask(tokens)
    for s in range(sets):
        v_s[s, HEAD_DIM:] = jnp.ones((16, length), jnp.bfloat16)
    results = []
    for h in range(heads):
        c0 = h * group
        for s in range(sets):
            source = earlier[s] if s < sets - 1 else arrived
            if s == sets - 1:
                for d in range(seq - 1):
                    copies[h, d].wait_recv()
                heads_out[c0 : c0 + group, :] = arrived[c0 : c0 + group, :]
                q_s[...] = arrived[c0 : c0 + HEAD_DIM, :] * jnp.bfloat16(HEAD_DIM**-0.5)
            k_s[s] = source[c0 + HEAD_DIM : c0 + 2 * HEAD_DIM, :].T
            v_s[s, :HEAD_DIM] = source[c0 + 2 * HEAD_DIM : c0 + 3 * HEAD_DIM, :]

        for i in range(seq):
            queries = q_s[:, i * tokens : (i + 1) * tokens]
            peak = total = None
            for j in [i] + list(range(i)):
                keys = slice(j * tokens, (j + 1) * tokens)
                scores = []
                for s in range(sets):
                    block = nn(k_s[s, keys, :], queries)
                    if j == i:
                        block = jnp.where(mask, block, -1e30)
                    scores.append(block)
                peak_now = peak
                for block in scores:
                    top = jnp.max(block, axis=0, keepdims=True)
                    peak_now = top if peak_now is None else jnp.maximum(peak_now, top)
                if total is not None:
                    total = total * jnp.exp(peak - peak_now)
                for s, block in enumerate(scores):
                    weights = jnp.exp(block - peak_now).astype(jnp.bfloat16)
                    part = nn(v_s[s, :, keys], weights)
                    total = part if total is None else total + part
                peak = peak_now
            row_sum = total[HEAD_DIM : HEAD_DIM + 1]
            own_out[h * HEAD_DIM : (h + 1) * HEAD_DIM, i * tokens : (i + 1) * tokens] = (
                total[:HEAD_DIM] / row_sum
            ).astype(jnp.bfloat16)
            totals_out[h, :, i * tokens : (i + 1) * tokens] = peak + jnp.log(row_sum)

        mine = pl.ds(pl.multiple_of((me * heads + h) * HEAD_DIM, HEAD_DIM), HEAD_DIM)
        for d, peer in enumerate(peers):
            copy = remote(
                own_out.at[
                    pl.ds(h * HEAD_DIM, HEAD_DIM),
                    pl.ds(pl.multiple_of(peer * tokens, tokens), tokens),
                ],
                mixed_in.at[mine],
                out_send.at[h, d],
                out_recv.at[h, d],
                {"seq": peer},
            )
            copy.start()
            results.append(copy)
        mixed_in[mine] = own_out[h * HEAD_DIM : (h + 1) * HEAD_DIM, own_lanes]
        if units:
            if h == 0:
                gather.forward_z(0)
            elif h == 1:
                gather.forward_y(0)
                gather.forward_z(1)
    if units:
        gather.forward_z(2)
        gather.forward_y(1)
        gather.forward_y(2)
        for unit in range(units):
            gather.finish(unit)
        gather.drain()
    for copy in copies.values():
        copy.wait_send()
    for copy in results:
        copy.wait()
    mixed_out[...] = mixed_in[...]


def attend_forward(seq, dp, heads, packed, earlier, shards, call_id):
    width, tokens = packed.shape
    length = tokens * seq
    sets, units = 1 + len(earlier), len(shards)
    rows = heads * 3 * HEAD_DIM
    vmem = pl.BlockSpec(memory_space=pltpu.VMEM)
    hbm = pl.BlockSpec(memory_space=pl.ANY)
    dma = pltpu.SemaphoreType.DMA
    outs = pl.pallas_call(
        functools.partial(forward_kernel, seq, dp, sets, units, heads),
        out_shape=(
            jax.ShapeDtypeStruct((rows, length), jnp.bfloat16),
            jax.ShapeDtypeStruct((width // 3, tokens), jnp.bfloat16),
            jax.ShapeDtypeStruct((heads * HEAD_DIM, length), jnp.bfloat16),
            jax.ShapeDtypeStruct((heads, 1, length), jnp.float32),
        )
        + tuple(whole_shape(shard, dp) for shard in shards),
        in_specs=[vmem] * sets + [hbm] * units,
        out_specs=(vmem,) * 4 + (hbm,) * units,
        scratch_shapes=[
            pltpu.VMEM((rows, length), jnp.bfloat16),
            pltpu.VMEM((width // 3, tokens), jnp.bfloat16),
            pltpu.VMEM((HEAD_DIM, length), jnp.bfloat16),
            pltpu.VMEM((sets, length, HEAD_DIM), jnp.bfloat16),
            pltpu.VMEM((sets, HEAD_DIM + 16, length), jnp.bfloat16),
            dma((heads, seq)),
            dma((heads, seq)),
            dma((heads, seq)),
            dma((heads, seq)),
        ]
        + (Gather.sems(units, dp) if units else []),
        compiler_params=pltpu.CompilerParams(
            collective_id=call_id, has_side_effects=True, vmem_limit_bytes=40 << 20
        ),
        name=f"attend_forward_{sets}",
    )(packed, *earlier, *shards)
    return outs[:4], outs[4:]


def backward_kernel(seq, sets, carried, heads, *refs):
    refs = list(refs)

    def take(count):
        taken = refs[:count]
        del refs[:count]
        return taken

    (d_mixed,) = take(1)
    packs = take(sets)
    own_in, totals_in = take(2)
    carry_in = take(1)[0] if carried else None
    (d_packed_out,) = take(1)
    carry_out = take(1)[0] if sets == 2 else None
    arrived, local_grad, d_packed_in, q_s, k_s, kt_s, v_s, delta_s, dq_s, dkv_s = take(10)
    in_send, in_recv, out_send, out_recv = refs

    tokens = d_mixed.shape[1]
    length = tokens * seq
    group = 3 * HEAD_DIM
    me = lax.axis_index("seq")
    peers = seq_peers(seq)
    greet([{"seq": peer} for peer in peers])
    own_lanes = pl.ds(pl.multiple_of(me * tokens, tokens), tokens)
    scale = jnp.bfloat16(HEAD_DIM**-0.5)

    copies = {}
    for h in range(heads):
        for d, peer in enumerate(peers):
            copy = remote(
                d_mixed.at[pl.ds(pl.multiple_of((peer * heads + h) * HEAD_DIM, HEAD_DIM), HEAD_DIM)],
                arrived.at[pl.ds(h * HEAD_DIM, HEAD_DIM), own_lanes],
                in_send.at[h, d],
                in_recv.at[h, d],
                {"seq": peer},
            )
            copy.start()
            copies[h, d] = copy
    for h in range(heads):
        arrived[h * HEAD_DIM : (h + 1) * HEAD_DIM, own_lanes] = d_mixed[
            pl.ds(pl.multiple_of((me * heads + h) * HEAD_DIM, HEAD_DIM), HEAD_DIM), :
        ]

    mask = causal_mask(tokens)
    results = []
    for h in range(heads):
        c0 = h * group
        r0 = h * HEAD_DIM
        q_s[...] = packs[-1][c0 : c0 + HEAD_DIM, :] * scale
        for s in range(sets):
            keys = packs[s][c0 + HEAD_DIM : c0 + 2 * HEAD_DIM, :]
            k_s[s] = keys.T
            kt_s[s] = keys * scale
            v_s[s] = packs[s][c0 + 2 * HEAD_DIM : c0 + 3 * HEAD_DIM, :].T
        for d in range(seq - 1):
            copies[h, d].wait_recv()
        delta_s[...] = jnp.sum(
            arrived[r0 : r0 + HEAD_DIM, :].astype(jnp.float32)
            * own_in[r0 : r0 + HEAD_DIM, :].astype(jnp.float32),
            axis=0,
            keepdims=True,
        )
        for j in range(seq):
            keys = slice(j * tokens, (j + 1) * tokens)
            for i in range(j, seq):
                span = slice(i * tokens, (i + 1) * tokens)
                queries = q_s[:, span]
                grads = arrived[r0 : r0 + HEAD_DIM, span]
                d_query = dq_s[:, span] if j > 0 else None
                for s in range(sets):
                    chances = jnp.exp(nn(k_s[s, keys, :], queries) - totals_in[h, :, span])
                    if i == j:
                        chances = jnp.where(mask, chances, 0.0)
                    d_chance = nn(v_s[s, keys, :], grads)
                    d_score = (chances * (d_chance - delta_s[:, span])).astype(jnp.bfloat16)
                    d_key = nt(queries, d_score)
                    d_value = nt(grads, chances.astype(jnp.bfloat16))
                    if i == j:
                        if carried:
                            d_key = d_key + carry_in[h, :HEAD_DIM, keys]
                            d_value = d_value + carry_in[h, HEAD_DIM:, keys]
                        dkv_s[s, :HEAD_DIM, keys] = d_key
                        dkv_s[s, HEAD_DIM:, keys] = d_value
                    else:
                        dkv_s[s, :HEAD_DIM, keys] += d_key
                        dkv_s[s, HEAD_DIM:, keys] += d_value
                    part = nn(kt_s[s, :, keys], d_score)
                    d_query = part if d_query is None else d_query + part
                dq_s[:, span] = d_query
            local_grad[c0 : c0 + HEAD_DIM, keys] = dq_s[:, keys].astype(jnp.bfloat16)
            local_grad[c0 + HEAD_DIM : c0 + group, keys] = dkv_s[sets - 1, :, keys].astype(
                jnp.bfloat16
            )
        if sets == 2:
            carry_out[h] = dkv_s[0]
        mine = pl.ds(pl.multiple_of((me * heads + h) * group, group), group)
        for d, peer in enumerate(peers):
            copy = remote(
                local_grad.at[
                    pl.ds(c0, group), pl.ds(pl.multiple_of(peer * tokens, tokens), tokens)
                ],
                d_packed_in.at[mine],
                out_send.at[h, d],
                out_recv.at[h, d],
                {"seq": peer},
            )
            copy.start()
            results.append(copy)
        d_packed_in[mine] = local_grad[c0 : c0 + group, own_lanes]
    for copy in copies.values():
        copy.wait_send()
    for copy in results:
        copy.wait()
    d_packed_out[...] = d_packed_in[...]


def attend_backward(seq, heads, d_mixed, packs, own, totals, carried, call_id):
    width, tokens = d_mixed.shape
    length = tokens * seq
    sets = len(packs)
    rows = heads * 3 * HEAD_DIM
    extra = [] if carried is None else [carried]
    vmem = pl.BlockSpec(memory_space=pltpu.VMEM)
    dma = pltpu.SemaphoreType.DMA
    out_shape = [jax.ShapeDtypeStruct((3 * width, tokens), jnp.bfloat16)]
    if sets == 2:
        out_shape.append(jax.ShapeDtypeStruct((heads, 2 * HEAD_DIM, length), jnp.float32))
    return pl.pallas_call(
        functools.partial(backward_kernel, seq, sets, bool(extra), heads),
        out_shape=tuple(out_shape),
        in_specs=[vmem] * (3 + sets + len(extra)),
        out_specs=(vmem,) * len(out_shape),
        scratch_shapes=[
            pltpu.VMEM((heads * HEAD_DIM, length), jnp.bfloat16),
            pltpu.VMEM((rows, length), jnp.bfloat16),
            pltpu.VMEM((3 * width, tokens), jnp.bfloat16),
            pltpu.VMEM((HEAD_DIM, length), jnp.bfloat16),
            pltpu.VMEM((sets, length, HEAD_DIM), jnp.bfloat16),
            pltpu.VMEM((sets, HEAD_DIM, length), jnp.bfloat16),
            pltpu.VMEM((sets, length, HEAD_DIM), jnp.bfloat16),
            pltpu.VMEM((1, length), jnp.float32),
            pltpu.VMEM((HEAD_DIM, length), jnp.float32),
            pltpu.VMEM((sets, 2 * HEAD_DIM, length), jnp.float32),
            dma((heads, seq)),
            dma((heads, seq)),
            dma((heads, seq)),
            dma((heads, seq)),
        ],
        compiler_params=pltpu.CompilerParams(
            collective_id=call_id, has_side_effects=True, vmem_limit_bytes=48 << 20
        ),
        name=f"attend_backward_{sets}",
    )(d_mixed, *packs, own, totals, *extra)


def block_forward(sizes, call_id, stream, qkv_w, gains, earlier, weights, shards):
    seq, dp, heads = sizes
    normed = layer_norm(stream, gains[0]).astype(jnp.bfloat16)
    packed = lax.dot_general(
        qkv_w, normed, (((0,), (1,)), ((), ())), preferred_element_type=jnp.float32
    ).astype(jnp.bfloat16)
    (head_rows, mixed, own, totals), gathered = attend_forward(
        seq, dp, heads, packed, earlier, shards, call_id
    )
    out_w, up_w, down_w = weights or gathered
    middle = stream + contract_rows(mixed, out_w)
    normed_b = layer_norm(middle, gains[1]).astype(jnp.bfloat16)
    hidden = jnp.dot(normed_b, up_w, preferred_element_type=jnp.float32)
    active = gelu_value(hidden).astype(jnp.bfloat16)
    result = middle + jnp.dot(active, down_w, preferred_element_type=jnp.float32)
    stored = (stream, normed, earlier + [head_rows], own, totals, mixed, middle, normed_b, hidden, active)
    return result, stored, (out_w, up_w, down_w)


def block_backward(sizes, call_id, upstream, stored, qkv_w, gains, weights, carried):
    seq, dp, heads = sizes
    out_w, up_w, down_w = weights
    stream, normed, packs, own, totals, mixed, middle, normed_b, hidden, active = stored
    out_bf = upstream.astype(jnp.bfloat16)
    down_grad = contract_rows(active, out_bf)
    d_active = contract_cols(out_bf, down_w)
    d_hidden = jax.vjp(gelu_value, hidden)[1](d_active)[0].astype(jnp.bfloat16)
    up_grad = contract_rows(normed_b, d_hidden)
    d_normed_b = contract_cols(d_hidden, up_w)
    d_middle_norm, gain_b_grad = jax.vjp(layer_norm, middle, gains[1])[1](d_normed_b)
    d_middle = upstream + d_middle_norm
    middle_bf = d_middle.astype(jnp.bfloat16)
    out_grad = jnp.dot(mixed, middle_bf, preferred_element_type=jnp.float32)
    d_mixed = contract_cols(out_w, middle_bf).astype(jnp.bfloat16)
    outs = attend_backward(seq, heads, d_mixed, packs, own, totals, carried, call_id)
    d_packed = outs[0]
    passed = outs[1] if len(outs) > 1 else None
    qkv_grad = lax.dot_general(
        normed, d_packed, (((0,), (1,)), ((), ())), preferred_element_type=jnp.float32
    )
    d_normed = lax.dot_general(
        d_packed, qkv_w, (((0,), (1,)), ((), ())), preferred_element_type=jnp.float32
    )
    d_stream_norm, gain_a_grad = jax.vjp(layer_norm, stream, gains[0])[1](d_normed)
    grads = (qkv_grad, out_grad, up_grad, down_grad, gain_a_grad, gain_b_grad)
    return d_middle + d_stream_norm, grads, passed


def local(
    seq,
    dp,
    tokens,
    qkv_weight,
    out_weight,
    up_weight,
    down_weight,
    norm_gain,
    mlp_gain,
    pass_embed,
    cotangent,
):
    share = norm_gain.shape[0]
    small = jnp.zeros((8, 256), jnp.bfloat16)
    small = small.at[0, :share].set(norm_gain).at[1, :share].set(mlp_gain)
    small = small.at[0, 128 : 128 + share].set(pass_embed)
    qkv_w, small = gather_now(seq, dp, [qkv_weight, small])
    small = small.reshape(dp, 8, 256)
    gains = [small[:, row, :share].reshape(-1).astype(jnp.float32) for row in (0, 1)]
    embedding = small[:, 0, 128 : 128 + share].reshape(-1).astype(jnp.float32)
    heads = qkv_weight.shape[1] // (3 * HEAD_DIM * seq)
    sizes = (seq, dp, heads)
    first_out, first_kept, weights = block_forward(
        sizes,
        1,
        tokens[0].astype(jnp.float32),
        qkv_w,
        gains,
        [],
        None,
        [out_weight, up_weight, down_weight],
    )
    second_out, second_kept, weights = block_forward(
        sizes, 2, first_out + embedding, qkv_w, gains, [first_kept[2][0]], weights, []
    )
    d_second, second_grads, passed = block_backward(
        sizes, 3, cotangent[0].astype(jnp.float32), second_kept, qkv_w, gains, weights, None
    )
    embed_grad = jnp.sum(d_second, axis=0)
    d_first, first_grads, unused = block_backward(
        sizes, 4, d_second, first_kept, qkv_w, gains, weights, passed
    )
    summed = jax.tree.map(jnp.add, first_grads, second_grads) + (embed_grad,)
    shards = (
        lax.psum_scatter(
            summed[0].astype(jnp.bfloat16), "dp", scatter_dimension=0, tiled=True
        ).astype(jnp.float32),
        lax.psum_scatter(
            summed[1].astype(jnp.bfloat16), "dp", scatter_dimension=0, tiled=True
        ).astype(jnp.float32),
        lax.psum_scatter(
            summed[2].astype(jnp.bfloat16), "dp", scatter_dimension=0, tiled=True
        ).astype(jnp.float32),
        lax.psum_scatter(
            summed[3].astype(jnp.bfloat16), "dp", scatter_dimension=0, tiled=True
        ).astype(jnp.float32),
        lax.psum_scatter(
            summed[4].astype(jnp.bfloat16), "dp", scatter_dimension=0, tiled=True
        ).astype(jnp.float32),
        lax.psum_scatter(
            summed[5].astype(jnp.bfloat16), "dp", scatter_dimension=0, tiled=True
        ).astype(jnp.float32),
        lax.psum_scatter(
            summed[6].astype(jnp.bfloat16), "dp", scatter_dimension=0, tiled=True
        ).astype(jnp.float32),
    )
    final = (
        lax.psum(shards[0].astype(jnp.bfloat16), "seq").astype(jnp.float32),
        lax.psum(shards[1].astype(jnp.bfloat16), "seq").astype(jnp.float32),
        lax.psum(shards[2].astype(jnp.bfloat16), "seq").astype(jnp.float32),
        lax.psum(shards[3].astype(jnp.bfloat16), "seq").astype(jnp.float32),
        lax.psum(shards[4].astype(jnp.bfloat16), "seq").astype(jnp.float32),
        lax.psum(shards[5].astype(jnp.bfloat16), "seq").astype(jnp.float32),
        lax.psum(shards[6].astype(jnp.bfloat16), "seq").astype(jnp.float32),
    )
    return (
        second_out.astype(jnp.bfloat16)[None],
        d_first[None],
        final[0],
        final[1],
        final[2],
        final[3],
        final[4],
        final[5],
        final[6],
    )


def solution(mesh):
    in_specs = (
        P("dp", "seq", None),
        P("dp", None),
        P("dp", None),
        P("dp", None),
        P("dp", None),
        P("dp"),
        P("dp"),
        P("dp"),
        P("dp", "seq", None),
    )
    out_specs = (
        P("dp", "seq", None),
        P("dp", "seq", None),
        P("dp", None),
        P("dp", None),
        P("dp", None),
        P("dp", None),
        P("dp"),
        P("dp"),
        P("dp"),
    )
    return jax.shard_map(
        functools.partial(local, mesh.shape["seq"], mesh.shape["dp"]), mesh=mesh, in_specs=in_specs, out_specs=out_specs, check_vma=False)
```

time: 1610 us -> 721 us (0.45)
  matrix products: 640 us -> 98.2 us
  Pallas kernels: 0 us -> 260 us
  waiting for transfers between devices: 477 us -> 266 us
  other arithmetic: 233 us -> 22.7 us
  local copies, waits for them, and re-layouts: 89.5 us -> 19.7 us
  blocking collectives: 96.8 us -> 33.6 us
  loops' own time: 28.1 us -> 0 us
  starting transfers between devices: 24.8 us -> 1.07 us
    dot_general x60 -> x8, matrix products: 549 us -> 20.9 us  [the longest x2 7.45 us: block_backward(): lax.dot_general(d_packed, qkv_w, (((0,), (1,)), ((), ())), preferred_elem...]
    pallas_call x0 -> x5, Pallas kernels: none -> 260 us  [the longest x2 121 us: attend_forward(): pl.pallas_call(functools.partial(forward_kernel, seq, dp, sets, units, he...]
    all_to_all x6 -> x0, waiting for transfers between devices: 116 us -> none  [the longest x2 56.5 us: block_forward(): lax.all_to_all(packed, 'seq', split_axis=1, concat_axis=0, tiled=True)]
    convert_element_type x12 -> x1, other arithmetic: 112 us -> 0.69 us  [local(): small[:, row, :share].reshape(-1).astype(jnp.float32)]
    all_gather x4 -> x0, waiting for transfers between devices: 74.9 us -> none  [the longest x1 37.5 us: local(): lax.all_gather(down_weight, 'dp', axis=0, tiled=True)]
    reduce_sum x8 -> x0, other arithmetic: 74.4 us -> none  [one_block(): row_sum = jnp.sum(weights, axis=-1, keepdims=True)]
    all_to_all x2 -> x0, blocking collectives: 46.8 us -> none  [the longest x1 31.5 us: block_backward(): lax.all_to_all(d_packed, 'seq', split_axis=0, concat_axis=1, tiled=True)]
    reduce_scatter x1, waiting for transfers between devices: 70 us -> 29.1 us  [local(): lax.psum_scatter(summed[0].astype(jnp.bfloat16), 'dp', scatter_dimension=...]
  transfers between devices with their start and end apart: 15 -> 5, of which waited for: 12 -> 4; matrix products, arithmetic and copies ran while one was open for 11% -> 7% of each run, Pallas kernels for 0% -> 6%
where the time goes in v2:
time: 721 us; the launch traced here: 717 us
  waiting for transfers between devices  266 us (37%)
  Pallas kernels  260 us (36%)
  matrix products  98.2 us (14%)
  blocking collectives  33.6 us (5%)
  other arithmetic  22.7 us (3%)
  local copies, waits for them, and re-layouts  19.7 us (3%)
  between operations  15.8 us (2%)
    pallas_call x2, Pallas kernels, attend_forward(): pl.pallas_call(functools.partial(forward_kernel, seq, dp, sets, units, he...  121 us
    pallas_call x2, Pallas kernels, attend_backward(): pl.pallas_call(functools.partial(backward_kernel, seq, sets, bool(extra),...  105 us
    reduce_scatter x1, waiting for transfers between devices, local(): lax.psum_scatter(summed[3].astype(jnp.bfloat16), 'dp', scatter_dimension=...  98.7 us
    reduce_scatter x1, waiting for transfers between devices, local(): lax.psum_scatter(summed[2].astype(jnp.bfloat16), 'dp', scatter_dimension=...  98.5 us
    psum x1, waiting for transfers between devices, local(): lax.psum(shards[0].astype(jnp.bfloat16), 'seq').astype(jnp.float32)  40.1 us
    pallas_call x1, Pallas kernels, gather_now(): pl.pallas_call(functools.partial(gather_kernel, seq, dp, units), out_shap...  33.5 us
    reduce_scatter x1, waiting for transfers between devices, local(): lax.psum_scatter(summed[0].astype(jnp.bfloat16), 'dp', scatter_dimension=...  29.1 us
    unnamed x1, blocking collectives  27.9 us
  transfers between devices with their start and end apart: 5, of which 4 were waited for; matrix products, arithmetic and copies ran while one was open for 7% of the time, Pallas kernels for 6%

profile of v2, /device:TPU:0, one launch (start us, length us, event | category | flops | bytes accessed | tf_op | source)
XLA Modules:
  0.0 717.1 jit_solution(4842467905094606964)
XLA Ops:
  15.7 33.5 %gather_first.1 = (bf16[768,2304]{1,0:T(8,128)(2,1)S(1)}, bf16[64,256]{1,0:T(8,128)(2,1)S(1)}) custom-call(bf16[96,2304]{1,0:T(8,128)(2,1)S(1)} %copy-done.10, bf16[8,256]{1,0:T(8,128)(2,1)S(1)} %scatter.14.refs_1_), custom_call_target="tpu_custom_call" | custom-call | tf_op jit(solution)/shard_map/gather_first/pallas_call | solution.py:201
  56.2 81.4 %attend_forward_1.1 = (bf16[576,2048]{1,0:T(8,128)(2,1)S(1)}, bf16[768,512]{1,0:T(8,128)(2,1)S(1)}, bf16[192,2048]{1,0:T(8,128)(2,1)S(1)}, f32[3,1,2048]{2,1,0:T...) custom-call(bf16[2304,512]{1,0:T(8,128)(2,1)S(1)} %convolution_convert_fusion.1., ...), custom_call_target="tpu_custom_call" | custom-call | tf_op jit(solution)/shard_map/attend_forward_1/pallas_call | solution.py:350
  145.2 5.6 fusion.54
  150.9 8.5 %fusion.62 = (f32[512]{0:T(512)S(1)}, f32[512,768]{1,0:T(8,128)S(1)}) fusion(f32[768]{0:T(1024)S(1)} %copy-done.66, f32[512,768]{1,0:T(8,128)S(1)} %copy-done.28, bf16[3072,768]{1,0:T(8,128)(2,1)} %get-tuple-element.65, f32[512,3072]{1,0:T(8,128)S(1)} %fusion.54), kind=kOutput, calls=%fused_computation.123 | convolution fusion | flops 2431254016 | bytes 14160896 | tf_op jit(solution)/shard_map/dot_general | solution.py:550
  162.0 39.3 %attend_forward_2.1 = (bf16[576,2048]{1,0:T(8,128)(2,1)S(1)}, bf16[768,512]{1,0:T(8,128)(2,1)S(1)}, bf16[192,2048]{1,0:T(8,128)(2,1)S(1)}, f32[3,1,2048]{2,1,0:T(1,128)S(1)}) custom-call(bf16[2304,512]{1,0:T(8,128)(2,1)S(1)} %convolution_convert_fusion.refs_0_, bf16[576,2048]{1,0:T(8,128)(2,1)S(1)} %get-tuple-element.66.refs_1_), custom_call_target="tpu_custom_call" | custom-call | tf_op jit(solution)/shard_map/attend_forward_2/pallas_call | solution.py:350
  205.9 6.6 fusion.13
  212.5 3.4 multiply_reduce_fusion
  218.7 61.7 %attend_backward_2.1 = (bf16[2304,512]{1,0:T(8,128)(2,1)S(1)}, f32[3,128,2048]{2,1,0:T(8,128)}) custom-call(bf16[768,512]{1,0:T(8,128)(2,1)S(1)} %convolution_convert_fusion.3.refs_0_, bf16[576,2048]{1,0:T(8,128)(2,1)} %copy-done, bf16[576,2048]{1,0:T(8,128)(2,1)} %copy-done.1, bf16[192,2048]{1,0:T(8,128)(2,1)S(1)} %get-tuple-element.69.refs_3_, ...), custom_call_target="tpu_custom_call" | custom-call | tf_op jit(solution)/shard_map/attend_backward_2/pallas_call | solution.py:508
  285.9 9.3 %fusion.6 = bf16[512,3072]{1,0:T(8,128)(2,1)S(1)} fusion(f32[512,3072]{1,0:T(8,128)} %copy-done.69, bf16[3072,768]{1,0:T(8,128)(2,1)} %get-tuple-element.65, f32[512,768]{1,0:T(8,128)S(1)} %get-tuple-element.97), kind=kOutput, calls=%fused_computation.13 | convolution fusion | flops 2447769600 | bytes 15728640 | tf_op jit(solution)/shard_map/dot_general | solution.py:33
  295.2 3.4 multiply_reduce_fusion.1
  306.2 43.6 %attend_backward_1.1 = bf16[2304,512]{1,0:T(8,128)(2,1)S(1)} custom-call(bf16[768,512]{1,0:T(8,128)(2,1)S(1)} %convolution_convert_fusion.2.refs_0_, bf16[576,2048]{1,0:T(8,128)(2,1)} %copy-done, bf16[192,2048]{1,0:T(8,128)(2,1)S(1)} %copy-done.7, f32[3,1,2048]{2,1,0:T(1,128)S(1)} %copy-done.13, f32[3,128,2048]{2,1,0:T(8,128)} %get-tuple-element.74.refs_4_), custom_call_target="tpu_custom_call" | custom-call | tf_op jit(solution)/shard_map/attend_backward_1/pallas_call | solution.py:508
  352.2 4.1 add_convert_fusion.2
  357.7 5.5 fusion.36
  363.2 8.8 %add_convert_fusion = bf16[3072,768]{1,0:T(8,128)(2,1)} fusion(f32[3072,768]{1,0:T(8,128)S(1)} %fusion.36, bf16[1,512,768]{2,1,0:T(8,128)(2,1)S(1)} %copy-done.39, f32[512,3072]{1,0:T(8,128)} %copy-done.68), kind=kOutput, calls=%fused_computation | convolution fusion | flops 2434793472 | bytes 21233664 | tf_op jit(solution)/shard_map/dot_general | solution.py:27
  373.5 4.8 fusion.53
  378.4 4.7 add_convert_fusion.1
  385.0 4.5 fusion.28
  391.5 27.9 %all-reduce.4 = (bf16[768]{0:T(1024)(128)(2,1)S(1)}, bf16[768]{0:T(1024)(128)(2,1)S(1)}, bf16[768]{0:T(1024)(128)(2,1)S(1)}) all-reduce(bf16[768]{0:T(1024)(128)(2,1)S(1)} %get-tuple-element.118, bf16[768]{0:T(1024)(128)(2,1)S(1)} %get-tuple-element.117, bf16[768]{0:T(1024)(128)(2,1)S(1)} %copy-done.60), channel_id=6, replica_groups=mesh['seq'=4,'dp'=8] {'dp'}, use_global_device_ids=true, to_apply=%region_27.0.clone | all-reduce | flops 2304 | bytes 9216
  419.7 5.6 all-reduce.5
  430.0 29.1 %reduce-scatter.5.cloned.1.call-done = bf16[96,2304]{1,0:T(8,128)(2,1)} async-done(((bf16[768,2304]{1,0:T(8,128)(2,1)}), bf16[96,2304]{1,0:T(8,128)(2,1)}) %reduce-scatter.5.cloned.1.call-update) | async-done | bytes 442384 | tf_op jit(solution)/shard_map/reduce_scatter | solution.py:629
  459.1 98.7 %reduce-scatter.11.cloned.1.call-done = bf16[384,768]{1,0:T(8,128)(2,1)} async-done(((bf16[3072,768]{1,0:T(8,128)(2,1)}), bf16[384,768]{1,0:T(8,128)(2,1)}) %reduce-scatter.11.cloned.1.call-update) | async-done | bytes 589840 | tf_op jit(solution)/shard_map/reduce_scatter | solution.py:638
  557.8 98.5 %reduce-scatter.9.cloned.1.call-done = bf16[96,3072]{1,0:T(8,128)(2,1)} async-done(((bf16[768,3072]{1,0:T(8,128)(2,1)}), bf16[96,3072]{1,0:T(8,128)(2,1)}) %reduce-scatter.9.cloned.1.call-update) | async-done | bytes 589840 | tf_op jit(solution)/shard_map/reduce_scatter | solution.py:635
  656.4 8.8 %fusion.29 = bf16[1,512,768]{2,1,0:T(8,128)(2,1)} fusion(f32[512,768]{1,0:T(8,128)S(1)} %copy-done.22, bf16[3072,768]{1,0:T(8,128)(2,1)} %get-tuple-element.65, f32[512,3072]{1,0:T(8,128)} %copy-done.68), kind=kOutput, calls=%fused_computation.70 | convolution fusion | flops 2430861312 | bytes 13369344 | tf_op jit(solution)/shard_map/dot_general | solution.py:550
  665.1 40.1 %all-reduce.9.cloned.1.call-done = (bf16[96,2304]{1,0:T(8,128)(2,1)}, bf16[96,768]{1,0:T(8,128)(2,1)}, bf16[96,3072]{1,0:T(8,128)(2,1)}, bf16[384,768]{1,0:T(8,128)(2,1)}) async-done(((bf16[96,2304]{1,0:T(8,128)(2,1)}, bf16[96,768]{1,0:T(8,128)(2,1)}, bf16[96,3072]{1,0:T(8,128)(2,1)}, bf16[384,768]{1,0:T(8,128)(2,1)}), (bf16[96,2304]{1,0:T(8,128)(2,1)}, bf16[96,768]{1,0:T(8,128)(2,1)}, ...) | async-done | bytes 1769488 | tf_op jit(solution)/shard_map/psum | solution.py:652
  (228 shorter events, 63.8 us)
Async XLA Ops:
  7.2 422.8 %reduce-scatter.7.cloned.1.call-start = ((), (), s32[]{:S(2)}) async-start(), calls=%async_computation.5 | async-start | bytes 1327104 | tf_op jit(solution)/shard_map/reduce_scatter | solution.py:632
  139.8 22.2 %copy-start = (bf16[576,2048]{1,0:T(8,128)(2,1)}, bf16[576,2048]{1,0:T(8,128)(2,1)S(1)}, u32[]{:S(2)}) copy-start(bf16[576,2048]{1,0:T(8,128)(2,1)S(1)} %get-tuple-element.66.refs_1_) | copy-start | bytes 7077892
  150.9 8.5 %copy-start.69 = (f32[512,3072]{1,0:T(8,128)}, f32[512,3072]{1,0:T(8,128)S(1)}, u32[]{:S(2)}) copy-start(f32[512,3072]{1,0:T(8,128)S(1)} %fusion.54) | copy-start | bytes 18874372
  150.9 8.8 %copy-start.16 = (bf16[768,2304]{1,0:T(8,128)(2,1)S(1)}, bf16[768,2304]{1,0:T(8,128)(2,1)}, u32[]{:S(2)}) copy-start(bf16[768,2304]{1,0:T(8,128)(2,1)} %copy-done.15) | copy-start | bytes 10616836
  159.4 123.9 %copy-start.18 = (f32[512,768]{1,0:T(8,128)}, f32[512,768]{1,0:T(8,128)S(1)}, u32[]{:S(2)}) copy-start(f32[512,768]{1,0:T(8,128)S(1)} %get-tuple-element.109) | copy-start | bytes 4718596
  159.4 123.9 %copy-start.47 = (f32[512]{0:T(512)}, f32[512]{0:T(512)S(1)}, u32[]{:S(2)}) copy-start(f32[512]{0:T(512)S(1)} %broadcast_multiply_fusion.1) | copy-start | bytes 6148
  159.4 43.7 %slice-start = ((s8[4718592]{0:T(1024)(128)(4,1)}), s8[4194304]{0:T(1024)(128)(4,1)S(1)}, s32[]{:S(2)}) async-start(s8[4718592]{0:T(1024)(128)(4,1)} %bitcast.98), calls=%async_computation.9 | async-start | bytes 8388608
  159.7 123.6 %copy-start.54 = (f32[512]{0:T(512)}, f32[512]{0:T(512)S(1)}, u32[]{:S(2)}) copy-start(f32[512]{0:T(512)S(1)} %fusion.47) | copy-start | bytes 6148
  159.7 43.4 %slice-start.1 = ((s8[4718592]{0:T(1024)(128)(4,1)}), s8[524288]{0:T(1024)(128)(4,1)S(1)}, s32[]{:S(2)}) async-start(s8[4718592]{0:T(1024)(128)(4,1)} %bitcast.98), calls=%async_computation.10 | async-start | bytes 1048576
  202.8 13.2 %copy-start.20 = (f32[512,768]{1,0:T(8,128)}, f32[512,768]{1,0:T(8,128)S(1)}, u32[]{:S(2)}) copy-start(f32[512,768]{1,0:T(8,128)S(1)} %get-tuple-element.111) | copy-start | bytes 4718596
  202.8 13.2 %copy-start.52 = (f32[512]{0:T(512)}, f32[512]{0:T(512)S(1)}, u32[]{:S(2)}) copy-start(f32[512]{0:T(512)S(1)} %broadcast_multiply_fusion) | copy-start | bytes 6148
  203.1 12.8 %copy-start.61 = (f32[512]{0:T(512)}, f32[512]{0:T(512)S(1)}, u32[]{:S(2)}) copy-start(f32[512]{0:T(512)S(1)} %fusion.48) | copy-start | bytes 6148
  218.6 61.7 %copy-start.17 = (bf16[768,2304]{1,0:T(8,128)(2,1)S(1)}, bf16[768,2304]{1,0:T(8,128)(2,1)}, u32[]{:S(2)}) copy-start(bf16[768,2304]{1,0:T(8,128)(2,1)} %copy-done.15) | copy-start | bytes 10616836
  285.9 13.3 %copy-start.35 = (f32[512,768]{1,0:T(8,128)}, f32[512,768]{1,0:T(8,128)S(1)}, u32[]{:S(2)}) copy-start(f32[512,768]{1,0:T(8,128)S(1)} %get-tuple-element.97) | copy-start | bytes 4718596
  285.9 9.3 %copy-start.29 = (f32[512,768]{1,0:T(8,128)S(1)}, f32[512,768]{1,0:T(8,128)}, u32[]{:S(2)}) copy-start(f32[512,768]{1,0:T(8,128)} %copy-done.27) | copy-start | bytes 4718596
  303.3 155.8 %reduce-scatter.5.cloned.1.call-start = ((), (), s32[]{:S(2)}) async-start(), calls=%async_computation.4 | async-start | bytes 3981312 | tf_op jit(solution)/shard_map/reduce_scatter | solution.py:629
  306.1 43.6 %copy-start.32 = (bf16[1,512,768]{2,1,0:T(8,128)(2,1)S(1)}, bf16[1,512,768]{2,1,0:T(8,128)(2,1)}, u32[]{:S(2)}) copy-start(bf16[1,512,768]{2,1,0:T(8,128)(2,1)} %param.15) | copy-start | bytes 2359300
  306.1 43.6 %copy-start.45 = (f32[512]{0:T(512)S(1)}, f32[512]{0:T(512)}, u32[]{:S(2)}) copy-start(f32[512]{0:T(512)} %copy-done.44) | copy-start | bytes 6148
  306.2 43.6 %copy-start.50 = (f32[512]{0:T(512)S(1)}, f32[512]{0:T(512)}, u32[]{:S(2)}) copy-start(f32[512]{0:T(512)} %copy-done.49) | copy-start | bytes 6148
  356.3 201.5 %reduce-scatter.11.cloned.1.call-start = ((), (), s32[]{:S(2)}) async-start(), calls=%async_computation.7 | async-start | bytes 5308416 | tf_op jit(solution)/shard_map/reduce_scatter | solution.py:638
  372.1 284.2 %reduce-scatter.9.cloned.1.call-start = ((), (), s32[]{:S(2)}) async-start(), calls=%async_computation.6 | async-start | bytes 5308416 | tf_op jit(solution)/shard_map/reduce_scatter | solution.py:635
  383.1 322.1 %all-reduce.9.cloned.1.call-start = ((), (), s32[]{:S(2)}) async-start(), calls=%async_computation.8 | async-start | bytes 3538944 | tf_op jit(solution)/shard_map/psum | solution.py:652
  389.6 37.3 %copy-start.24 = (f32[512,768]{1,0:T(8,128)S(1)}, f32[512,768]{1,0:T(8,128)}, u32[]{:S(2)}) copy-start(f32[512,768]{1,0:T(8,128)} %copy-done.23) | copy-start | bytes 4718596
  430.0 226.4 %copy-start.22 = (f32[512,768]{1,0:T(8,128)S(1)}, f32[512,768]{1,0:T(8,128)}, u32[]{:S(2)}) copy-start(f32[512,768]{1,0:T(8,128)} %copy-done.20) | copy-start | bytes 4718596
  (57 other events, 154.4 us)
Sparse Core Ops, SparseCore 0:
  303.5 73.1 reduce-scatter.6
  380.3 78.7 reduce-scatter.4
  462.8 94.9 reduce-scatter.10
  561.3 95.0 reduce-scatter.8
  658.8 46.3 all-reduce.8

commit v3 on v2

--- a/solution.py
+++ b/solution.py
@@ -8,6 +8,7 @@
 from jax.sharding import PartitionSpec as P
 
 HEAD_DIM = 64
+BACKGROUND = 3
 
 
 epsilon = 1e-05
@@ -209,6 +210,157 @@
         ),
         name="gather_first",
     )(*shards)
+
+
+class Scatter:
+    SEMS = 11
+
+    def __init__(self, seq, dp, grads, outs, scratch):
+        self.seq, self.dp, self.line, self.chips = seq, dp, dp // 2, seq // 2
+        self.grads, self.outs = grads, outs
+        me = lax.axis_index("seq")
+        self.core, self.chip = lax.rem(me, 2), lax.div(me, 2)
+        self.core_peer = {"seq": me + 1 - 2 * self.core}
+        self.rank = lax.axis_index("dp")
+        self.a, self.b = lax.div(self.rank, 2), lax.rem(self.rank, 2)
+        self.y_peer = {"dp": self.a * 2 + 1 - self.b}
+        self.buffers = [scratch[7 * u : 7 * u + 7] for u in range(len(grads))]
+        self.sems = scratch[7 * len(grads) :]
+        self.flying, self.sent = {}, []
+
+    @staticmethod
+    def scratch(seq, dp, grads):
+        shapes = []
+        line, chips = dp // 2, seq // 2
+        for grad in grads:
+            rows, half = grad.shape[1], grad.shape[2] // 2
+            for lead in ((dp,), (dp,), (line,), (line,), (), (chips,)):
+                shapes.append(pltpu.VMEM(lead + (rows, half), jnp.bfloat16))
+            shapes.append(pltpu.VMEM((rows, 2 * half), jnp.float32))
+        units, dma = len(grads), pltpu.SemaphoreType.DMA
+        sizes = (1, 1, 1, line, line, line, line, chips, chips, 1, 1)
+        return shapes + [dma((units, size)) for size in sizes]
+
+    def peers(self):
+        z = [{"dp": self.other(d) * 2 + self.b} for d in range(1, self.line)]
+        return z + [self.y_peer]
+
+    def x_peers(self):
+        return [
+            {"seq": lax.rem(self.chip + d, self.chips) * 2 + self.core}
+            for d in range(1, self.chips)
+        ]
+
+    def other(self, offset):
+        return lax.rem(self.a + offset, self.line)
+
+    def half(self, unit, core):
+        half = self.grads[unit].shape[2] // 2
+        return pl.ds(pl.multiple_of(core * half, 128), half)
+
+    def send(self, key, src, dst, sems, slot, device):
+        unit = key[1]
+        copy = remote(
+            src, dst, self.sems[sems].at[unit, slot], self.sems[sems + 1].at[unit, slot], device
+        )
+        copy.start()
+        self.flying[key] = copy
+        self.sent.append(copy)
+
+    def start(self, unit):
+        total, core_in = self.buffers[unit][:2]
+        grad = self.grads[unit]
+        self.send(
+            ("core", unit), grad.at[:, :, self.half(unit, 1 - self.core)], core_in, 0, 0, self.core_peer
+        )
+        copy = pltpu.make_async_copy(
+            grad.at[:, :, self.half(unit, self.core)], total, self.sems[2].at[unit, 0]
+        )
+        copy.start()
+        self.flying["own", unit] = copy
+
+    def chip_sum(self, unit):
+        total, core_in, y_in = self.buffers[unit][:3]
+        self.flying["core", unit].wait_recv()
+        self.flying["own", unit].wait()
+        for place in range(self.line):
+            row = place * 2 + 1 - self.b
+            total[row] = add(total[row], core_in[row]).astype(jnp.bfloat16)
+            self.send(("y", unit, place), total.at[row], y_in.at[place], 3, place, self.y_peer)
+
+    def y_sum(self, unit):
+        total, core_in, y_in, z_in = self.buffers[unit][:4]
+        for d in range(1, self.line):
+            place = self.other(d)
+            row = place * 2 + self.b
+            if d == 1:
+                for slot in range(self.line):
+                    self.flying["y", unit, slot].wait_recv()
+            total[row] = add(total[row], core_in[row], y_in[place]).astype(jnp.bfloat16)
+            self.send(("z", unit, d), total.at[row], z_in.at[d], 5, d, {"dp": row})
+
+    def z_sum(self, unit):
+        total, core_in, y_in, z_in, x_out, x_in = self.buffers[unit][:6]
+        for d in range(1, self.line):
+            self.flying["z", unit, d].wait_recv()
+        terms = [total[self.rank], core_in[self.rank], y_in[self.a]]
+        terms += [z_in[d] for d in range(1, self.line)]
+        x_out[...] = add(*terms).astype(jnp.bfloat16)
+        for d, peer in enumerate(self.x_peers()):
+            self.send(("x", unit, d), x_out, x_in.at[d], 7, d, peer)
+
+    def x_sum(self, unit):
+        x_out, x_in, final = self.buffers[unit][4:]
+        for d in range(self.chips - 1):
+            self.flying["x", unit, d].wait_recv()
+        mine = self.half(unit, self.core)
+        final[:, mine] = add(x_out[...], *[x_in[d] for d in range(self.chips - 1)])
+        self.send(("f", unit), final.at[:, mine], final.at[:, mine], 9, 0, self.core_peer)
+
+    def finish(self, unit):
+        self.flying["f", unit].wait_recv()
+        self.outs[unit][...] = self.buffers[unit][6][...]
+
+    def drain(self):
+        for copy in self.sent:
+            copy.wait_send()
+
+
+def add(*terms):
+    total = terms[0].astype(jnp.float32)
+    for term in terms[1:]:
+        total = total + term.astype(jnp.float32)
+    return total
+
+
+def scatter_kernel(seq, dp, units, *refs):
+    grads, outs, scratch = refs[:units], refs[units : 2 * units], refs[2 * units :]
+    work = Scatter(seq, dp, grads, outs, scratch)
+    greet(work.peers() + work.x_peers() + [work.core_peer])
+    stages = (work.start, work.chip_sum, work.y_sum, work.z_sum, work.x_sum, work.finish)
+    for stage in stages:
+        for unit in range(units):
+            stage(unit)
+    work.drain()
+
+
+def owned_shape(grad):
+    return jax.ShapeDtypeStruct(grad.shape[1:], jnp.float32)
+
+
+def scatter_now(seq, dp, grads, call_id):
+    units = len(grads)
+    return pl.pallas_call(
+        functools.partial(scatter_kernel, seq, dp, units),
+        out_shape=tuple(owned_shape(grad) for grad in grads),
+        in_specs=[pl.BlockSpec(memory_space=pl.ANY)] * units,
+        out_specs=(pl.BlockSpec(memory_space=pltpu.VMEM),) * units,
+        scratch_shapes=Scatter.scratch(seq, dp, grads),
+        compiler_params=pltpu.CompilerParams(
+            collective_id=call_id, has_side_effects=True, vmem_limit_bytes=48 << 20
+        ),
+        name="scatter_last",
+    )(*grads)
 
 
 def causal_mask(size):
@@ -378,7 +530,7 @@
     return outs[:4], outs[4:]
 
 
-def backward_kernel(seq, sets, carried, heads, *refs):
+def backward_kernel(seq, dp, sets, carried, units, heads, *refs):
     refs = list(refs)
 
     def take(count):
@@ -390,17 +542,20 @@
     packs = take(sets)
     own_in, totals_in = take(2)
     carry_in = take(1)[0] if carried else None
+    grads_in = take(units)
     (d_packed_out,) = take(1)
     carry_out = take(1)[0] if sets == 2 else None
+    grads_out = take(units)
     arrived, local_grad, d_packed_in, q_s, k_s, kt_s, v_s, delta_s, dq_s, dkv_s = take(10)
-    in_send, in_recv, out_send, out_recv = refs
+    in_send, in_recv, out_send, out_recv = take(4)
+    work = Scatter(seq, dp, grads_in, grads_out, refs) if units else None
 
     tokens = d_mixed.shape[1]
     length = tokens * seq
     group = 3 * HEAD_DIM
     me = lax.axis_index("seq")
     peers = seq_peers(seq)
-    greet([{"seq": peer} for peer in peers])
+    greet([{"seq": peer} for peer in peers] + (work.peers() if units else []))
     own_lanes = pl.ds(pl.multiple_of(me * tokens, tokens), tokens)
     scale = jnp.bfloat16(HEAD_DIM**-0.5)
 
@@ -416,6 +571,11 @@
             )
             copy.start()
             copies[h, d] = copy
+    stages = []
+    if units:
+        for unit in range(units):
+            work.start(unit)
+        stages = background_order(work, units)
     for h in range(heads):
         arrived[h * HEAD_DIM : (h + 1) * HEAD_DIM, own_lanes] = d_mixed[
             pl.ds(pl.multiple_of((me * heads + h) * HEAD_DIM, HEAD_DIM), HEAD_DIM), :
@@ -471,6 +631,8 @@
             local_grad[c0 + HEAD_DIM : c0 + group, keys] = dkv_s[sets - 1, :, keys].astype(
                 jnp.bfloat16
             )
+            if stages:
+                stages.pop(0)()
         if sets == 2:
             carry_out[h] = dkv_s[0]
         mine = pl.ds(pl.multiple_of((me * heads + h) * group, group), group)
@@ -487,6 +649,10 @@
             copy.start()
             results.append(copy)
         d_packed_in[mine] = local_grad[c0 : c0 + group, own_lanes]
+    for stage in stages:
+        stage()
+    if units:
+        work.drain()
     for copy in copies.values():
         copy.wait_send()
     for copy in results:
@@ -494,7 +660,16 @@
     d_packed_out[...] = d_packed_in[...]
 
 
-def attend_backward(seq, heads, d_mixed, packs, own, totals, carried, call_id):
+def background_order(work, units):
+    order = []
+    for step in range(units + 4):
+        for stage, call in enumerate((work.chip_sum, work.y_sum, work.z_sum, work.x_sum, work.finish)):
+            if 0 <= step - stage < units:
+                order.append(functools.partial(call, step - stage))
+    return order
+
+
+def attend_backward(seq, dp, heads, d_mixed, packs, own, totals, carried, grads, call_id):
     width, tokens = d_mixed.shape
     length = tokens * seq
     sets = len(packs)
@@ -505,10 +680,13 @@
     out_shape = [jax.ShapeDtypeStruct((3 * width, tokens), jnp.bfloat16)]
     if sets == 2:
         out_shape.append(jax.ShapeDtypeStruct((heads, 2 * HEAD_DIM, length), jnp.float32))
+    units = len(grads)
+    out_shape += [owned_shape(grad) for grad in grads]
+    hbm = pl.BlockSpec(memory_space=pl.ANY)
     return pl.pallas_call(
-        functools.partial(backward_kernel, seq, sets, bool(extra), heads),
+        functools.partial(backward_kernel, seq, dp, sets, bool(extra), units, heads),
         out_shape=tuple(out_shape),
-        in_specs=[vmem] * (3 + sets + len(extra)),
+        in_specs=[vmem] * (3 + sets + len(extra)) + [hbm] * units,
         out_specs=(vmem,) * len(out_shape),
         scratch_shapes=[
             pltpu.VMEM((heads * HEAD_DIM, length), jnp.bfloat16),
@@ -525,12 +703,13 @@
             dma((heads, seq)),
             dma((heads, seq)),
             dma((heads, seq)),
-        ],
+        ]
+        + (Scatter.scratch(seq, dp, grads) if units else []),
         compiler_params=pltpu.CompilerParams(
-            collective_id=call_id, has_side_effects=True, vmem_limit_bytes=48 << 20
+            collective_id=call_id, has_side_effects=True, vmem_limit_bytes=58 << 20
         ),
         name=f"attend_backward_{sets}",
-    )(d_mixed, *packs, own, totals, *extra)
+    )(d_mixed, *packs, own, totals, *extra, *grads)
 
 
 def block_forward(sizes, call_id, stream, qkv_w, gains, earlier, weights, shards):
@@ -552,7 +731,12 @@
     return result, stored, (out_w, up_w, down_w)
 
 
-def block_backward(sizes, call_id, upstream, stored, qkv_w, gains, weights, carried):
+def split_rows(dp, first, second):
+    total = (first + second).astype(jnp.bfloat16)
+    return total.reshape(dp, total.shape[0] // dp, total.shape[1])
+
+
+def block_backward(sizes, call_id, upstream, stored, qkv_w, gains, weights, carried, later):
     seq, dp, heads = sizes
     out_w, up_w, down_w = weights
     stream, normed, packs, own, totals, mixed, middle, normed_b, hidden, active = stored
@@ -567,9 +751,17 @@
     middle_bf = d_middle.astype(jnp.bfloat16)
     out_grad = jnp.dot(mixed, middle_bf, preferred_element_type=jnp.float32)
     d_mixed = contract_cols(out_w, middle_bf).astype(jnp.bfloat16)
-    outs = attend_backward(seq, heads, d_mixed, packs, own, totals, carried, call_id)
+    background = []
+    if later is not None:
+        background = [
+            split_rows(dp, one, two)
+            for one, two in zip((out_grad, up_grad, down_grad)[:BACKGROUND], later[1 : 1 + BACKGROUND])
+        ]
+    outs = attend_backward(
+        seq, dp, heads, d_mixed, packs, own, totals, carried, background, call_id
+    )
     d_packed = outs[0]
-    passed = outs[1] if len(outs) > 1 else None
+    passed = outs[1] if later is None else outs[1:]
     qkv_grad = lax.dot_general(
         normed, d_packed, (((0,), (1,)), ((), ())), preferred_element_type=jnp.float32
     )
@@ -618,55 +810,35 @@
         sizes, 2, first_out + embedding, qkv_w, gains, [first_kept[2][0]], weights, []
     )
     d_second, second_grads, passed = block_backward(
-        sizes, 3, cotangent[0].astype(jnp.float32), second_kept, qkv_w, gains, weights, None
+        sizes, 3, cotangent[0].astype(jnp.float32), second_kept, qkv_w, gains, weights, None, None
     )
     embed_grad = jnp.sum(d_second, axis=0)
-    d_first, first_grads, unused = block_backward(
-        sizes, 4, d_second, first_kept, qkv_w, gains, weights, passed
-    )
-    summed = jax.tree.map(jnp.add, first_grads, second_grads) + (embed_grad,)
-    shards = (
-        lax.psum_scatter(
-            summed[0].astype(jnp.bfloat16), "dp", scatter_dimension=0, tiled=True
-        ).astype(jnp.float32),
-        lax.psum_scatter(
-            summed[1].astype(jnp.bfloat16), "dp", scatter_dimension=0, tiled=True
-        ).astype(jnp.float32),
-        lax.psum_scatter(
-            summed[2].astype(jnp.bfloat16), "dp", scatter_dimension=0, tiled=True
-        ).astype(jnp.float32),
-        lax.psum_scatter(
-            summed[3].astype(jnp.bfloat16), "dp", scatter_dimension=0, tiled=True
-        ).astype(jnp.float32),
-        lax.psum_scatter(
-            summed[4].astype(jnp.bfloat16), "dp", scatter_dimension=0, tiled=True
-        ).astype(jnp.float32),
-        lax.psum_scatter(
-            summed[5].astype(jnp.bfloat16), "dp", scatter_dimension=0, tiled=True
-        ).astype(jnp.float32),
-        lax.psum_scatter(
-            summed[6].astype(jnp.bfloat16), "dp", scatter_dimension=0, tiled=True
-        ).astype(jnp.float32),
-    )
-    final = (
-        lax.psum(shards[0].astype(jnp.bfloat16), "seq").astype(jnp.float32),
-        lax.psum(shards[1].astype(jnp.bfloat16), "seq").astype(jnp.float32),
-        lax.psum(shards[2].astype(jnp.bfloat16), "seq").astype(jnp.float32),
-        lax.psum(shards[3].astype(jnp.bfloat16), "seq").astype(jnp.float32),
-        lax.psum(shards[4].astype(jnp.bfloat16), "seq").astype(jnp.float32),
-        lax.psum(shards[5].astype(jnp.bfloat16), "seq").astype(jnp.float32),
-        lax.psum(shards[6].astype(jnp.bfloat16), "seq").astype(jnp.float32),
-    )
+    d_first, first_grads, done = block_backward(
+        sizes, 4, d_second, first_kept, qkv_w, gains, weights, passed, second_grads
+    )
+    vectors = [first_grads[4] + second_grads[4], first_grads[5] + second_grads[5], embed_grad]
+    gain_a, gain_b, embed = [
+        jnp.pad(v.astype(jnp.bfloat16).reshape(dp, 1, share), ((0, 0), (0, 0), (0, 128 - share)))
+        for v in vectors
+    ]
+    top = jnp.concatenate([gain_a, embed], axis=2)
+    low = jnp.concatenate([gain_b, jnp.zeros_like(embed)], axis=2)
+    small = jnp.concatenate([top, low, jnp.zeros((dp, 6, 256), jnp.bfloat16)], axis=1)
+    last = [
+        split_rows(dp, one, two)
+        for one, two in list(zip(first_grads, second_grads))[1 + BACKGROUND : 4] + [(first_grads[0], second_grads[0])]
+    ]
+    rest = scatter_now(seq, dp, [small] + last, 5)
+    small, qkv = rest[0], rest[-1]
+    others = list(done) + list(rest[1:-1])
     return (
         second_out.astype(jnp.bfloat16)[None],
         d_first[None],
-        final[0],
-        final[1],
-        final[2],
-        final[3],
-        final[4],
-        final[5],
-        final[6],
+        qkv,
+        *others,
+        small[0, :share],
+        small[1, :share],
+        small[0, 128 : 128 + share],
     )
 
 

time: 721 us -> 533 us (0.74)
  waiting for transfers between devices: 266 us -> 0 us
  Pallas kernels: 260 us -> 393 us
  blocking collectives: 33.6 us -> 0 us
  between operations: 15.8 us -> 1.62 us
    reduce_scatter x4 -> x0, waiting for transfers between devices: 226 us -> none  [the longest x1 98.7 us: local(): lax.psum_scatter(summed[3].astype(jnp.bfloat16), 'dp', scatter_dimension=...]
    pallas_call x2 -> x3, Pallas kernels: 105 us -> 239 us  [the longest x2 185 us: attend_backward(): pl.pallas_call(functools.partial(backward_kernel, seq, dp, sets, bool(ext...]
    psum x1 -> x0, waiting for transfers between devices: 40.1 us -> none  [local(): lax.psum(shards[0].astype(jnp.bfloat16), 'seq').astype(jnp.float32)]
    unnamed x1 -> x0, blocking collectives: 27.9 us -> none
    dot_general x2, matrix products: 17.2 us -> 8.53 us  [block_forward(): jnp.dot(active, down_w, preferred_element_type=jnp.float32)]
    dot_general x6, matrix products: 26.1 us -> 34.5 us  [contract_rows(): lax.dot_general(left_side, right_side, (((0,), (0,)), ((), ())), preferre...]
  transfers between devices with their start and end apart: 5 -> 0, of which waited for: 4 -> 0; matrix products, arithmetic and copies ran while one was open for 7% -> 0% of each run, Pallas kernels for 6% -> 0%
where the time goes in v3:
time: 533 us; the launch traced here: 525 us
  Pallas kernels  393 us (74%)
  matrix products  99.6 us (19%)
  other arithmetic  16.4 us (3%)
  local copies, waits for them, and re-layouts  14.2 us (3%)
    pallas_call x2, Pallas kernels, attend_backward(): pl.pallas_call(functools.partial(backward_kernel, seq, dp, sets, bool(ext...  185 us
    pallas_call x2, Pallas kernels, attend_forward(): pl.pallas_call(functools.partial(forward_kernel, seq, dp, sets, units, he...  120 us
    pallas_call x1, Pallas kernels, scatter_now(): pl.pallas_call(functools.partial(scatter_kernel, seq, dp, units), out_sha...  54.6 us
    dot_general x6, matrix products, contract_rows(): lax.dot_general(left_side, right_side, (((0,), (0,)), ((), ())), preferre...  34.5 us
    pallas_call x1, Pallas kernels, gather_now(): pl.pallas_call(functools.partial(gather_kernel, seq, dp, units), out_shap...  33.5 us
    dot_general x6, matrix products, contract_cols(): lax.dot_general(left_side, right_side, (((1,), (1,)), ((), ())), preferre...  25.8 us

profile of v3, /device:TPU:0, one launch (start us, length us, event | category | flops | bytes accessed | tf_op | source)
XLA Modules:
  0.0 524.8 jit_solution(15743853813612375196)
XLA Ops:
  4.0 2.7 broadcast_select_fusion
  9.1 33.5 %gather_first.1 = (bf16[768,2304]{1,0:T(8,128)(2,1)S(1)}, bf16[64,256]{1,0:T(8,128)(2,1)S(1)}) custom-call(bf16[96,2304]{1,0:T(8,128)(2,1)S(1)} %copy-done.8, bf16[8,256]{1,0:T(8,128)(2,1)S(1)} %scatter.14.refs_1_), custom_call_target="tpu_custom_call" | custom-call | tf_op jit(solution)/shard_map/gather_first/pallas_call | solution.py:202
  49.1 78.9 %attend_forward_1.1 = (bf16[576,2048]{1,0:T(8,128)(2,1)S(1)}, bf16[768,512]{1,0:T(8,128)(2,1)S(1)}, bf16[192,2048]{1,0:T(8,128)(2,1)S(1)}, f32[3,1,2048]{2,1,0:T...) custom-call(bf16[2304,512]{1,0:T(8,128)(2,1)S(1)} %convolution_convert_fusion.1., ...), custom_call_target="tpu_custom_call" | custom-call | tf_op jit(solution)/shard_map/attend_forward_1/pallas_call | solution.py:502
  130.2 3.1 fusion.72
  136.1 4.7 fusion.65
  140.8 3.8 fusion.73
  147.3 41.2 %attend_forward_2.1 = (bf16[576,2048]{1,0:T(8,128)(2,1)S(1)}, bf16[768,512]{1,0:T(8,128)(2,1)S(1)}, bf16[192,2048]{1,0:T(8,128)(2,1)S(1)}, f32[3,1,2048]{2,1,0:T(1,128)S(1)}) custom-call(bf16[2304,512]{1,0:T(8,128)(2,1)S(1)} %convolution_convert_fusion.refs_0_, bf16[576,2048]{1,0:T(8,128)(2,1)S(1)} %get-tuple-element.72.refs_1_), custom_call_target="tpu_custom_call" | custom-call | tf_op jit(solution)/shard_map/attend_forward_2/pallas_call | solution.py:502
  190.5 2.7 fusion.66
  193.3 4.7 fusion.29
  198.0 6.5 %fusion.13 = bf16[512,3072]{1,0:T(8,128)(2,1)S(1)} fusion(f32[512,3072]{1,0:T(8,128)S(1)} %fusion.66, bf16[3072,768]{1,0:T(8,128)(2,1)S(1)} %bitcast.118, bf16[1,512,768]{2,1,0:T(8,128)(2,1)S(1)} %copy-done.26), kind=kOutput, calls=%fused_computation.20 | convolution fusion | flops 2447376384 | bytes 14942208 | tf_op jit(solution)/shard_map/dot_general | solution.py:34
  204.5 3.4 multiply_reduce_fusion
  210.5 63.0 %attend_backward_2.1 = (bf16[2304,512]{1,0:T(8,128)(2,1)}, f32[3,128,2048]{2,1,0:T(8,128)}) custom-call(bf16[768,512]{1,0:T(8,128)(2,1)} %convolution_convert_fusion.3.refs_0_, bf16[576,2048]{1,0:T(8,128)(2,1)} %copy-done, bf16[576,2048]{1,0:T(8,128)(2,1)} %copy-done.1, bf16[192,2048]{1,0:T(8,128)(2,1)} %copy-done.5, f32[3,1,2048]{2,1,0:T(1,128)} %copy-done.11), custom_call_target="tpu_custom_call" | custom-call | tf_op jit(solution)/shard_map/attend_backward_2/pallas_call | solution.py:686
  273.5 5.7 %multiply_reduce_fusion.2 = (f32[768]{0:T(1024)}, f32[512]{0:T(512)S(1)}, f32[512,768]{1,0:T(8,128)S(1)}) fusion(f32[512,768]{1,0:T(8,128)S(1)} %copy-done.17, f32[512]{0:T(512)S(1)} %fusion.58, f32[512]{0:T(512)S(1)} %broadcast_multiply_fusion.1, f32[768]{0:T(1024)S(1)} %reshape.323, bf16[2304,512]{1,0:T(8,128)(2,1)} %get-tuple-element.77, ...), kind=kOutput, calls=%fused_computation.51 | convolution fusion | flops 1814690560 | bytes 9056256 | tf_op jit(solution)/shard_map/dot_general | solution.py:768
  281.4 9.1 %fusion.6 = bf16[512,3072]{1,0:T(8,128)(2,1)S(1)} fusion(f32[512,3072]{1,0:T(8,128)} %copy-done.43, bf16[3072,768]{1,0:T(8,128)(2,1)} %get-tuple-element.71, f32[512,768]{1,0:T(8,128)S(1)} %get-tuple-element.99), kind=kOutput, calls=%fused_computation.13 | convolution fusion | flops 2447769600 | bytes 15728640 | tf_op jit(solution)/shard_map/dot_general | solution.py:34
  290.5 3.4 multiply_reduce_fusion.1
  299.1 2.8 fusion.64
  301.9 6.7 %add_convert_fusion.1 = bf16[768,3072]{1,0:T(8,128)(2,1)} fusion(f32[768,3072]{1,0:T(8,128)S(1)} %fusion.64, bf16[512,3072]{1,0:T(8,128)(2,1)} %copy-done.45, f32[512,768]{1,0:T(8,128)S(1)} %copy-done.19, f32[512]{0:T(512)S(1)} %fusion.59, f32[512]{0:T(512)S(1)} %broadcast_multiply_fusion, f32[768]{0:T(1024)S(1)} %reshape.324), kind=kOutput, calls=%fused_computation.1 | convolution fusion | flops 2422210560 | bytes 18881536 | tf_op jit(solution)/shard_map/dot_general | solution.py:28
  308.7 9.7 %fusion.36 = f32[3072,768]{1,0:T(8,128)} fusion(f32[512,768]{1,0:T(8,128)S(1)} %get-tuple-element.99, f32[512,3072]{1,0:T(8,128)} %copy-done.43), kind=kOutput, calls=%fused_computation.77 | convolution fusion | flops 2430468096 | bytes 17301504 | tf_op jit(solution)/shard_map/dot_general | solution.py:28
  318.3 11.2 %add_convert_fusion = bf16[3072,768]{1,0:T(8,128)(2,1)} fusion(f32[3072,768]{1,0:T(8,128)} %fusion.36, bf16[1,512,768]{2,1,0:T(8,128)(2,1)S(1)} %copy-done.27, f32[512,3072]{1,0:T(8,128)} %copy-done.44), kind=kOutput, calls=%fused_computation | convolution fusion | flops 2434793472 | bytes 21233664 | tf_op jit(solution)/shard_map/dot_general | solution.py:28
  329.6 121.8 %attend_backward_1.1 = (bf16[2304,512]{1,0:T(8,128)(2,1)}, f32[96,768]{1,0:T(8,128)}, f32[96,3072]{1,0:T(8,128)}, f32[384,768]{1,0:T(8,128)}) custom-call(bf16[768,512]{1,0:T(8,128)(2,1)} %convolution_convert_fusion.2.refs_0_, bf16[576,2048]{1,0:T(8,128)(2,1)} %copy-done, bf16[192,2048]{1,0:T(8,128)(2,1)} %copy-done.2, f32[3,1,2048]{2,1,0:T(1,128)} %copy-done.10, ...), custom_call_target="tpu_custom_call" | custom-call | tf_op jit(solution)/shard_map/attend_backward_1/pallas_call | solution.py:686
  451.5 3.9 fusion.28
  459.0 4.1 fusion.60
  463.1 2.6 add_convert_fusion.2
  465.7 54.6 %scatter_last.1 = (f32[8,256]{1,0:T(8,128)S(1)}, f32[96,2304]{1,0:T(8,128)S(1)}) custom-call(bf16[8,8,256]{2,1,0:T(8,128)(2,1)S(1)} %fusion.51.refs_0_, bf16[8,96,2304]{2,1,0:T(8,128)(2,1)S(1)} %bitcast.106), custom_call_target="tpu_custom_call" | custom-call | tf_op jit(solution)/shard_map/scatter_last/pallas_call | solution.py:353
  (166 shorter events, 39.2 us)
Async XLA Ops:
  42.6 4.1 copy-start.13
  130.2 17.2 %copy-start = (bf16[576,2048]{1,0:T(8,128)(2,1)}, bf16[576,2048]{1,0:T(8,128)(2,1)S(1)}, u32[]{:S(2)}) copy-start(bf16[576,2048]{1,0:T(8,128)(2,1)S(1)} %get-tuple-element.72.refs_1_) | copy-start | bytes 7077892
  134.2 6.6 %slice-start.4 = ((s8[4718592]{0:T(1024)(128)(4,1)}), s8[4194304]{0:T(1024)(128)(4,1)S(1)}, s32[]{:S(2)}) async-start(s8[4718592]{0:T(1024)(128)(4,1)} %bitcast.117), calls=%async_computation.4 | async-start | bytes 8388608
  136.1 4.7 copy-start.42
  136.1 4.7 slice-start.5
  140.8 3.8 copy-start.43
  140.8 4.3 copy-start.14
  144.7 43.9 %copy-start.16 = (f32[512,768]{1,0:T(8,128)}, f32[512,768]{1,0:T(8,128)S(1)}, u32[]{:S(2)}) copy-start(f32[512,768]{1,0:T(8,128)S(1)} %get-tuple-element.114) | copy-start | bytes 4718596
  144.7 45.8 %slice-start = ((s8[4718592]{0:T(1024)(128)(4,1)}), s8[4194304]{0:T(1024)(128)(4,1)S(1)}, s32[]{:S(2)}) async-start(s8[4718592]{0:T(1024)(128)(4,1)} %bitcast.108), calls=%async_computation | async-start | bytes 8388608
  145.1 134.1 %copy-start.34 = (f32[512]{0:T(512)}, f32[512]{0:T(512)S(1)}, u32[]{:S(2)}) copy-start(f32[512]{0:T(512)S(1)} %fusion.58) | copy-start | bytes 6148
  145.1 45.4 %slice-start.1 = ((s8[4718592]{0:T(1024)(128)(4,1)}), s8[524288]{0:T(1024)(128)(4,1)S(1)}, s32[]{:S(2)}) async-start(s8[4718592]{0:T(1024)(128)(4,1)} %bitcast.108), calls=%async_computation.1 | async-start | bytes 1048576
  190.2 17.8 %copy-start.18 = (f32[512,768]{1,0:T(8,128)}, f32[512,768]{1,0:T(8,128)S(1)}, u32[]{:S(2)}) copy-start(f32[512,768]{1,0:T(8,128)S(1)} %get-tuple-element.116) | copy-start | bytes 4718596
  193.2 4.7 copy-start.44
  193.3 4.7 copy-start.26
  210.5 63.0 %copy-start.17 = (f32[512,768]{1,0:T(8,128)S(1)}, f32[512,768]{1,0:T(8,128)}, u32[]{:S(2)}) copy-start(f32[512,768]{1,0:T(8,128)} %copy-done.16) | copy-start | bytes 4718596
  280.4 10.1 %slice-start.2 = ((s8[4718592]{0:T(1024)(128)(4,1)}), s8[4194304]{0:T(1024)(128)(4,1)S(1)}, s32[]{:S(2)}) async-start(s8[4718592]{0:T(1024)(128)(4,1)} %bitcast.110), calls=%async_computation.2 | async-start | bytes 8388608
  281.4 9.1 %slice-start.3 = ((s8[4718592]{0:T(1024)(128)(4,1)}), s8[524288]{0:T(1024)(128)(4,1)S(1)}, s32[]{:S(2)}) async-start(s8[4718592]{0:T(1024)(128)(4,1)} %bitcast.110), calls=%async_computation.3 | async-start | bytes 1048576
  281.4 9.1 %copy-start.23 = (f32[512,768]{1,0:T(8,128)S(1)}, f32[512,768]{1,0:T(8,128)}, u32[]{:S(2)}) copy-start(f32[512,768]{1,0:T(8,128)} %get-tuple-element.112) | copy-start | bytes 4718596
  329.6 121.9 %copy-start.15 = (bf16[768,2304]{1,0:T(8,128)(2,1)S(1)}, bf16[768,2304]{1,0:T(8,128)(2,1)}, u32[]{:S(2)}) copy-start(bf16[768,2304]{1,0:T(8,128)(2,1)} %copy-done.13) | copy-start | bytes 10616836
  329.6 121.9 %copy-start.25 = (bf16[1,512,768]{2,1,0:T(8,128)(2,1)S(1)}, bf16[1,512,768]{2,1,0:T(8,128)(2,1)}, u32[]{:S(2)}) copy-start(bf16[1,512,768]{2,1,0:T(8,128)(2,1)} %param.15) | copy-start | bytes 2359300
  451.4 4.0 copy-start.37
  451.5 4.0 copy-start.33
  459.0 4.1 copy-start.28
  459.0 4.2 copy-start.35
  (28 other events, 59.4 us)

commit v4 on v2

v4 whole, which is shorter than its diff:
```python
import functools

import jax
import jax.numpy as jnp
from jax import lax
from jax.experimental import pallas as pl
from jax.experimental.pallas import tpu as pltpu
from jax.sharding import PartitionSpec as P

HEAD_DIM = 64
CHUNK = 768
EVERY = 3
SLOTS = 5


epsilon = 1e-05


def layer_norm(vector, gain_vec):
    centre = vector - jnp.mean(vector, axis=-1, keepdims=True)
    spread = jnp.mean(centre * centre, axis=-1, keepdims=True)
    return centre * lax.rsqrt(spread + epsilon) * gain_vec


def gelu_value(vector):
    return jax.nn.gelu(vector, approximate=True)


def contract_rows(left_side, right_side):
    return lax.dot_general(
        left_side, right_side, (((0,), (0,)), ((), ())), preferred_element_type=jnp.float32
    )


def contract_cols(left_side, right_side):
    return lax.dot_general(
        left_side, right_side, (((1,), (1,)), ((), ())), preferred_element_type=jnp.float32
    )


def nt(left, right):
    return lax.dot_general(
        left, right, (((1,), (1,)), ((), ())), preferred_element_type=jnp.float32
    )


def nn(left, right):
    return lax.dot_general(
        left, right, (((1,), (0,)), ((), ())), preferred_element_type=jnp.float32
    )


def remote(src, dst, send_sem, recv_sem, device):
    return pltpu.make_async_remote_copy(
        src_ref=src,
        dst_ref=dst,
        send_sem=send_sem,
        recv_sem=recv_sem,
        device_id=device,
        device_id_type=pl.DeviceIdType.MESH,
    )


def greet(devices):
    barrier = pltpu.get_barrier_semaphore()
    for device in devices:
        pl.semaphore_signal(
            barrier, inc=1, device_id=device, device_id_type=pl.DeviceIdType.MESH
        )
    pl.semaphore_wait(barrier, len(devices))


def seq_peers(seq):
    me = lax.axis_index("seq")
    return [lax.rem(me + d, seq) for d in range(1, seq)]


class Gather:
    def __init__(self, seq, dp, shards, wholes, units, sems):
        self.line = dp // 2
        self.shards, self.wholes, self.units = shards, wholes, units
        self.z_send, self.z_recv, self.y_send, self.y_recv, self.c_send, self.c_recv, self.own = sems
        me = lax.axis_index("seq")
        self.core = lax.rem(me, 2)
        self.core_peer = {"seq": me + 1 - 2 * self.core}
        self.rank = lax.axis_index("dp")
        self.a, self.b = lax.div(self.rank, 2), lax.rem(self.rank, 2)
        self.y_peer = {"dp": self.a * 2 + 1 - self.b}
        self.flying, self.sent = {}, []

    @staticmethod
    def sems(arrays, units, dp):
        line, dma = dp // 2, pltpu.SemaphoreType.DMA
        sizes = (line, line, line, line, 2 * line, 2 * line)
        return [dma((units, size)) for size in sizes] + [dma((arrays,))]

    def z_rank(self, offset):
        return lax.rem(self.a + offset, self.line) * 2 + self.b

    def peers(self):
        z = [{"dp": self.z_rank(d)} for d in range(1, self.line)]
        return z + [self.y_peer]

    def columns(self, unit):
        array, row, rows, column, columns = self.units[unit]
        half = columns // 2
        return pl.ds(pl.multiple_of(column + self.core * half, 128), half)

    def block(self, unit, rank):
        array, row, rows, column, columns = self.units[unit]
        first = rank * self.shards[array].shape[0] + row
        return self.wholes[array].at[pl.ds(pl.multiple_of(first, 8), rows), self.columns(unit)]

    def send(self, key, src, dst, send_sem, recv_sem, device):
        copy = remote(src, dst, send_sem, recv_sem, device)
        copy.start()
        self.flying[key] = copy
        self.sent.append(copy)

    def keep_own(self):
        for array, (shard, whole) in enumerate(zip(self.shards, self.wholes)):
            rows = shard.shape[0]
            copy = pltpu.make_async_copy(
                shard, whole.at[pl.ds(pl.multiple_of(self.rank * rows, 8), rows)], self.own.at[array]
            )
            copy.start()
            self.flying["own", array] = copy

    def start(self, unit):
        array, row, rows = self.units[unit][:3]
        mine = self.shards[array].at[pl.ds(row, rows), self.columns(unit)]
        there = self.block(unit, self.rank)
        for d in range(1, self.line):
            self.send(
                ("z", unit, d),
                mine,
                there,
                self.z_send.at[unit, d],
                self.z_recv.at[unit, d],
                {"dp": self.z_rank(d)},
            )
        self.send(
            ("y", unit, 0), mine, there, self.y_send.at[unit, 0], self.y_recv.at[unit, 0], self.y_peer
        )

    def to_core(self, unit, slot, rank):
        block = self.block(unit, rank)
        self.send(
            ("core", unit, slot),
            block,
            block,
            self.c_send.at[unit, slot],
            self.c_recv.at[unit, slot],
            self.core_peer,
        )

    def forward_z(self, unit):
        for d in range(1, self.line):
            self.flying["z", unit, d].wait_recv()
            rank = self.z_rank(self.line - d)
            block = self.block(unit, rank)
            self.send(
                ("y", unit, d),
                block,
                block,
                self.y_send.at[unit, d],
                self.y_recv.at[unit, d],
                self.y_peer,
            )
            self.to_core(unit, d, rank)

    def forward_y(self, unit):
        for d in range(self.line):
            self.flying["y", unit, d].wait_recv()
            rank = lax.rem(self.a + self.line - d, self.line) * 2 + 1 - self.b
            self.to_core(unit, self.line + d, rank)

    def finish(self):
        for unit in range(len(self.units)):
            for slot in range(1, 2 * self.line):
                self.flying["core", unit, slot].wait_recv()
        for array in range(len(self.shards)):
            self.flying["own", array].wait()
        for copy in self.sent:
            copy.wait_send()

    def steps(self):
        count, calls = len(self.units), []
        for step in range(count + 1):
            if step < count:
                calls.append(functools.partial(self.forward_z, step))
            if step > 0:
                calls.append(functools.partial(self.forward_y, step - 1))
        return calls


def cut(shapes, rows, size):
    units = []
    for array, shape in enumerate(shapes):
        high, wide = min(shape[0], rows), min(shape[1], size)
        for row in range(0, shape[0], high):
            for column in range(0, shape[1], wide):
                units.append((array, row, high, column, wide))
    return units


def gather_kernel(seq, dp, units, arrays, *refs):
    shards, wholes, sems = refs[:arrays], refs[arrays : 2 * arrays], refs[2 * arrays :]
    gather = Gather(seq, dp, shards, wholes, units, sems)
    greet(gather.peers() + [gather.core_peer])
    for unit in range(len(units)):
        gather.start(unit)
    gather.keep_own()
    for call in gather.steps():
        call()
    gather.finish()


def whole_shape(shard, dp):
    return jax.ShapeDtypeStruct((shard.shape[0] * dp, shard.shape[1]), shard.dtype)


def gather_now(seq, dp, shards):
    arrays = len(shards)
    units = cut([shard.shape for shard in shards], shards[0].shape[0], CHUNK)
    hbm = pl.BlockSpec(memory_space=pl.ANY)
    return pl.pallas_call(
        functools.partial(gather_kernel, seq, dp, units, arrays),
        out_shape=tuple(whole_shape(shard, dp) for shard in shards),
        in_specs=[hbm] * arrays,
        out_specs=(hbm,) * arrays,
        scratch_shapes=Gather.sems(arrays, len(units), dp),
        compiler_params=pltpu.CompilerParams(
            collective_id=0, has_side_effects=True, vmem_limit_bytes=4 << 20
        ),
        name="gather_first",
    )(*shards)


class Scatter:
    def __init__(self, seq, dp, units, outs, scratch):
        self.seq, self.dp, self.line, self.chips = seq, dp, dp // 2, seq // 2
        self.units, self.outs = units, outs
        me = lax.axis_index("seq")
        self.core, self.chip = lax.rem(me, 2), lax.div(me, 2)
        self.core_peer = {"seq": me + 1 - 2 * self.core}
        self.rank = lax.axis_index("dp")
        self.a, self.b = lax.div(self.rank, 2), lax.rem(self.rank, 2)
        self.y_peer = {"dp": self.a * 2 + 1 - self.b}
        count = len(units)
        self.small, self.terms = scratch[0], scratch[1]
        self.buffers = [scratch[2 + 6 * u : 8 + 6 * u] for u in range(count)]
        self.sems = scratch[2 + 6 * count :]
        self.flying, self.sent = {}, {}

    @staticmethod
    def scratch(seq, dp, units):
        line, chips, b = dp // 2, seq // 2, jnp.bfloat16
        rows, columns = units[1][1:3]
        shapes = [
            pltpu.VMEM((dp,) + units[0][1:3], b),
            pltpu.VMEM((SLOTS, dp, rows, columns), b),
        ]
        for unit in units:
            rows, half = unit[1], unit[2] // 2
            for lead in ((dp,), (line,), (line,), (), (chips,)):
                shapes.append(pltpu.VMEM(lead + (rows, half), b))
            shapes.append(pltpu.VMEM((rows, 2 * half), jnp.float32))
        count, dma = len(units), pltpu.SemaphoreType.DMA
        sizes = (1, 1, 1, line, line, line, line, chips, chips, 1, 1)
        return shapes + [dma((count, size)) for size in sizes]

    def peers(self):
        z = [{"dp": self.other(d) * 2 + self.b} for d in range(1, self.line)]
        return z + [self.y_peer]

    def x_peers(self):
        return [
            {"seq": lax.rem(self.chip + d, self.chips) * 2 + self.core}
            for d in range(1, self.chips)
        ]

    def other(self, offset):
        return lax.rem(self.a + offset, self.line)

    def half(self, unit, core):
        half = self.units[unit][2] // 2
        return pl.ds(pl.multiple_of(core * half, 128), half)

    def term(self, unit, row, core):
        lanes = self.half(unit, core)
        if unit == 0:
            return self.small.at[row, :, lanes]
        return self.terms.at[(unit - 1) % SLOTS, row, :, lanes]

    def all_terms(self, unit, core):
        lanes = self.half(unit, core)
        if unit == 0:
            return self.small.at[:, :, lanes]
        return self.terms.at[(unit - 1) % SLOTS, :, :, lanes]

    def send(self, key, src, dst, sems, slot, device):
        unit = key[1]
        copy = remote(
            src, dst, self.sems[sems].at[unit, slot], self.sems[sems + 1].at[unit, slot], device
        )
        copy.start()
        self.flying[key] = copy
        self.sent.setdefault((unit, key[0] in ("core", "y", "z")), []).append(copy)

    def free(self, unit):
        if unit >= 1:
            for copy in self.sent.pop((unit, True), []):
                copy.wait_send()

    def start(self, unit):
        self.send(
            ("core", unit), self.all_terms(unit, 1 - self.core), self.buffers[unit][0], 0, 0, self.core_peer
        )

    def chip_sum(self, unit):
        core_in, y_in = self.buffers[unit][:2]
        self.flying["core", unit].wait_recv()
        for place in range(self.line):
            row = place * 2 + 1 - self.b
            total = self.term(unit, row, self.core)
            total[...] = add(total[...], core_in[row]).astype(jnp.bfloat16)
            self.send(("y", unit, place), total, y_in.at[place], 3, place, self.y_peer)

    def y_sum(self, unit):
        core_in, y_in, z_in = self.buffers[unit][:3]
        for place in range(self.line):
            self.flying["y", unit, place].wait_recv()
        for d in range(1, self.line):
            place = self.other(d)
            row = place * 2 + self.b
            total = self.term(unit, row, self.core)
            total[...] = add(total[...], core_in[row], y_in[place]).astype(jnp.bfloat16)
            self.send(("z", unit, d), total, z_in.at[d], 5, d, {"dp": row})

    def z_sum(self, unit):
        core_in, y_in, z_in, x_out, x_in = self.buffers[unit][:5]
        for d in range(1, self.line):
            self.flying["z", unit, d].wait_recv()
        terms = [self.term(unit, self.rank, self.core)[...], core_in[self.rank], y_in[self.a]]
        terms += [z_in[d] for d in range(1, self.line)]
        x_out[...] = add(*terms).astype(jnp.bfloat16)
        for d, peer in enumerate(self.x_peers()):
            self.send(("x", unit, d), x_out, x_in.at[d], 7, d, peer)

    def x_sum(self, unit):
        x_out, x_in, final = self.buffers[unit][3:]
        for d in range(self.chips - 1):
            self.flying["x", unit, d].wait_recv()
        mine = self.half(unit, self.core)
        final[:, mine] = add(x_out[...], *[x_in[d] for d in range(self.chips - 1)])
        self.send(("f", unit), final.at[:, mine], final.at[:, mine], 9, 0, self.core_peer)

    def finish(self, unit):
        array, rows, columns, row, column = self.units[unit]
        self.flying["f", unit].wait_recv()
        self.sent.pop((unit, False))
        for key in (("f", unit), *[("x", unit, d) for d in range(self.chips - 1)]):
            self.flying[key].wait_send()
        copy = pltpu.make_async_copy(
            self.buffers[unit][5],
            self.outs[array].at[pl.ds(row, rows), pl.ds(column, columns)],
            self.sems[2].at[unit, 0],
        )
        copy.start()
        self.flying["out", unit] = copy

    def drain(self):
        for copies in self.sent.values():
            for copy in copies:
                copy.wait_send()
        for unit in range(len(self.units)):
            self.flying["out", unit].wait()


def add(*terms):
    total = terms[0].astype(jnp.float32)
    for term in terms[1:]:
        total = total + term.astype(jnp.float32)
    return total


class Products:
    def __init__(self, refs, scratch, work, d_packed):
        (
            self.small,
            mixed,
            middle,
            active,
            upstream,
            normed_b,
            d_hidden,
            normed,
            self.second_packed,
        ) = refs
        self.stream, self.keep_rows, self.keep_left, self.result, self.sems = scratch
        self.work, self.d_packed = work, d_packed
        self.width, self.both = self.stream.shape[1:]
        self.tokens = self.both // 2
        self.mixed, self.active, self.d_hidden = mixed, active, d_hidden
        self.kept = [(middle, self.keep_rows.at[0]), (upstream, self.keep_rows.at[1])]
        self.kept += [(normed_b, self.keep_left.at[0]), (normed, self.keep_left.at[1])]
        self.flying = {}

    @staticmethod
    def scratch(width, tokens):
        b = jnp.bfloat16
        return [
            pltpu.VMEM((2, width, 2 * tokens), b),
            pltpu.VMEM((2, 2 * tokens, width), b),
            pltpu.VMEM((2, width, 2 * tokens), b),
            pltpu.VMEM((width, width), jnp.float32),
            pltpu.SemaphoreType.DMA((32, 2)),
        ]

    def copy(self, key, slot, side, src, dst):
        copy = pltpu.make_async_copy(src, dst, self.sems.at[slot, side])
        copy.start()
        self.flying.setdefault(key, []).append(copy)

    def wait(self, key):
        for copy in self.flying.pop(key, []):
            copy.wait()

    def begin(self):
        self.copy("small", 30, 0, self.small, self.work.small)
        self.fetch(1)
        for index, (pair, place) in enumerate(self.kept):
            for side in range(2):
                span = pl.ds(side * self.tokens, self.tokens)
                where = place.at[span] if index < 2 else place.at[:, span]
                self.copy(("kept", index), 20 + index, side, pair[side], where)
        self.fetch(2)

    def kind(self, unit):
        array, rows, columns, row, column = self.work.units[unit]
        return array, row // rows, column // columns

    def fetch(self, unit):
        if unit >= len(self.work.units):
            return
        array, row, column = self.kind(unit)
        slot = unit % 2
        for side in range(2):
            lanes = pl.ds(side * self.tokens, self.tokens)
            if array == 1:
                self.copy(unit, unit, side, self.mixed[side], self.stream.at[slot, :, lanes])
            elif array == 3:
                rows = self.work.units[unit][1]
                for rank in range(self.work.dp):
                    pltpu.make_async_copy(
                        self.active[side].at[rank, row],
                        self.stream.at[slot, pl.ds(rank * rows, rows), lanes],
                        self.sems.at[unit, side],
                    ).start()
                all_ranks = pltpu.make_async_copy(
                    self.d_hidden[side].at[pl.ds(0, self.width)],
                    self.stream.at[slot, :, lanes],
                    self.sems.at[unit, side],
                )
                self.flying.setdefault(unit, []).append(all_ranks)
            elif array == 2:
                self.copy(
                    unit,
                    unit,
                    side,
                    self.d_hidden[side].at[pl.ds(column * self.width, self.width)],
                    self.stream.at[slot, :, lanes],
                )
            elif side == 1:
                self.copy(
                    unit,
                    unit,
                    side,
                    self.second_packed.at[pl.ds(column * self.width, self.width)],
                    self.stream.at[slot, :, lanes],
                )

    def make(self, unit):
        work = self.work
        if unit == 0:
            self.wait("small")
            work.start(0)
            return
        array, row, column = self.kind(unit)
        slot = unit % 2
        kept = {1: 0, 3: 1, 2: 2, 4: 3}[array]
        self.wait(("kept", kept))
        self.wait(unit)
        if array == 4:
            self.stream[slot, :, : self.tokens] = self.d_packed[
                column * self.width : (column + 1) * self.width, :
            ]
        step = self.width // 3
        for part in range(3):
            span = slice(part * step, (part + 1) * step)
            if kept < 2:
                self.result[span, :] = nn(self.stream[slot, span, :], self.keep_rows[kept])
            else:
                self.result[span, :] = nt(self.keep_left[kept - 2, span, :], self.stream[slot])
        work.free(unit - SLOTS)
        rows = work.units[unit][1]
        for rank in range(work.dp):
            work.terms[(unit - 1) % SLOTS, rank] = self.result[
                rank * rows : (rank + 1) * rows, :
            ].astype(jnp.bfloat16)
        work.start(unit)
        self.fetch(unit + 2)


def background_order(work, products):
    count = len(work.units)
    stages = (
        (3, products.make),
        (2, work.chip_sum),
        (0, work.y_sum),
        (-1, work.z_sum),
        (-2, work.x_sum),
        (-3, work.finish),
    )
    order = []
    for step in range(-3, count + 3):
        calls = [
            functools.partial(call, step + ahead) for ahead, call in stages if 0 <= step + ahead < count
        ]
        order.append(calls)
    return order


def causal_mask(size):
    rows = lax.broadcasted_iota(jnp.int32, (size, size), 0)
    columns = lax.broadcasted_iota(jnp.int32, (size, size), 1)
    return rows <= columns


def forward_kernel(seq, dp, sets, units, arrays, heads, *refs):
    refs = list(refs)

    def take(count):
        taken = refs[:count]
        del refs[:count]
        return taken

    (packed,) = take(1)
    earlier = take(sets - 1)
    shards = take(arrays)
    heads_out, mixed_out, own_out, totals_out = take(4)
    wholes = take(arrays)
    arrived, mixed_in, q_s, k_s, v_s, in_send, in_recv, out_send, out_recv = take(9)
    gather = Gather(seq, dp, shards, wholes, units, refs) if units else None

    tokens = packed.shape[1]
    length = tokens * seq
    group = 3 * HEAD_DIM
    me = lax.axis_index("seq")
    peers = seq_peers(seq)
    greet([{"seq": peer} for peer in peers] + (gather.peers() if units else []))

    own_lanes = pl.ds(pl.multiple_of(me * tokens, tokens), tokens)
    copies = {}
    for h in range(heads):
        for d, peer in enumerate(peers):
            copy = remote(
                packed.at[pl.ds(pl.multiple_of((peer * heads + h) * group, group), group)],
                arrived.at[pl.ds(h * group, group), own_lanes],
                in_send.at[h, d],
                in_recv.at[h, d],
                {"seq": peer},
            )
            copy.start()
            copies[h, d] = copy
    steps = []
    if units:
        for unit in range(len(units)):
            gather.start(unit)
        gather.keep_own()
        steps = gather.steps()
        steps.pop(0)()
    for h in range(heads):
        arrived[h * group : (h + 1) * group, own_lanes] = packed[
            pl.ds(pl.multiple_of((me * heads + h) * group, group), group), :
        ]

    mask = causal_mask(tokens)
    for s in range(sets):
        v_s[s, HEAD_DIM:] = jnp.ones((16, length), jnp.bfloat16)
    results = []
    for h in range(heads):
        c0 = h * group
        for s in range(sets):
            source = earlier[s] if s < sets - 1 else arrived
            if s == sets - 1:
                for d in range(seq - 1):
                    copies[h, d].wait_recv()
                heads_out[c0 : c0 + group, :] = arrived[c0 : c0 + group, :]
                q_s[...] = arrived[c0 : c0 + HEAD_DIM, :] * jnp.bfloat16(HEAD_DIM**-0.5)
            k_s[s] = source[c0 + HEAD_DIM : c0 + 2 * HEAD_DIM, :].T
            v_s[s, :HEAD_DIM] = source[c0 + 2 * HEAD_DIM : c0 + 3 * HEAD_DIM, :]

        for i in range(seq):
            queries = q_s[:, i * tokens : (i + 1) * tokens]
            peak = total = None
            for j in [i] + list(range(i)):
                keys = slice(j * tokens, (j + 1) * tokens)
                scores = []
                for s in range(sets):
                    block = nn(k_s[s, keys, :], queries)
                    if j == i:
                        block = jnp.where(mask, block, -1e30)
                    scores.append(block)
                peak_now = peak
                for block in scores:
                    top = jnp.max(block, axis=0, keepdims=True)
                    peak_now = top if peak_now is None else jnp.maximum(peak_now, top)
                if total is not None:
                    total = total * jnp.exp(peak - peak_now)
                for s, block in enumerate(scores):
                    weights = jnp.exp(block - peak_now).astype(jnp.bfloat16)
                    part = nn(v_s[s, :, keys], weights)
                    total = part if total is None else total + part
                peak = peak_now
            row_sum = total[HEAD_DIM : HEAD_DIM + 1]
            own_out[h * HEAD_DIM : (h + 1) * HEAD_DIM, i * tokens : (i + 1) * tokens] = (
                total[:HEAD_DIM] / row_sum
            ).astype(jnp.bfloat16)
            totals_out[h, :, i * tokens : (i + 1) * tokens] = peak + jnp.log(row_sum)
            if steps and i % 2 == 1:
                steps.pop(0)()

        mine = pl.ds(pl.multiple_of((me * heads + h) * HEAD_DIM, HEAD_DIM), HEAD_DIM)
        for d, peer in enumerate(peers):
            copy = remote(
                own_out.at[
                    pl.ds(h * HEAD_DIM, HEAD_DIM),
                    pl.ds(pl.multiple_of(peer * tokens, tokens), tokens),
                ],
                mixed_in.at[mine],
                out_send.at[h, d],
                out_recv.at[h, d],
                {"seq": peer},
            )
            copy.start()
            results.append(copy)
        mixed_in[mine] = own_out[h * HEAD_DIM : (h + 1) * HEAD_DIM, own_lanes]
    for step in steps:
        step()
    if units:
        gather.finish()
    for copy in copies.values():
        copy.wait_send()
    for copy in results:
        copy.wait()
    mixed_out[...] = mixed_in[...]


def attend_forward(seq, dp, heads, packed, earlier, shards, call_id):
    width, tokens = packed.shape
    length = tokens * seq
    sets, arrays = 1 + len(earlier), len(shards)
    units = cut([shard.shape for shard in shards], shards[0].shape[0], CHUNK) if arrays else []
    rows = heads * 3 * HEAD_DIM
    vmem = pl.BlockSpec(memory_space=pltpu.VMEM)
    hbm = pl.BlockSpec(memory_space=pl.ANY)
    dma = pltpu.SemaphoreType.DMA
    outs = pl.pallas_call(
        functools.partial(forward_kernel, seq, dp, sets, units, arrays, heads),
        out_shape=(
            jax.ShapeDtypeStruct((rows, length), jnp.bfloat16),
            jax.ShapeDtypeStruct((width // 3, tokens), jnp.bfloat16),
            jax.ShapeDtypeStruct((heads * HEAD_DIM, length), jnp.bfloat16),
            jax.ShapeDtypeStruct((heads, 1, length), jnp.float32),
        )
        + tuple(whole_shape(shard, dp) for shard in shards),
        in_specs=[vmem] * sets + [hbm] * arrays,
        out_specs=(vmem,) * 4 + (hbm,) * arrays,
        scratch_shapes=[
            pltpu.VMEM((rows, length), jnp.bfloat16),
            pltpu.VMEM((width // 3, tokens), jnp.bfloat16),
            pltpu.VMEM((HEAD_DIM, length), jnp.bfloat16),
            pltpu.VMEM((sets, length, HEAD_DIM), jnp.bfloat16),
            pltpu.VMEM((sets, HEAD_DIM + 16, length), jnp.bfloat16),
            dma((heads, seq)),
            dma((heads, seq)),
            dma((heads, seq)),
            dma((heads, seq)),
        ]
        + (Gather.sems(arrays, len(units), dp) if units else []),
        compiler_params=pltpu.CompilerParams(
            collective_id=call_id, has_side_effects=True, vmem_limit_bytes=40 << 20
        ),
        name=f"attend_forward_{sets}",
    )(packed, *earlier, *shards)
    return outs[:4], outs[4:]


def backward_kernel(seq, dp, sets, units, heads, *refs):
    refs = list(refs)

    def take(count):
        taken = refs[:count]
        del refs[:count]
        return taken

    (d_mixed,) = take(1)
    packs = take(sets)
    own_in, totals_in = take(2)
    if units:
        (carry_in, small) = take(2)
        pairs = [take(2) for _ in range(7)]
        (second_packed,) = take(1)
    (d_packed_out,) = take(1)
    carry_out = None if units else take(1)[0]
    grads_out = take(5) if units else []
    arrived, local_grad, d_packed_in, q_s, k_s, kt_s, v_s, delta_s, dq_s, dkv_s = take(10)
    in_send, in_recv, out_send, out_recv, out_sem = take(5)
    if units:
        carry_s, carry_sem = take(2)
        product_scratch = take(5)
        work = Scatter(seq, dp, units, grads_out, refs)
        products = Products([small] + pairs + [second_packed], product_scratch, work, d_packed_in)

    tokens = d_mixed.shape[1]
    length = tokens * seq
    group = 3 * HEAD_DIM
    me = lax.axis_index("seq")
    peers = seq_peers(seq)
    greet([{"seq": peer} for peer in peers] + (work.peers() if units else []))
    own_lanes = pl.ds(pl.multiple_of(me * tokens, tokens), tokens)
    scale = jnp.bfloat16(HEAD_DIM**-0.5)

    copies = {}
    for h in range(heads):
        for d, peer in enumerate(peers):
            copy = remote(
                d_mixed.at[pl.ds(pl.multiple_of((peer * heads + h) * HEAD_DIM, HEAD_DIM), HEAD_DIM)],
                arrived.at[pl.ds(h * HEAD_DIM, HEAD_DIM), own_lanes],
                in_send.at[h, d],
                in_recv.at[h, d],
                {"seq": peer},
            )
            copy.start()
            copies[h, d] = copy
    steps = []
    if units:
        products.begin()
        steps = background_order(work, products)
        early = [unit[0] for unit in units].index(4)
        later = steps[early:]
        steps = steps[:early]
    for h in range(heads):
        arrived[h * HEAD_DIM : (h + 1) * HEAD_DIM, own_lanes] = d_mixed[
            pl.ds(pl.multiple_of((me * heads + h) * HEAD_DIM, HEAD_DIM), HEAD_DIM), :
        ]

    def run(calls):
        for call in calls:
            call()

    def outgoing(h, rank, send_slot):
        return remote(
            local_grad.at[
                pl.ds(h * group, group), pl.ds(pl.multiple_of(rank * tokens, tokens), tokens)
            ],
            d_packed_in.at[pl.ds(pl.multiple_of((me * heads + h) * group, group), group)],
            out_send.at[h, send_slot],
            out_recv.at[h, me],
            {"seq": rank},
        )

    if steps:
        run(steps.pop(0))
    mask = causal_mask(tokens)
    hook = 0
    for h in range(heads):
        c0 = h * group
        r0 = h * HEAD_DIM
        if units:
            carried = pltpu.make_async_copy(carry_in.at[h], carry_s, carry_sem.at[h])
            carried.start()
        q_s[...] = packs[-1][c0 : c0 + HEAD_DIM, :] * scale
        for s in range(sets):
            keys = packs[s][c0 + HEAD_DIM : c0 + 2 * HEAD_DIM, :]
            k_s[s] = keys.T
            kt_s[s] = keys * scale
            v_s[s] = packs[s][c0 + 2 * HEAD_DIM : c0 + 3 * HEAD_DIM, :].T
        for d in range(seq - 1):
            copies[h, d].wait_recv()
        delta_s[...] = jnp.sum(
            arrived[r0 : r0 + HEAD_DIM, :].astype(jnp.float32)
            * own_in[r0 : r0 + HEAD_DIM, :].astype(jnp.float32),
            axis=0,
            keepdims=True,
        )
        if units:
            carried.wait()
        for j in range(seq):
            keys = slice(j * tokens, (j + 1) * tokens)
            for i in range(j, seq):
                span = slice(i * tokens, (i + 1) * tokens)
                queries = q_s[:, span]
                grads = arrived[r0 : r0 + HEAD_DIM, span]
                d_query = dq_s[:, span] if j > 0 else None
                for s in range(sets):
                    chances = jnp.exp(nn(k_s[s, keys, :], queries) - totals_in[h, :, span])
                    if i == j:
                        chances = jnp.where(mask, chances, 0.0)
                    d_chance = nn(v_s[s, keys, :], grads)
                    d_score = (chances * (d_chance - delta_s[:, span])).astype(jnp.bfloat16)
                    d_key = nt(queries, d_score)
                    d_value = nt(grads, chances.astype(jnp.bfloat16))
                    if i == j:
                        if units:
                            d_key = d_key + carry_s[:HEAD_DIM, keys]
                            d_value = d_value + carry_s[HEAD_DIM:, keys]
                        dkv_s[s, :HEAD_DIM, keys] = d_key
                        dkv_s[s, HEAD_DIM:, keys] = d_value
                    else:
                        dkv_s[s, :HEAD_DIM, keys] += d_key
                        dkv_s[s, HEAD_DIM:, keys] += d_value
                    part = nn(kt_s[s, :, keys], d_score)
                    d_query = part if d_query is None else d_query + part
                dq_s[:, span] = d_query
                hook += 1
                if steps and hook % EVERY == 0:
                    run(steps.pop(0))
            local_grad[c0 : c0 + HEAD_DIM, keys] = dq_s[:, keys].astype(jnp.bfloat16)
            local_grad[c0 + HEAD_DIM : c0 + group, keys] = dkv_s[sets - 1, :, keys].astype(
                jnp.bfloat16
            )
            if h == heads - 1:

                @pl.when(me != j)
                def _():
                    outgoing(h, jnp.int32(j), j).start()

        if not units:
            carry_out[h] = dkv_s[0]
        if h < heads - 1:
            for d, peer in enumerate(peers):
                outgoing(h, peer, d).start()
        d_packed_in[pl.ds(pl.multiple_of((me * heads + h) * group, group), group)] = local_grad[
            c0 : c0 + group, own_lanes
        ]
    for calls in steps:
        run(calls)
    for h in range(heads):
        for peer in peers:
            remote(
                local_grad.at[pl.ds(h * group, group), own_lanes],
                d_packed_in.at[pl.ds(pl.multiple_of((peer * heads + h) * group, group), group)],
                out_send.at[h, 0],
                out_recv.at[h, peer],
                {"seq": peer},
            ).wait_recv()
    finished = pltpu.make_async_copy(d_packed_in, d_packed_out, out_sem.at[0])
    finished.start()
    if units:
        for calls in later:
            run(calls)
        work.drain()
    for copy in copies.values():
        copy.wait_send()
    for h in range(heads - 1):
        for d, peer in enumerate(peers):
            outgoing(h, peer, d).wait_send()
    for j in range(seq):

        @pl.when(me != j)
        def _():
            outgoing(heads - 1, jnp.int32(j), j).wait_send()

    finished.wait()


def attend_backward(seq, dp, heads, d_mixed, packs, own, totals, extra, units, call_id):
    width, tokens = d_mixed.shape
    length = tokens * seq
    sets = len(packs)
    rows = heads * 3 * HEAD_DIM
    vmem = pl.BlockSpec(memory_space=pltpu.VMEM)
    hbm = pl.BlockSpec(memory_space=pl.ANY)
    dma = pltpu.SemaphoreType.DMA
    f32 = jnp.float32
    out_shape = [jax.ShapeDtypeStruct((3 * width, tokens), jnp.bfloat16)]
    out_specs = [hbm]
    more = []
    if units:
        heights = [0] * 5
        for array, high, wide, row, column in units:
            heights[array] = max(heights[array], row + high)
        widths = [0] * 5
        for array, high, wide, row, column in units:
            widths[array] = max(widths[array], column + wide)
        out_shape += [jax.ShapeDtypeStruct(shape, f32) for shape in zip(heights, widths)]
        out_specs += [hbm] * 5
        more = [pltpu.VMEM((2 * HEAD_DIM, length), f32), dma((heads,))]
        more += Products.scratch(width, tokens) + Scatter.scratch(seq, dp, units)
    else:
        out_shape.append(jax.ShapeDtypeStruct((heads, 2 * HEAD_DIM, length), f32))
        out_specs.append(vmem)
    return pl.pallas_call(
        functools.partial(backward_kernel, seq, dp, sets, units, heads),
        out_shape=tuple(out_shape),
        in_specs=[vmem] * (3 + sets) + [hbm] * len(extra),
        out_specs=tuple(out_specs),
        scratch_shapes=[
            pltpu.VMEM((heads * HEAD_DIM, length), jnp.bfloat16),
            pltpu.VMEM((rows, length), jnp.bfloat16),
            pltpu.VMEM((3 * width, tokens), jnp.bfloat16),
            pltpu.VMEM((HEAD_DIM, length), jnp.bfloat16),
            pltpu.VMEM((sets, length, HEAD_DIM), jnp.bfloat16),
            pltpu.VMEM((sets, HEAD_DIM, length), jnp.bfloat16),
            pltpu.VMEM((sets, length, HEAD_DIM), jnp.bfloat16),
            pltpu.VMEM((1, length), f32),
            pltpu.VMEM((HEAD_DIM, length), f32),
            pltpu.VMEM((sets, 2 * HEAD_DIM, length), f32),
            dma((heads, seq)),
            dma((heads, seq)),
            dma((heads, seq)),
            dma((heads, seq)),
            dma((1,)),
        ]
        + more,
        compiler_params=pltpu.CompilerParams(
            collective_id=call_id, has_side_effects=True, vmem_limit_bytes=60 << 20
        ),
        name=f"attend_backward_{sets}",
    )(d_mixed, *packs, own, totals, *extra)


def dots(left, right, left_side, right_side):
    return lax.dot_general(
        left,
        right,
        (((left_side,), (right_side,)), ((), ())),
        preferred_element_type=jnp.float32,
    )


def block_forward(sizes, call_id, stream, qkv_w, gains, earlier, weights, shards):
    seq, dp, heads = sizes
    normed = layer_norm(stream, gains[0]).astype(jnp.bfloat16)
    packed = dots(qkv_w, normed, 0, 1).astype(jnp.bfloat16)
    (head_rows, mixed, own, totals), gathered = attend_forward(
        seq, dp, heads, packed, earlier, shards, call_id
    )
    out_w, up_w, down_w = weights or gathered
    middle = stream + dots(mixed, out_w, 0, 0)
    normed_b = layer_norm(middle, gains[1]).astype(jnp.bfloat16)
    hidden = dots(up_w, normed_b, 0, 1)
    active = gelu_value(hidden).astype(jnp.bfloat16)
    result = middle + dots(active, down_w, 0, 0)
    stored = (
        stream,
        normed.T,
        earlier + [head_rows],
        own,
        totals,
        mixed,
        middle,
        normed_b.T,
        hidden,
        active,
    )
    return result, stored, (out_w, up_w, down_w)


def block_backward(sizes, call_id, upstream, stored, qkv_w, gains, weights, second):
    seq, dp, heads = sizes
    out_w, up_w, down_w = weights
    stream, normed, packs, own, totals, mixed, middle, normed_b, hidden, active = stored
    out_bf = upstream.astype(jnp.bfloat16)
    d_active = dots(down_w, out_bf, 1, 1)
    d_hidden = jax.vjp(gelu_value, hidden)[1](d_active)[0].astype(jnp.bfloat16)
    d_normed_b = dots(d_hidden, up_w, 0, 1)
    d_middle_norm = jax.vjp(layer_norm, middle, gains[1])[1](d_normed_b)[0]
    d_middle = upstream + d_middle_norm
    middle_bf = d_middle.astype(jnp.bfloat16)
    d_mixed = dots(out_w, middle_bf, 1, 1).astype(jnp.bfloat16)
    width, tokens = d_mixed.shape
    rows = width // dp
    active = active.reshape(dp, active.shape[0] // width, rows, tokens)
    factors = (mixed, middle_bf, active, out_bf, normed_b, d_hidden, normed)
    extra, units = [], []
    if second is not None:
        passed, small, second_factors, second_packed = second
        extra = [passed, small]
        for pair in zip(factors, second_factors):
            extra += pair
        extra.append(second_packed)
        ff = d_hidden.shape[0]
        units = [(0, 8, 256, 0, 0)]
        units += [(1, rows, width, 0, 0)]
        units += [(3, rows, width, row, 0) for row in range(0, ff // dp, rows)]
        units += [(2, rows, width, 0, column) for column in range(0, ff, width)]
        units += [(4, rows, width, 0, column) for column in range(0, 3 * width, width)]
    outs = attend_backward(seq, dp, heads, d_mixed, packs, own, totals, extra, units, call_id)
    d_packed = outs[0]
    d_normed = dots(d_packed, qkv_w, 0, 1)
    d_stream_norm = jax.vjp(layer_norm, stream, gains[0])[1](d_normed)[0]
    return d_middle + d_stream_norm, factors, outs


def local(
    seq,
    dp,
    tokens,
    qkv_weight,
    out_weight,
    up_weight,
    down_weight,
    norm_gain,
    mlp_gain,
    pass_embed,
    cotangent,
):
    share = norm_gain.shape[0]
    lanes = [
        jnp.pad(v.reshape(1, share), ((0, 0), (0, 128 - share)))
        for v in (norm_gain, pass_embed, mlp_gain)
    ]
    small = jnp.concatenate(
        [
            jnp.concatenate(lanes[:2], axis=1),
            jnp.pad(lanes[2], ((0, 0), (0, 128))),
            jnp.zeros((6, 256), jnp.bfloat16),
        ]
    )
    qkv_w, small = gather_now(seq, dp, [qkv_weight, small])
    small = small.reshape(dp, 8, 256)
    gains = [small[:, row, :share].reshape(-1).astype(jnp.float32) for row in (0, 1)]
    embedding = small[:, 0, 128 : 128 + share].reshape(-1).astype(jnp.float32)
    heads = qkv_weight.shape[1] // (3 * HEAD_DIM * seq)
    sizes = (seq, dp, heads)
    first_out, first_kept, weights = block_forward(
        sizes,
        1,
        tokens[0].astype(jnp.float32),
        qkv_w,
        gains,
        [],
        None,
        [out_weight, up_weight, down_weight],
    )
    second_out, second_kept, weights = block_forward(
        sizes, 2, first_out + embedding, qkv_w, gains, [first_kept[2][0]], weights, []
    )
    d_second, factors, outs = block_backward(
        sizes, 3, cotangent[0].astype(jnp.float32), second_kept, qkv_w, gains, weights, None
    )
    embed = jnp.sum(d_second, axis=0).astype(jnp.bfloat16).reshape(dp, 1, share)
    embed = jnp.pad(embed, ((0, 0), (0, 7), (0, 256 - share)))
    second = (outs[1], embed, factors, outs[0])
    d_first, factors, outs = block_backward(
        sizes, 4, d_second, first_kept, qkv_w, gains, weights, second
    )
    packed, small, out_grad, up_grad, down_grad, qkv_grad = outs
    f32 = jnp.float32
    gain_a = jnp.sum(qkv_weight.astype(f32) * qkv_grad, axis=1) / norm_gain.astype(f32)
    gain_b = jnp.sum(up_weight.astype(f32) * up_grad, axis=1) / mlp_gain.astype(f32)
    return (
        second_out.astype(jnp.bfloat16)[None],
        d_first[None],
        qkv_grad,
        out_grad,
        up_grad,
        down_grad,
        gain_a,
        gain_b,
        small[0, :share],
    )


def solution(mesh):
    in_specs = (
        P("dp", "seq", None),
        P("dp", None),
        P("dp", None),
        P("dp", None),
        P("dp", None),
        P("dp"),
        P("dp"),
        P("dp"),
        P("dp", "seq", None),
    )
    out_specs = (
        P("dp", "seq", None),
        P("dp", "seq", None),
        P("dp", None),
        P("dp", None),
        P("dp", None),
        P("dp", None),
        P("dp"),
        P("dp"),
        P("dp"),
    )
    return jax.shard_map(
        functools.partial(local, mesh.shape["seq"], mesh.shape["dp"]), mesh=mesh, in_specs=in_specs, out_specs=out_specs, check_vma=False)
```

time: 721 us -> 446 us (0.62)
  waiting for transfers between devices: 266 us -> 0 us
  Pallas kernels: 260 us -> 334 us
  matrix products: 98.2 us -> 63.5 us
  blocking collectives: 33.6 us -> 0 us
  between operations: 15.8 us -> 1.68 us
    reduce_scatter x4 -> x0, waiting for transfers between devices: 226 us -> none  [the longest x1 98.7 us: local(): lax.psum_scatter(summed[3].astype(jnp.bfloat16), 'dp', scatter_dimension=...]
    pallas_call x5, Pallas kernels: 260 us -> 334 us  [the longest x2 185 us: attend_backward(): pl.pallas_call(functools.partial(backward_kernel, seq, dp, sets, units, h...]
    psum x1 -> x0, waiting for transfers between devices: 40.1 us -> none  [local(): lax.psum(shards[0].astype(jnp.bfloat16), 'seq').astype(jnp.float32)]
    dot_general x24 -> x16, matrix products: 98.2 us -> 63.5 us  [dots(): lax.dot_general(left, right, (((left_side,), (right_side,)), ((), ())), p...]
    unnamed x1 -> x0, blocking collectives: 27.9 us -> none
    unnamed x156 -> x142, local copies, waits for them, and re-layouts: 14 us -> 16.6 us
  transfers between devices with their start and end apart: 5 -> 0, of which waited for: 4 -> 0; matrix products, arithmetic and copies ran while one was open for 7% -> 0% of each run, Pallas kernels for 6% -> 0%
where the time goes in v4:
time: 446 us; the launch traced here: 438 us
  Pallas kernels  334 us (75%)
  matrix products  63.5 us (14%)
  local copies, waits for them, and re-layouts  23.7 us (5%)
  other arithmetic  15.6 us (3%)
    pallas_call x2, Pallas kernels, attend_backward(): pl.pallas_call(functools.partial(backward_kernel, seq, dp, sets, units, h...  185 us
    pallas_call x2, Pallas kernels, attend_forward(): pl.pallas_call(functools.partial(forward_kernel, seq, dp, sets, units, ar...  117 us
    dot_general x16, matrix products, dots(): lax.dot_general(left, right, (((left_side,), (right_side,)), ((), ())), p...  63.5 us
    pallas_call x1, Pallas kernels, gather_now(): pl.pallas_call(functools.partial(gather_kernel, seq, dp, units, arrays),...  32.2 us
    unnamed x142, local copies, waits for them, and re-layouts  16.6 us

profile of v4, /device:TPU:0, one launch (start us, length us, event | category | flops | bytes accessed | tf_op | source)
XLA Modules:
  0.0 438.4 jit_solution(18252748699602604161)
XLA Ops:
  4.3 32.2 %gather_first.1 = (bf16[768,2304]{1,0:T(8,128)(2,1)S(1)}, bf16[64,256]{1,0:T(8,128)(2,1)S(1)}) custom-call(bf16[96,2304]{1,0:T(8,128)(2,1)S(1)} %copy-done.5, bf16[8,256]{1,0:T(8,128)(2,1)S(1)} %fusion.40.refs_1_), custom_call_target="tpu_custom_call" | custom-call | tf_op jit(solution)/shard_map/gather_first/pallas_call | solution.py:227
  36.6 1.8 copy-done.17
  38.6 4.2 convolution_convert_fusion.1.refs_0_
  42.8 75.8 %attend_forward_1.1 = (bf16[576,2048]{1,0:T(8,128)(2,1)S(1)}, bf16[768,512]{1,0:T(8,128)(2,1)S(1)}, bf16[192,2048]{1,0:T(8,128)(2,1)S(1)}, f32[3,1,2048]{2,1,0:T...) custom-call(bf16[2304,512]{1,0:T(8,128)(2,1)S(1)} %convolution_convert_fusion.1., ...), custom_call_target="tpu_custom_call" | custom-call | tf_op jit(solution)/shard_map/attend_forward_1/pallas_call | solution.py:670
  120.1 5.8 %multiply_convert_fusion.1 = (bf16[3072,512]{1,0:T(8,128)(2,1)S(1)}, f32[3072,512]{1,0:T(8,128)}) fusion(bf16[768,3072]{1,0:T(8,128)(2,1)S(1)} %get-tuple-element.34, f32[512,768]{0,1:T(8,128)S(1)} %get-tuple-element.84, f32[768]{0:T(1024)S(1)} %reshape.173, f32[512]{0:T(512)S(1)} %fusion.46, f32[512]{0:T(512)S(1)} %broadcast_multiply_fusion.2), kind=kOutput, calls=%fused_computation.19 | convolution fusion | flops 2431647744 | bytes 15735808 | tf_op jit(solution)/shard_map/dot_general | solution.py:937
  126.0 2.7 fusion.62
  129.1 2.1 convolution_convert_fusion.refs_0_
  131.3 41.2 %attend_forward_2.1 = (bf16[576,2048]{1,0:T(8,128)(2,1)S(1)}, bf16[768,512]{1,0:T(8,128)(2,1)S(1)}, bf16[192,2048]{1,0:T(8,128)(2,1)S(1)}, f32[3,1,2048]{2,1,0:T(1,128)S(1)}) custom-call(bf16[2304,512]{1,0:T(8,128)(2,1)S(1)} %convolution_convert_fusion.refs_0_, bf16[576,2048]{1,0:T(8,128)(2,1)S(1)} %get-tuple-element.36.refs_1_), custom_call_target="tpu_custom_call" | custom-call | tf_op jit(solution)/shard_map/attend_forward_2/pallas_call | solution.py:670
  174.7 4.2 multiply_convert_fusion
  178.9 7.8 %fusion.13.refs_17_ = bf16[3072,512]{1,0:T(8,128)(2,1)} fusion(f32[3072,512]{1,0:T(8,128)S(1)} %get-tuple-element.92, bf16[3072,768]{1,0:T(8,128)(2,1)S(1)} %bitcast.98, bf16[1,512,768]{2,1,0:T(8,128)(2,1)S(1)} %copy-done.41), kind=kOutput, calls=%fused_computation.17 | convolution fusion | flops 2447376384 | bytes 14942208 | tf_op jit(solution)/shard_map/dot_general | solution.py:937
  186.7 3.5 fusion.24
  190.3 2.3 copy.49
  192.5 6.4 %multiply_reduce_fusion.2 = (f32[512]{0:T(512)S(1)}, f32[512,768]{0,1:T(8,128)S(1)}) fusion(f32[512,768]{0,1:T(8,128)} %copy-done.24, f32[512]{0:T(512)S(1)} %broadcast_multiply_fusion, f32[768]{0:T(1024)S(1)} %reshape.173, bf16[768,3072]{1,0:T(8,128)(2,1)} %copy-done.16, bf16[3072,512]{1,0:T(8,128)(2,1)} %fusion.13.refs_17_), kind=kOutput, calls=%fused_computation.44 | convolution fusion | flops 2417491456 | bytes 11017216 | tf_op jit(solution)/shard_map/dot_general | solution.py:937
  203.3 2.4 copy.45.refs_9_
  205.7 2.8 convolution_convert_fusion.3.refs_0_
  208.5 60.7 %attend_backward_2.1 = (bf16[2304,512]{1,0:T(8,128)(2,1)}, f32[3,128,2048]{2,1,0:T(8,128)}) custom-call(bf16[768,512]{1,0:T(8,128)(2,1)} %convolution_convert_fusion.3.refs_0_, bf16[576,2048]{1,0:T(8,128)(2,1)} %copy-done, bf16[576,2048]{1,0:T(8,128)(2,1)} %copy-done.2, bf16[192,2048]{1,0:T(8,128)(2,1)} %copy-done.9, f32[3,1,2048]{2,1,0:T(1,128)} %copy-done.15), custom_call_target="tpu_custom_call" | custom-call | tf_op jit(solution)/shard_map/attend_backward_2/pallas_call | solution.py:906
  269.3 4.8 %multiply_reduce_fusion.1 = (f32[512]{0:T(512)S(1)}, f32[512,768]{0,1:T(8,128)S(1)}) fusion(f32[512,768]{0,1:T(8,128)S(1)} %get-tuple-element.88, f32[512]{0:T(512)S(1)} %broadcast_multiply_fusion.1, f32[768]{0:T(1024)S(1)} %copy-done.57, bf16[768,2304]{1,0:T(8,128)(2,1)} %copy-done.17, bf16[2304,512]{1,0:T(8,128)(2,1)} %get-tuple-element.41.refs_20_), kind=kOutput, calls=%fused_computation.42 | convolution fusion | flops 1813511680 | bytes 9051136 | tf_op jit(solution)/shard_map/dot_general | solution.py:937
  274.1 1.9 fusion.55
  280.2 9.2 %fusion.6.refs_16_ = bf16[3072,512]{1,0:T(8,128)(2,1)S(1)} fusion(f32[3072,512]{1,0:T(8,128)} %get-tuple-element.86, bf16[3072,768]{1,0:T(8,128)(2,1)} %get-tuple-element.35, bf16[512,768]{0,1:T(8,128)(2,1)S(1)} %convert_element_type.142), kind=kOutput, calls=%fused_computation.10 | convolution fusion | flops 2447376384 | bytes 14942208 | tf_op jit(solution)/shard_map/dot_general | solution.py:937
  289.5 2.6 multiply_reduce_fusion
  292.2 1.9 fusion.59
  295.8 1.8 fusion.27
  300.4 124.0 %attend_backward_1.1 = (bf16[2304,512]{1,0:T(8,128)(2,1)}, f32[8,256]{1,0:T(8,128)}, f32[96,768]{1,0:T(8,128)}, f32[96,3072]{1,0:T(8,128)}, f32[384,768]{1,0:T(8,128)}, /*index=5*/f32[96,2304]{1,0:T(8,128)}) custom-call(bf16[768,512]{1,0:T(8,128)(2,1)} %convolution_convert_fusion.2.refs_0_, bf16[576,2048]{1,0:T(8,128)(2,1)} %copy-done, ...), custom_call_target="tpu_custom_call" | custom-call | tf_op jit(solution)/shard_map/attend_backward_1/pallas_call | solution.py:906
  424.5 4.0 fusion.23
  (187 shorter events, 30.6 us)
Async XLA Ops:
  3.0 271.1 %copy-start.20 = (bf16[1,512,768]{1,2,0:T(8,128)(2,1)}, bf16[1,512,768]{1,2,0:T(8,128)(2,1)S(1)}, u32[]{:S(2)}) copy-start(bf16[1,512,768]{1,2,0:T(8,128)(2,1)S(1)} %copy.34) | copy-start | bytes 2359300
  3.4 34.9 %copy-start.46 = (f32[512]{0:T(512)}, f32[512]{0:T(512)S(1)}, u32[]{:S(2)}) copy-start(f32[512]{0:T(512)S(1)} %fusion.20) | copy-start | bytes 6148
  4.3 196.1 %copy-start.29 = (bf16[1,512,768]{1,2,0:T(8,128)(2,1)}, bf16[1,512,768]{1,2,0:T(8,128)(2,1)S(1)}, u32[]{:S(2)}) copy-start(bf16[1,512,768]{1,2,0:T(8,128)(2,1)S(1)} %copy.39) | copy-start | bytes 2359300
  38.6 90.3 %copy-start.56 = (f32[768]{0:T(1024)}, f32[768]{0:T(1024)S(1)}, u32[]{:S(2)}) copy-start(f32[768]{0:T(1024)S(1)} %reshape.172) | copy-start | bytes 9220
  118.6 12.6 %copy-start = (bf16[576,2048]{1,0:T(8,128)(2,1)}, bf16[576,2048]{1,0:T(8,128)(2,1)S(1)}, u32[]{:S(2)}) copy-start(bf16[576,2048]{1,0:T(8,128)(2,1)S(1)} %get-tuple-element.36.refs_1_) | copy-start | bytes 7077892
  118.6 53.9 %copy-start.7 = (bf16[768,768]{1,0:T(8,128)(2,1)}, bf16[768,768]{1,0:T(8,128)(2,1)S(1)}, u32[]{:S(2)}) copy-start(bf16[768,768]{1,0:T(8,128)(2,1)S(1)} %get-tuple-element.33) | copy-start | bytes 3538948
  118.7 56.1 %copy-start.16 = (bf16[768,3072]{1,0:T(8,128)(2,1)}, bf16[768,3072]{1,0:T(8,128)(2,1)S(1)}, u32[]{:S(2)}) copy-start(bf16[768,3072]{1,0:T(8,128)(2,1)S(1)} %get-tuple-element.34) | copy-start | bytes 14155780
  119.8 6.1 %copy-start.31 = (f32[512,768]{0,1:T(8,128)}, f32[512,768]{0,1:T(8,128)S(1)}, u32[]{:S(2)}) copy-start(f32[512,768]{0,1:T(8,128)S(1)} %get-tuple-element.84) | copy-start | bytes 4718596
  119.8 6.1 %copy-start.44 = (f32[512]{0:T(512)}, f32[512]{0:T(512)S(1)}, u32[]{:S(2)}) copy-start(f32[512]{0:T(512)S(1)} %broadcast_multiply_fusion.2) | copy-start | bytes 6148
  119.8 6.1 %slice-start.2 = ((s8[4718592]{0:T(1024)(128)(4,1)}), s8[4194304]{0:T(1024)(128)(4,1)S(1)}, s32[]{:S(2)}) async-start(s8[4718592]{0:T(1024)(128)(4,1)} %bitcast.97), calls=%async_computation.2 | async-start | bytes 8388608
  120.1 5.9 %copy-start.48 = (f32[512]{0:T(512)}, f32[512]{0:T(512)S(1)}, u32[]{:S(2)}) copy-start(f32[512]{0:T(512)S(1)} %multiply_reduce_fusion.5) | copy-start | bytes 6148
  120.1 5.9 %copy-start.59 = (f32[512]{0:T(512)}, f32[512]{0:T(512)S(1)}, u32[]{:S(2)}) copy-start(f32[512]{0:T(512)S(1)} %fusion.46) | copy-start | bytes 6148
  120.1 5.9 %slice-start.3 = ((s8[4718592]{0:T(1024)(128)(4,1)}), s8[524288]{0:T(1024)(128)(4,1)S(1)}, s32[]{:S(2)}) async-start(s8[4718592]{0:T(1024)(128)(4,1)} %bitcast.97), calls=%async_computation.3 | async-start | bytes 1048576
  174.5 12.3 %copy-start.24 = (f32[512,768]{0,1:T(8,128)}, f32[512,768]{0,1:T(8,128)S(1)}, u32[]{:S(2)}) copy-start(f32[512,768]{0,1:T(8,128)S(1)} %get-tuple-element.90) | copy-start | bytes 4718596
  178.9 7.8 %copy-start.38 = (bf16[3072,512]{1,0:T(8,128)(2,1)}, bf16[3072,512]{1,0:T(8,128)(2,1)S(1)}, u32[]{:S(2)}) copy-start(bf16[3072,512]{1,0:T(8,128)(2,1)S(1)} %get-tuple-element.91) | copy-start | bytes 9437188
  192.5 6.5 %copy-start.25 = (f32[512,768]{0,1:T(8,128)S(1)}, f32[512,768]{0,1:T(8,128)}, u32[]{:S(2)}) copy-start(f32[512,768]{0,1:T(8,128)} %copy-done.24) | copy-start | bytes 4718596
  208.5 60.7 %copy-start.57 = (f32[768]{0:T(1024)S(1)}, f32[768]{0:T(1024)}, u32[]{:S(2)}) copy-start(f32[768]{0:T(1024)} %copy-done.56) | copy-start | bytes 9220
  278.5 10.9 %slice-start = ((s8[4718592]{0:T(1024)(128)(4,1)}), s8[4194304]{0:T(1024)(128)(4,1)S(1)}, s32[]{:S(2)}) async-start(s8[4718592]{0:T(1024)(128)(4,1)} %bitcast.89), calls=%async_computation | async-start | bytes 8388608
  280.2 9.3 %slice-start.1 = ((s8[4718592]{0:T(1024)(128)(4,1)}), s8[524288]{0:T(1024)(128)(4,1)S(1)}, s32[]{:S(2)}) async-start(s8[4718592]{0:T(1024)(128)(4,1)} %bitcast.89), calls=%async_computation.1 | async-start | bytes 1048576
  280.2 9.3 %copy-start.32 = (f32[512,768]{0,1:T(8,128)S(1)}, f32[512,768]{0,1:T(8,128)}, u32[]{:S(2)}) copy-start(f32[512,768]{0,1:T(8,128)} %copy-done.31) | copy-start | bytes 4718596
  280.2 9.3 %copy-start.45 = (f32[512]{0:T(512)S(1)}, f32[512]{0:T(512)}, u32[]{:S(2)}) copy-start(f32[512]{0:T(512)} %copy-done.44) | copy-start | bytes 6148
  300.4 124.0 %copy-start.19 = (bf16[768,2304]{1,0:T(8,128)(2,1)S(1)}, bf16[768,2304]{1,0:T(8,128)(2,1)}, u32[]{:S(2)}) copy-start(bf16[768,2304]{1,0:T(8,128)(2,1)} %copy-done.17) | copy-start | bytes 10616836
  300.4 124.0 %copy-start.58 = (f32[768]{0:T(1024)S(1)}, f32[768]{0:T(1024)}, u32[]{:S(2)}) copy-start(f32[768]{0:T(1024)} %copy-done.56) | copy-start | bytes 9220
  424.5 5.6 %copy-start.33 = (f32[96,3072]{1,0:T(8,128)S(1)}, f32[96,3072]{1,0:T(8,128)}, u32[]{:S(2)}) copy-start(f32[96,3072]{1,0:T(8,128)} %get-tuple-element.116) | copy-start | bytes 3538948
  (43 other events, 103.2 us)

commit v5 on v4

--- a/solution.py
+++ b/solution.py
@@ -1,4 +1,5 @@
 import functools
+import math
 
 import jax
 import jax.numpy as jnp
@@ -11,31 +12,10 @@
 CHUNK = 768
 EVERY = 3
 SLOTS = 5
+PAIRS = 2
 
 
 epsilon = 1e-05
-
-
-def layer_norm(vector, gain_vec):
-    centre = vector - jnp.mean(vector, axis=-1, keepdims=True)
-    spread = jnp.mean(centre * centre, axis=-1, keepdims=True)
-    return centre * lax.rsqrt(spread + epsilon) * gain_vec
-
-
-def gelu_value(vector):
-    return jax.nn.gelu(vector, approximate=True)
-
-
-def contract_rows(left_side, right_side):
-    return lax.dot_general(
-        left_side, right_side, (((0,), (0,)), ((), ())), preferred_element_type=jnp.float32
-    )
-
-
-def contract_cols(left_side, right_side):
-    return lax.dot_general(
-        left_side, right_side, (((1,), (1,)), ((), ())), preferred_element_type=jnp.float32
-    )
 
 
 def nt(left, right):
@@ -78,20 +58,20 @@
 class Gather:
     def __init__(self, seq, dp, shards, wholes, units, sems):
         self.line = dp // 2
-        self.shards, self.wholes, self.units = shards, wholes, units
-        self.z_send, self.z_recv, self.y_send, self.y_recv, self.c_send, self.c_recv, self.own = sems
+        self.shards, self.wholes, self.units, self.sems = shards, wholes, units, sems
         me = lax.axis_index("seq")
-        self.core = lax.rem(me, 2)
+        self.core, self.chip = lax.rem(me, 2), lax.div(me, 2)
         self.core_peer = {"seq": me + 1 - 2 * self.core}
+        self.x_peer = {"seq": self.core + 2 - 2 * self.chip}
         self.rank = lax.axis_index("dp")
         self.a, self.b = lax.div(self.rank, 2), lax.rem(self.rank, 2)
         self.y_peer = {"dp": self.a * 2 + 1 - self.b}
         self.flying, self.sent = {}, []
 
     @staticmethod
-    def sems(arrays, units, dp):
+    def scratch(arrays, units, dp):
         line, dma = dp // 2, pltpu.SemaphoreType.DMA
-        sizes = (line, line, line, line, 2 * line, 2 * line)
+        sizes = (line, line, line, line, 2 * line, 2 * line, 2 * line, 2 * line, 2 * line, 2 * line)
         return [dma((units, size)) for size in sizes] + [dma((arrays,))]
 
     def z_rank(self, offset):
@@ -101,84 +81,92 @@
         z = [{"dp": self.z_rank(d)} for d in range(1, self.line)]
         return z + [self.y_peer]
 
-    def columns(self, unit):
-        array, row, rows, column, columns = self.units[unit]
+    def shared(self, unit):
+        return sum(self.units[unit][5:]) > 0
+
+    def place(self, unit, first, chip):
+        array, row, rows, column, columns, row_step, column_step = self.units[unit]
         half = columns // 2
-        return pl.ds(pl.multiple_of(column + self.core * half, 128), half)
-
-    def block(self, unit, rank):
-        array, row, rows, column, columns = self.units[unit]
-        first = rank * self.shards[array].shape[0] + row
-        return self.wholes[array].at[pl.ds(pl.multiple_of(first, 8), rows), self.columns(unit)]
-
-    def send(self, key, src, dst, send_sem, recv_sem, device):
-        copy = remote(src, dst, send_sem, recv_sem, device)
+        start = first + row
+        side = column + self.core * half
+        if row_step:
+            start = start + chip * row_step
+        if column_step:
+            side = side + chip * column_step
+        if not isinstance(start, int):
+            start = pl.multiple_of(start, 8)
+        return pl.ds(start, rows), pl.ds(pl.multiple_of(side, 128), half)
+
+    def block(self, unit, rank, chip):
+        array = self.units[unit][0]
+        return self.wholes[array].at[self.place(unit, rank * self.shards[array].shape[0], chip)]
+
+    def send(self, kind, unit, slot, src, dst, device):
+        sems = {"z": 0, "y": 2, "core": 4, "x": 6, "core2": 8}[kind]
+        copy = remote(
+            src, dst, self.sems[sems].at[unit, slot], self.sems[sems + 1].at[unit, slot], device
+        )
         copy.start()
-        self.flying[key] = copy
+        self.flying[kind, unit, slot] = copy
         self.sent.append(copy)
 
     def keep_own(self):
         for array, (shard, whole) in enumerate(zip(self.shards, self.wholes)):
             rows = shard.shape[0]
             copy = pltpu.make_async_copy(
-                shard, whole.at[pl.ds(pl.multiple_of(self.rank * rows, 8), rows)], self.own.at[array]
+                shard,
+                whole.at[pl.ds(pl.multiple_of(self.rank * rows, 8), rows)],
+                self.sems[10].at[array],
             )
             copy.start()
             self.flying["own", array] = copy
 
     def start(self, unit):
-        array, row, rows = self.units[unit][:3]
-        mine = self.shards[array].at[pl.ds(row, rows), self.columns(unit)]
-        there = self.block(unit, self.rank)
+        array = self.units[unit][0]
+        mine = self.shards[array].at[self.place(unit, 0, self.chip)]
+        there = self.block(unit, self.rank, self.chip)
         for d in range(1, self.line):
-            self.send(
-                ("z", unit, d),
-                mine,
-                there,
-                self.z_send.at[unit, d],
-                self.z_recv.at[unit, d],
-                {"dp": self.z_rank(d)},
-            )
-        self.send(
-            ("y", unit, 0), mine, there, self.y_send.at[unit, 0], self.y_recv.at[unit, 0], self.y_peer
-        )
-
-    def to_core(self, unit, slot, rank):
-        block = self.block(unit, rank)
-        self.send(
-            ("core", unit, slot),
-            block,
-            block,
-            self.c_send.at[unit, slot],
-            self.c_recv.at[unit, slot],
-            self.core_peer,
-        )
+            self.send("z", unit, d, mine, there, {"dp": self.z_rank(d)})
+        self.send("y", unit, 0, mine, there, self.y_peer)
+
+    def spread(self, unit, slot, rank):
+        block = self.block(unit, rank, self.chip)
+        if self.shared(unit):
+            self.send("x", unit, slot, block, block, self.x_peer)
+        self.send("core", unit, slot, block, block, self.core_peer)
 
     def forward_z(self, unit):
         for d in range(1, self.line):
             self.flying["z", unit, d].wait_recv()
             rank = self.z_rank(self.line - d)
-            block = self.block(unit, rank)
-            self.send(
-                ("y", unit, d),
-                block,
-                block,
-                self.y_send.at[unit, d],
-                self.y_recv.at[unit, d],
-                self.y_peer,
-            )
-            self.to_core(unit, d, rank)
+            block = self.block(unit, rank, self.chip)
+            self.send("y", unit, d, block, block, self.y_peer)
+            self.spread(unit, d, rank)
+
+    def y_rank(self, d):
+        return lax.rem(self.a + self.line - d, self.line) * 2 + 1 - self.b
 
     def forward_y(self, unit):
         for d in range(self.line):
             self.flying["y", unit, d].wait_recv()
-            rank = lax.rem(self.a + self.line - d, self.line) * 2 + 1 - self.b
-            self.to_core(unit, self.line + d, rank)
+            self.spread(unit, self.line + d, self.y_rank(d))
+
+    def forward_x(self, unit):
+        if not self.shared(unit):
+            return
+        for slot in range(1, 2 * self.line):
+            self.flying["x", unit, slot].wait_recv()
+            d = slot % self.line
+            rank = self.y_rank(d) if slot >= self.line else self.z_rank(self.line - d)
+            block = self.block(unit, rank, 1 - self.chip)
+            self.send("core2", unit, slot, block, block, self.core_peer)
 
     def finish(self):
         for unit in range(len(self.units)):
             for slot in range(1, 2 * self.line):
                 self.flying["core", unit, slot].wait_recv()
+                if self.shared(unit):
+                    self.flying["core2", unit, slot].wait_recv()
         for array in range(len(self.shards)):
             self.flying["own", array].wait()
         for copy in self.sent:
@@ -186,28 +174,37 @@
 
     def steps(self):
         count, calls = len(self.units), []
-        for step in range(count + 1):
-            if step < count:
-                calls.append(functools.partial(self.forward_z, step))
-            if step > 0:
-                calls.append(functools.partial(self.forward_y, step - 1))
+        for step in range(count + 2):
+            for call, unit in (
+                (self.forward_z, step),
+                (self.forward_y, step - 1),
+                (self.forward_x, step - 2),
+            ):
+                if 0 <= unit < count:
+                    calls.append(functools.partial(call, unit))
         return calls
 
 
-def cut(shapes, rows, size):
-    units = []
-    for array, shape in enumerate(shapes):
-        high, wide = min(shape[0], rows), min(shape[1], size)
-        for row in range(0, shape[0], high):
-            for column in range(0, shape[1], wide):
-                units.append((array, row, high, column, wide))
-    return units
+def first_units(shards):
+    (rows, wide), small = shards[0].shape, shards[1].shape
+    units = [(0, 0, rows, 0, CHUNK, 0, CHUNK)]
+    units += [(0, 0, rows, column, CHUNK, 0, 0) for column in range(2 * CHUNK, wide, CHUNK)]
+    return units + [(1, 0, small[0], 0, small[1], 0, 0)]
+
+
+def later_units(shards):
+    (rows, width), (_, up_wide), (down_rows, _) = [shard.shape for shard in shards]
+    ups = [(1, 0, rows, column, CHUNK, 0, 0) for column in range(0, up_wide, CHUNK)]
+    shared = 2 * PAIRS * rows
+    pairs = [(2, row, rows, 0, width, rows, 0) for row in range(0, shared, 2 * rows)]
+    downs = [(2, row, rows, 0, width, 0, 0) for row in range(shared, down_rows, rows)]
+    return [(0, 0, rows, 0, width, 0, 0)] + ups[:1] + pairs[:1] + ups[1:3] + pairs[1:] + ups[3:] + downs
 
 
 def gather_kernel(seq, dp, units, arrays, *refs):
     shards, wholes, sems = refs[:arrays], refs[arrays : 2 * arrays], refs[2 * arrays :]
     gather = Gather(seq, dp, shards, wholes, units, sems)
-    greet(gather.peers() + [gather.core_peer])
+    greet(gather.peers() + [gather.core_peer, gather.x_peer])
     for unit in range(len(units)):
         gather.start(unit)
     gather.keep_own()
@@ -222,14 +219,14 @@
 
 def gather_now(seq, dp, shards):
     arrays = len(shards)
-    units = cut([shard.shape for shard in shards], shards[0].shape[0], CHUNK)
+    units = first_units(shards)
     hbm = pl.BlockSpec(memory_space=pl.ANY)
     return pl.pallas_call(
         functools.partial(gather_kernel, seq, dp, units, arrays),
         out_shape=tuple(whole_shape(shard, dp) for shard in shards),
         in_specs=[hbm] * arrays,
         out_specs=(hbm,) * arrays,
-        scratch_shapes=Gather.sems(arrays, len(units), dp),
+        scratch_shapes=Gather.scratch(arrays, len(units), dp),
         compiler_params=pltpu.CompilerParams(
             collective_id=0, has_side_effects=True, vmem_limit_bytes=4 << 20
         ),
@@ -398,13 +395,12 @@
             normed,
             self.second_packed,
         ) = refs
-        self.stream, self.keep_rows, self.keep_left, self.result, self.sems = scratch
+        self.stream, self.keep, self.sems = scratch
         self.work, self.d_packed = work, d_packed
         self.width, self.both = self.stream.shape[1:]
         self.tokens = self.both // 2
         self.mixed, self.active, self.d_hidden = mixed, active, d_hidden
-        self.kept = [(middle, self.keep_rows.at[0]), (upstream, self.keep_rows.at[1])]
-        self.kept += [(normed_b, self.keep_left.at[0]), (normed, self.keep_left.at[1])]
+        self.kept = (middle, normed_b, upstream, normed)
         self.flying = {}
 
     @staticmethod
@@ -412,9 +408,7 @@
         b = jnp.bfloat16
         return [
             pltpu.VMEM((2, width, 2 * tokens), b),
-            pltpu.VMEM((2, 2 * tokens, width), b),
-            pltpu.VMEM((2, width, 2 * tokens), b),
-            pltpu.VMEM((width, width), jnp.float32),
+            pltpu.VMEM((4, width, 2 * tokens), b),
             pltpu.SemaphoreType.DMA((32, 2)),
         ]
 
@@ -430,11 +424,16 @@
     def begin(self):
         self.copy("small", 30, 0, self.small, self.work.small)
         self.fetch(1)
-        for index, (pair, place) in enumerate(self.kept):
+        for index in (0, 2, 1, 3):
             for side in range(2):
-                span = pl.ds(side * self.tokens, self.tokens)
-                where = place.at[span] if index < 2 else place.at[:, span]
-                self.copy(("kept", index), 20 + index, side, pair[side], where)
+                lanes = pl.ds(side * self.tokens, self.tokens)
+                self.copy(
+                    ("kept", index),
+                    20 + index,
+                    side,
+                    self.kept[index][side],
+                    self.keep.at[index, :, lanes],
+                )
         self.fetch(2)
 
     def kind(self, unit):
@@ -489,47 +488,60 @@
             return
         array, row, column = self.kind(unit)
         slot = unit % 2
-        kept = {1: 0, 3: 1, 2: 2, 4: 3}[array]
+        kept = array - 1
         self.wait(("kept", kept))
         self.wait(unit)
         if array == 4:
             self.stream[slot, :, : self.tokens] = self.d_packed[
                 column * self.width : (column + 1) * self.width, :
             ]
-        step = self.width // 3
-        for part in range(3):
-            span = slice(part * step, (part + 1) * step)
-            if kept < 2:
-                self.result[span, :] = nn(self.stream[slot, span, :], self.keep_rows[kept])
-            else:
-                self.result[span, :] = nt(self.keep_left[kept - 2, span, :], self.stream[slot])
         work.free(unit - SLOTS)
         rows = work.units[unit][1]
-        for rank in range(work.dp):
-            work.terms[(unit - 1) % SLOTS, rank] = self.result[
-                rank * rows : (rank + 1) * rows, :
-            ].astype(jnp.bfloat16)
+        ranks = work.dp // 2
+        for part in range(2):
+            span = slice(part * ranks * rows, (part + 1) * ranks * rows)
+            if array in (1, 3):
+                product = nt(self.stream[slot, span, :], self.keep[kept])
+            else:
+                product = nt(self.keep[kept, span, :], self.stream[slot])
+            for rank in range(ranks):
+                work.terms[(unit - 1) % SLOTS, part * ranks + rank] = product[
+                    rank * rows : (rank + 1) * rows, :
+                ].astype(jnp.bfloat16)
         work.start(unit)
         self.fetch(unit + 2)
 
 
-def background_order(work, products):
-    count = len(work.units)
-    stages = (
-        (3, products.make),
-        (2, work.chip_sum),
-        (0, work.y_sum),
-        (-1, work.z_sum),
-        (-2, work.x_sum),
-        (-3, work.finish),
-    )
-    order = []
-    for step in range(-3, count + 3):
-        calls = [
-            functools.partial(call, step + ahead) for ahead, call in stages if 0 <= step + ahead < count
-        ]
-        order.append(calls)
-    return order
+class Pipeline:
+    def __init__(self, work, products):
+        self.calls = (
+            products.make,
+            work.chip_sum,
+            work.y_sum,
+            work.z_sum,
+            work.x_sum,
+            work.finish,
+        )
+        self.lags = (0, 1, 2, 1, 1, 1)
+        self.done = [0] * len(self.calls)
+
+    def tick(self, limit):
+        made = self.done[0]
+        if made < limit and made - self.done[3] < SLOTS:
+            self.calls[0](made)
+            self.done[0] += 1
+        full = self.done[0] == limit
+        for stage in range(1, len(self.calls)):
+            now, ahead = self.done[stage], self.done[stage - 1]
+            ready = ahead - now > (0 if full else self.lags[stage])
+            full = full and ahead == limit
+            if ready:
+                self.calls[stage](now)
+                self.done[stage] += 1
+
+    def run_out(self, limit):
+        while self.done[-1] < limit:
+            self.tick(limit)
 
 
 def causal_mask(size):
@@ -629,7 +641,7 @@
                 total[:HEAD_DIM] / row_sum
             ).astype(jnp.bfloat16)
             totals_out[h, :, i * tokens : (i + 1) * tokens] = peak + jnp.log(row_sum)
-            if steps and i % 2 == 1:
+            if steps:
                 steps.pop(0)()
 
         mine = pl.ds(pl.multiple_of((me * heads + h) * HEAD_DIM, HEAD_DIM), HEAD_DIM)
@@ -662,7 +674,7 @@
     width, tokens = packed.shape
     length = tokens * seq
     sets, arrays = 1 + len(earlier), len(shards)
-    units = cut([shard.shape for shard in shards], shards[0].shape[0], CHUNK) if arrays else []
+    units = later_units(shards) if arrays else []
     rows = heads * 3 * HEAD_DIM
     vmem = pl.BlockSpec(memory_space=pltpu.VMEM)
     hbm = pl.BlockSpec(memory_space=pl.ANY)
@@ -689,7 +701,7 @@
             dma((heads, seq)),
             dma((heads, seq)),
         ]
-        + (Gather.sems(arrays, len(units), dp) if units else []),
+        + (Gather.scratch(arrays, len(units), dp) if units else []),
         compiler_params=pltpu.CompilerParams(
             collective_id=call_id, has_side_effects=True, vmem_limit_bytes=40 << 20
         ),
@@ -720,7 +732,7 @@
     in_send, in_recv, out_send, out_recv, out_sem = take(5)
     if units:
         carry_s, carry_sem = take(2)
-        product_scratch = take(5)
+        product_scratch = take(3)
         work = Scatter(seq, dp, units, grads_out, refs)
         products = Products([small] + pairs + [second_packed], product_scratch, work, d_packed_in)
 
@@ -745,21 +757,14 @@
             )
             copy.start()
             copies[h, d] = copy
-    steps = []
     if units:
         products.begin()
-        steps = background_order(work, products)
+        pipeline = Pipeline(work, products)
         early = [unit[0] for unit in units].index(4)
-        later = steps[early:]
-        steps = steps[:early]
     for h in range(heads):
         arrived[h * HEAD_DIM : (h + 1) * HEAD_DIM, own_lanes] = d_mixed[
             pl.ds(pl.multiple_of((me * heads + h) * HEAD_DIM, HEAD_DIM), HEAD_DIM), :
         ]
-
-    def run(calls):
-        for call in calls:
-            call()
 
     def outgoing(h, rank, send_slot):
         return remote(
@@ -772,8 +777,9 @@
             {"seq": rank},
         )
 
-    if steps:
-        run(steps.pop(0))
+    if units:
+        pipeline.tick(early)
+        pipeline.tick(early)
     mask = causal_mask(tokens)
     hook = 0
     for h in range(heads):
@@ -826,8 +832,8 @@
                     d_query = part if d_query is None else d_query + part
                 dq_s[:, span] = d_query
                 hook += 1
-                if steps and hook % EVERY == 0:
-                    run(steps.pop(0))
+                if units and hook % EVERY == 0:
+                    pipeline.tick(early)
             local_grad[c0 : c0 + HEAD_DIM, keys] = dq_s[:, keys].astype(jnp.bfloat16)
             local_grad[c0 + HEAD_DIM : c0 + group, keys] = dkv_s[sets - 1, :, keys].astype(
                 jnp.bfloat16
@@ -846,8 +852,6 @@
         d_packed_in[pl.ds(pl.multiple_of((me * heads + h) * group, group), group)] = local_grad[
             c0 : c0 + group, own_lanes
         ]
-    for calls in steps:
-        run(calls)
     for h in range(heads):
         for peer in peers:
             remote(
@@ -860,8 +864,7 @@
     finished = pltpu.make_async_copy(d_packed_in, d_packed_out, out_sem.at[0])
     finished.start()
     if units:
-        for calls in later:
-            run(calls)
+        pipeline.run_out(len(units))
         work.drain()
     for copy in copies.values():
         copy.wait_send()
@@ -933,6 +936,156 @@
     )(d_mixed, *packs, own, totals, *extra)
 
 
+def column(row):
+    return jnp.broadcast_to(row, (8, row.shape[1])).T[:, :1]
+
+
+def norm_unit(rows):
+    centre = rows - jnp.mean(rows, axis=0, keepdims=True)
+    inverse = lax.rsqrt(jnp.mean(centre * centre, axis=0, keepdims=True) + epsilon)
+    return centre * inverse, inverse
+
+
+def norm_backward(unit, inverse, gain, grad):
+    grad = grad * gain
+    share = jnp.mean(grad * unit, axis=0, keepdims=True)
+    return inverse * (grad - jnp.mean(grad, axis=0, keepdims=True) - unit * share)
+
+
+def gelu_slope(hidden):
+    root = (2.0 / math.pi) ** 0.5
+    square = hidden * hidden
+    bend = jnp.tanh(root * hidden * (1.0 + 0.044715 * square))
+    inner = (0.5 * root) * hidden * (1.0 + 3 * 0.044715 * square)
+    return 0.5 * (1.0 + bend) + inner * (1.0 - bend * bend)
+
+
+def dense_kernel(first, mlp, chunks, *refs):
+    refs = list(refs)
+
+    def take(count):
+        taken = refs[:count]
+        del refs[:count]
+        return taken
+
+    both = first * mlp
+    count = 5 * first + (1 - first) + 6 * mlp + both
+    sources = take(count)
+    results = take(1 - mlp + mlp * 5 + both * 4)
+    places = take(count)
+    sems, out_sems = take(2)
+    fetched = [
+        pltpu.make_async_copy(source, place, sems.at[index])
+        for index, (source, place) in enumerate(zip(sources, places))
+    ]
+    for copy in fetched:
+        copy.start()
+
+    def get(index):
+        fetched[index].wait()
+        return places[index]
+
+    sent = []
+
+    def put(place, result):
+        copy = pltpu.make_async_copy(place, result, out_sems.at[len(sent)])
+        copy.start()
+        sent.append(copy)
+
+    if first:
+        grad = nn(get(1)[...], get(0)[...])
+        unit, inverse = norm_unit(get(2)[...].T)
+        gain_a = column(get(4)[...])
+        upstream = get(3)[...] + norm_backward(unit, inverse, gain_a, grad)
+    else:
+        upstream = get(0)[...].astype(jnp.float32)
+    if not mlp:
+        (out_s,) = refs
+        out_s[...] = upstream.T
+        put(out_s, results[0])
+    else:
+        base = 5 * first + (1 - first)
+        middle, hidden, down_w, up_w, out_w, gain = range(base, base + 6)
+        hidden_s, grad_s, middle_s, mixed_s, normed_s, up_s, rounded_s = refs[:7]
+        up_s[...] = upstream
+        rounded_s[...] = upstream.astype(jnp.bfloat16)
+        if first:
+            first_s, second_s = refs[7:]
+            rounded_out, sum_out, first_out, second_out = results[5:]
+            put(rounded_s, rounded_out)
+            sum_out[...] = jnp.sum(upstream, axis=1, keepdims=True)
+            second_s[...] = (unit * gain_a).astype(jnp.bfloat16)
+            put(second_s, second_out)
+        size = places[hidden].shape[0] // chunks
+        get(down_w)
+        get(hidden)
+        total = None
+        for chunk in range(chunks):
+            span = slice(chunk * size, (chunk + 1) * size)
+            d_active = nn(places[down_w][span, :], rounded_s[...])
+            hidden_s[span, :] = (d_active * gelu_slope(places[hidden][span, :])).astype(jnp.bfloat16)
+            put(hidden_s.at[span], results[0].at[span])
+            if chunk == 0:
+                get(up_w)
+            part = nn(places[up_w][:, span], hidden_s[span, :])
+            total = part if total is None else total + part
+        unit, inverse = norm_unit(get(middle)[...].T)
+        gain_b = column(get(gain)[...])
+        d_middle = up_s[...] + norm_backward(unit, inverse, gain_b, total)
+        grad_s[...] = d_middle
+        middle_s[...] = d_middle.astype(jnp.bfloat16)
+        normed_s[...] = (unit * gain_b).astype(jnp.bfloat16)
+        put(grad_s, results[1])
+        put(middle_s, results[2])
+        put(normed_s, results[4])
+        mixed_s[...] = nn(get(out_w)[...], middle_s[...]).astype(jnp.bfloat16)
+        put(mixed_s, results[3])
+        if first:
+            first_s[...] = (norm_unit(get(base + 6)[...].T)[0] * gain_a).astype(jnp.bfloat16)
+            put(first_s, first_out)
+    for copy in sent:
+        copy.wait()
+
+
+def dense_backward(before, after):
+    first, mlp = int(len(before) > 1), int(len(after) > 0)
+    args = list(before) + list(after)
+    width, tokens = (before[3] if first else before[0]).shape
+    hbm = pl.BlockSpec(memory_space=pl.ANY)
+    b, f32 = jnp.bfloat16, jnp.float32
+    chunks, outs, specs, more = 1, [jax.ShapeDtypeStruct((tokens, width), f32)], [hbm], []
+    flops = 6 * width * width * tokens * first
+    if mlp:
+        ff = after[1].shape[0]
+        chunks = ff // width
+        flops += 2 * tokens * width * (2 * ff + width)
+        flat = (width, tokens)
+        shapes = [((ff, tokens), b), (flat, f32), (flat, b), (flat, b), (flat, b)]
+        more = [pltpu.VMEM(shape, kind) for shape, kind in shapes]
+        more += [pltpu.VMEM(flat, f32), pltpu.VMEM(flat, b)]
+        outs = [jax.ShapeDtypeStruct(shape, kind) for shape, kind in shapes]
+        specs = [hbm] * 5
+        if first:
+            more += [pltpu.VMEM(flat, b)] * 2
+            outs += [jax.ShapeDtypeStruct(flat, b), jax.ShapeDtypeStruct((width, 1), f32)]
+            outs += [jax.ShapeDtypeStruct(flat, b)] * 2
+            specs += [hbm, pl.BlockSpec(memory_space=pltpu.VMEM), hbm, hbm]
+    else:
+        more = [pltpu.VMEM((tokens, width), f32)]
+    return pl.pallas_call(
+        functools.partial(dense_kernel, first, mlp, chunks),
+        out_shape=tuple(outs),
+        in_specs=[hbm] * len(args),
+        out_specs=tuple(specs),
+        scratch_shapes=[pltpu.VMEM(arg.shape, arg.dtype) for arg in args]
+        + [pltpu.SemaphoreType.DMA((len(args),)), pltpu.SemaphoreType.DMA((16,))]
+        + more,
+        compiler_params=pltpu.CompilerParams(vmem_limit_bytes=58 << 20),
+        cost_estimate=pl.CostEstimate(flops=flops, bytes_accessed=24 << 20, transcendentals=0),
+        name=f"dense_backward_{first}{mlp}",
+    )(*args)
+
+
 def dots(left, right, left_side, right_side):
     return lax.dot_general(
         left,
@@ -942,54 +1095,48 @@
     )
 
 
+def norm_rows(rows, gain):
+    centre = rows - jnp.mean(rows, axis=1, keepdims=True)
+    spread = jnp.mean(centre * centre, axis=1, keepdims=True)
+    return (centre * lax.rsqrt(spread + epsilon) * gain).astype(jnp.bfloat16)
+
+
 def block_forward(sizes, call_id, stream, qkv_w, gains, earlier, weights, shards):
     seq, dp, heads = sizes
-    normed = layer_norm(stream, gains[0]).astype(jnp.bfloat16)
+    normed = norm_rows(stream, gains[0])
     packed = dots(qkv_w, normed, 0, 1).astype(jnp.bfloat16)
     (head_rows, mixed, own, totals), gathered = attend_forward(
         seq, dp, heads, packed, earlier, shards, call_id
     )
     out_w, up_w, down_w = weights or gathered
     middle = stream + dots(mixed, out_w, 0, 0)
-    normed_b = layer_norm(middle, gains[1]).astype(jnp.bfloat16)
+    normed_b = norm_rows(middle, gains[1])
     hidden = dots(up_w, normed_b, 0, 1)
-    active = gelu_value(hidden).astype(jnp.bfloat16)
+    active = jax.nn.gelu(hidden, approximate=True).astype(jnp.bfloat16)
     result = middle + dots(active, down_w, 0, 0)
-    stored = (
-        stream,
-        normed.T,
-        earlier + [head_rows],
-        own,
-        totals,
-        mixed,
-        middle,
-        normed_b.T,
-        hidden,
-        active,
-    )
+    packs = earlier + [head_rows]
+    stored = (stream, packs, own, totals, mixed, middle, hidden, active)
     return result, stored, (out_w, up_w, down_w)
 
 
-def block_backward(sizes, call_id, upstream, stored, qkv_w, gains, weights, second):
+def block_backward(sizes, call_id, before, stored, gains, weights, second):
     seq, dp, heads = sizes
     out_w, up_w, down_w = weights
-    stream, normed, packs, own, totals, mixed, middle, normed_b, hidden, active = stored
-    out_bf = upstream.astype(jnp.bfloat16)
-    d_active = dots(down_w, out_bf, 1, 1)
-    d_hidden = jax.vjp(gelu_value, hidden)[1](d_active)[0].astype(jnp.bfloat16)
-    d_normed_b = dots(d_hidden, up_w, 0, 1)
-    d_middle_norm = jax.vjp(layer_norm, middle, gains[1])[1](d_normed_b)[0]
-    d_middle = upstream + d_middle_norm
-    middle_bf = d_middle.astype(jnp.bfloat16)
-    d_mixed = dots(out_w, middle_bf, 1, 1).astype(jnp.bfloat16)
+    stream, packs, own, totals, mixed, middle, hidden, active = stored
+    after = (middle, hidden, down_w, up_w, out_w, gains[1])
+    done = dense_backward(before, after if second is None else after + (stream,))
+    d_hidden, d_middle, middle_bf, d_mixed, normed_b = done[:5]
     width, tokens = d_mixed.shape
     rows = width // dp
     active = active.reshape(dp, active.shape[0] // width, rows, tokens)
-    factors = (mixed, middle_bf, active, out_bf, normed_b, d_hidden, normed)
+    upstream = before[0] if second is None else done[5]
+    factors = [mixed, middle_bf, active, upstream, normed_b, d_hidden]
     extra, units = [], []
     if second is not None:
-        passed, small, second_factors, second_packed = second
-        extra = [passed, small]
+        passed, second_factors, second_packed = second
+        embed = done[6].astype(jnp.bfloat16).reshape(dp, 1, rows)
+        factors, second_factors = factors + [done[7]], second_factors + [done[8]]
+        extra = [passed, jnp.pad(embed, ((0, 0), (0, 7), (0, 256 - rows)))]
         for pair in zip(factors, second_factors):
             extra += pair
         extra.append(second_packed)
@@ -1000,10 +1147,7 @@
         units += [(2, rows, width, 0, column) for column in range(0, ff, width)]
         units += [(4, rows, width, 0, column) for column in range(0, 3 * width, width)]
     outs = attend_backward(seq, dp, heads, d_mixed, packs, own, totals, extra, units, call_id)
-    d_packed = outs[0]
-    d_normed = dots(d_packed, qkv_w, 0, 1)
-    d_stream_norm = jax.vjp(layer_norm, stream, gains[0])[1](d_normed)[0]
-    return d_middle + d_stream_norm, factors, outs
+    return (stream, d_middle), factors, outs
 
 
 def local(
@@ -1033,8 +1177,8 @@
     )
     qkv_w, small = gather_now(seq, dp, [qkv_weight, small])
     small = small.reshape(dp, 8, 256)
-    gains = [small[:, row, :share].reshape(-1).astype(jnp.float32) for row in (0, 1)]
-    embedding = small[:, 0, 128 : 128 + share].reshape(-1).astype(jnp.float32)
+    gains = [small[:, row, :share].reshape(1, -1).astype(jnp.float32) for row in (0, 1)]
+    embedding = small[:, 0, 128 : 128 + share].reshape(1, -1).astype(jnp.float32)
     heads = qkv_weight.shape[1] // (3 * HEAD_DIM * seq)
     sizes = (seq, dp, heads)
     first_out, first_kept, weights = block_forward(
@@ -1048,17 +1192,17 @@
         [out_weight, up_weight, down_weight],
     )
     second_out, second_kept, weights = block_forward(
-        sizes, 2, first_out + embedding, qkv_w, gains, [first_kept[2][0]], weights, []
+        sizes, 2, first_out + embedding, qkv_w, gains, [first_kept[1][0]], weights, []
     )
-    d_second, factors, outs = block_backward(
-        sizes, 3, cotangent[0].astype(jnp.float32), second_kept, qkv_w, gains, weights, None
+    (stream, d_middle), factors, outs = block_backward(
+        sizes, 3, (cotangent[0].T,), second_kept, gains, weights, None
     )
-    embed = jnp.sum(d_second, axis=0).astype(jnp.bfloat16).reshape(dp, 1, share)
-    embed = jnp.pad(embed, ((0, 0), (0, 7), (0, 256 - share)))
-    second = (outs[1], embed, factors, outs[0])
-    d_first, factors, outs = block_backward(
-        sizes, 4, d_second, first_kept, qkv_w, gains, weights, second
+    second = (outs[1], factors, outs[0])
+    before = (outs[0], qkv_w, stream, d_middle, gains[0])
+    (stream, d_middle), factors, outs = block_backward(
+        sizes, 4, before, first_kept, gains, weights, second
     )
+    d_first = dense_backward((outs[0], qkv_w, stream, d_middle, gains[0]), ())[0]
     packed, small, out_grad, up_grad, down_grad, qkv_grad = outs
     f32 = jnp.float32
     gain_a = jnp.sum(qkv_weight.astype(f32) * qkv_grad, axis=1) / norm_gain.astype(f32)

time: 446 us -> 423 us (0.948); the launches traced: 438 us -> 426 us
  Pallas kernels: 334 us -> 378 us
  matrix products: 63.5 us -> 25.4 us
  local copies, waits for them, and re-layouts: 23.7 us -> 11.7 us
  other arithmetic: 15.6 us -> 9.14 us
    pallas_call x0 -> x3, Pallas kernels: none -> 46.1 us  [dense_backward(): pl.pallas_call(functools.partial(dense_kernel, first, mlp, chunks), out_s...]
    dot_general x16 -> x8, matrix products: 63.5 us -> 25.4 us  [dots(): lax.dot_general(left, right, (((left_side,), (right_side,)), ((), ())), p...]
    unnamed x142 -> x81, local copies, waits for them, and re-layouts: 16.6 us -> 7.45 us
    pallas_call x2, Pallas kernels: 117 us -> 123 us  [attend_forward(): pl.pallas_call(functools.partial(forward_kernel, seq, dp, sets, units, ar...]
    pallas_call x1, Pallas kernels: 32.2 us -> 27.5 us  [gather_now(): pl.pallas_call(functools.partial(gather_kernel, seq, dp, units, arrays),...]
where the time goes in v5:
time: 423 us; the launch traced here: 426 us
  Pallas kernels  378 us (89%)
  matrix products  25.4 us (6%)
  local copies, waits for them, and re-layouts  11.7 us (3%)
  other arithmetic  9.14 us (2%)
    pallas_call x2, Pallas kernels, attend_backward(): pl.pallas_call(functools.partial(backward_kernel, seq, dp, sets, units, h...  182 us
    pallas_call x2, Pallas kernels, attend_forward(): pl.pallas_call(functools.partial(forward_kernel, seq, dp, sets, units, ar...  123 us
    pallas_call x3, Pallas kernels, dense_backward(): pl.pallas_call(functools.partial(dense_kernel, first, mlp, chunks), out_s...  46.1 us
    pallas_call x1, Pallas kernels, gather_now(): pl.pallas_call(functools.partial(gather_kernel, seq, dp, units, arrays),...  27.5 us
    dot_general x8, matrix products, dots(): lax.dot_general(left, right, (((left_side,), (right_side,)), ((), ())), p...  25.4 us

profile of v5, /device:TPU:0, one launch (start us, length us, event | category | flops | bytes accessed | tf_op | source)
XLA Modules:
  0.0 425.8 jit_solution(7696668938222122437)
XLA Ops:
  0.8 1.4 convert_reduce_fusion
  2.2 1.5 multiply_reduce_fusion.3
  4.4 1.2 copy.23
  5.5 1.3 convert_bitcast_fusion.refs_11_.refs_2_
  6.8 27.5 %gather_first.1 = (bf16[768,2304]{1,0:T(8,128)(2,1)S(1)}, bf16[64,256]{1,0:T(8,128)(2,1)S(1)}) custom-call(bf16[96,2304]{1,0:T(8,128)(2,1)S(1)} %copy-done.9, bf16[8,256]{1,0:T(8,128)(2,1)S(1)} %fusion.40.refs_1_), custom_call_target="tpu_custom_call" | custom-call | tf_op jit(solution)/shard_map/gather_first/pallas_call | solution.py:224
  37.4 3.5 convolution_convert_fusion.1.refs_0_
  40.9 82.2 %attend_forward_1.1 = (bf16[576,2048]{1,0:T(8,128)(2,1)S(1)}, bf16[768,512]{1,0:T(8,128)(2,1)S(1)}, bf16[192,2048]{1,0:T(8,128)(2,1)S(1)}, f32[3,1,2048]{2,1,0:T...) custom-call(bf16[2304,512]{1,0:T(8,128)(2,1)S(1)} %convolution_convert_fusion.1., ...), custom_call_target="tpu_custom_call" | custom-call | tf_op jit(solution)/shard_map/attend_forward_1/pallas_call | solution.py:682
  124.7 0.9 fusion.44
  125.9 5.8 %fusion.7 = (bf16[3072,512]{1,0:T(8,128)(2,1)S(1)}, f32[3072,512]{1,0:T(8,128)}) fusion(bf16[768,3072]{1,0:T(8,128)(2,1)S(1)} %get-tuple-element.48.refs_4_.refs_8_, f32[512,768]{1,0:T(8,128)S(1)} %get-tuple-element.82.refs_5_, f32[768]{0:T(1024)S(1)} %reshape.139, f32[512]{0:T(512)S(1)} %add_rsqrt_fusion.2, f32[512]{0:T(512)S(1)} %broadcast_multiply_fusion.2), kind=kOutput, calls=%fused_computation.9 | convolution fusion | flops 2431647744 | bytes 15735808 | tf_op jit(solution)/shard_map/dot_general | solution.py:1090
  131.8 2.7 fusion.45
  134.9 2.2 convolution_convert_fusion.refs_0_
  137.1 40.3 %attend_forward_2.1 = (bf16[576,2048]{1,0:T(8,128)(2,1)S(1)}, bf16[768,512]{1,0:T(8,128)(2,1)S(1)}, bf16[192,2048]{1,0:T(8,128)(2,1)S(1)}, f32[3,1,2048]{2,1,0:T(1,128)S(1)}) custom-call(bf16[2304,512]{1,0:T(8,128)(2,1)S(1)} %convolution_convert_fusion.refs_0_, bf16[576,2048]{1,0:T(8,128)(2,1)S(1)} %get-tuple-element.50.refs_1_), custom_call_target="tpu_custom_call" | custom-call | tf_op jit(solution)/shard_map/attend_forward_2/pallas_call | solution.py:682
  179.7 5.8 %fusion.15 = (bf16[3072,512]{1,0:T(8,128)(2,1)S(1)}, f32[3072,512]{1,0:T(8,128)}) fusion(bf16[768,3072]{1,0:T(8,128)(2,1)S(1)} %get-tuple-element.48.refs_4_.refs_8_, f32[512,768]{1,0:T(8,128)S(1)} %get-tuple-element.88.refs_1_, f32[512]{0:T(512)S(1)} %add_rsqrt_fusion, f32[512]{0:T(512)S(1)} %broadcast_multiply_fusion, f32[768]{0:T(1024)S(1)} %reshape.139), kind=kOutput, calls=%fused_computation.17 | convolution fusion | flops 2431647744 | bytes 15735808 | tf_op jit(solution)/shard_map/dot_general | solution.py:1090
  185.5 3.5 fusion.16
  189.0 16.7 %dense_backward_01.1 = (bf16[3072,512]{1,0:T(8,128)(2,1)}, f32[768,512]{1,0:T(8,128)}, bf16[768,512]{1,0:T(8,128)(2,1)}, bf16[768,512]{1,0:T(8,128)(2,1)}, bf16[768,512]{1,0:T(8,128)(2,1)}) custom-call(bf16[768,512]{1,0:T(8,128)(2,1)} %bitcast.49, f32[512,768]{1,0:T(8,128)} %copy-done.22, f32[3072,512]{1,0:T(8,128)} %get-tuple-element.90.refs_2_, ...), custom_call_target="tpu_custom_call" | custom-call | flops 5435817984 | bytes 25165824 | tf_op jit(solution)/shard_map/dense_backward_01/pallas_call | solution.py:1075
  205.7 60.8 %attend_backward_2.1 = (bf16[2304,512]{1,0:T(8,128)(2,1)}, f32[3,128,2048]{2,1,0:T(8,128)}) custom-call(bf16[768,512]{1,0:T(8,128)(2,1)} %get-tuple-element.52.refs_0_, bf16[576,2048]{1,0:T(8,128)(2,1)} %copy-done, bf16[576,2048]{1,0:T(8,128)(2,1)} %copy-done.6, bf16[192,2048]{1,0:T(8,128)(2,1)} %copy-done.11, f32[3,1,2048]{2,1,0:T(1,128)} %copy-done.17), custom_call_target="tpu_custom_call" | custom-call | tf_op jit(solution)/shard_map/attend_backward_2/pallas_call | solution.py:909
  266.5 21.0 %dense_backward_11.1 = (bf16[3072,512]{1,0:T(8,128)(2,1)}, f32[768,512]{1,0:T(8,128)}, bf16[768,512]{1,0:T(8,128)(2,1)}, bf16[768,512]{1,0:T(8,128)(2,1)}, bf16[...) custom-call(bf16[2304,512]{1,0:T(8,128)(2,1)} %get-tuple-element.56., ...), custom_call_target="tpu_custom_call" | custom-call | flops 7247757312 | bytes 25165824 | tf_op jit(solution)/shard_map/dense_backward_11/pallas_call | solution.py:1075
  287.5 1.2 convert_reduce_fusion.1
  289.4 121.3 %attend_backward_1.1 = (bf16[2304,512]{1,0:T(8,128)(2,1)}, f32[8,256]{1,0:T(8,128)}, f32[96,768]{1,0:T(8,128)}, f32[96,3072]{1,0:T(8,128)}, f32[384,768]{1,0:T(8,128)}, /*index=5*/f32[96,2304]{1,0:T(8,128)}) custom-call(bf16[768,512]{1,0:T(8,128)(2,1)} %get-tuple-element.58.refs_0_, bf16[576,2048]{1,0:T(8,128)(2,1)} %copy-done, ...), custom_call_target="tpu_custom_call" | custom-call | tf_op jit(solution)/shard_map/attend_backward_1/pallas_call | solution.py:909
  410.8 8.4 %dense_backward_10.1 = f32[512,768]{1,0:T(8,128)} custom-call(bf16[2304,512]{1,0:T(8,128)(2,1)} %get-tuple-element.72.refs_0_, bf16[768,2304]{1,0:T(8,128)(2,1)} %copy-done.1, f32[512,768]{1,0:T(8,128)} %convert_bitcast_fusion.refs_11_.refs_2_, f32[768,512]{1,0:T(8,128)} %get-tuple-element.73.refs_3_, f32[1,768]{1,0:T(1,128)} %reshape.142.refs_4_), custom_call_target="tpu_custom_call" | custom-call | flops 1811939328 | bytes 25165824 | tf_op jit(solution)/shard_map/dense_backward_10/pallas_call | solution.py:1075
  419.2 1.2 slice_bitcast_fusion
  421.9 0.9 copy.33
  423.5 1.0 copy.35
  424.6 1.0 copy.36
  (107 shorter events, 11.1 us)
Async XLA Ops:
  0.6 3.7 copy-start.34
  0.7 3.7 copy-start.32
  0.7 3.7 copy-start.28
  0.7 3.6 copy-start.31
  0.8 4.8 %copy-start.23 = (bf16[1,512,768]{2,1,0:T(8,128)(2,1)S(1)}, bf16[1,512,768]{2,1,0:T(8,128)(2,1)}, u32[]{:S(2)}) copy-start(bf16[1,512,768]{2,1,0:T(8,128)(2,1)} %param.9) | copy-start | bytes 2359300
  37.4 3.5 copy-start.7
  37.4 3.5 copy-start.14
  37.4 3.5 copy-start.15
  40.9 83.7 %copy-start.24 = (bf16[1,512,768]{2,1,0:T(8,128)(2,1)S(1)}, bf16[1,512,768]{2,1,0:T(8,128)(2,1)}, u32[]{:S(2)}) copy-start(bf16[1,512,768]{2,1,0:T(8,128)(2,1)} %param.9) | copy-start | bytes 2359300
  124.7 7.1 %copy-start.12 = (bf16[768,512]{1,0:T(8,128)(2,1)}, bf16[768,512]{1,0:T(8,128)(2,1)S(1)}, u32[]{:S(2)}) copy-start(bf16[768,512]{1,0:T(8,128)(2,1)S(1)} %get-tuple-element.46.refs_6_) | copy-start | bytes 2359300
  124.7 12.4 %copy-start = (bf16[576,2048]{1,0:T(8,128)(2,1)}, bf16[576,2048]{1,0:T(8,128)(2,1)S(1)}, u32[]{:S(2)}) copy-start(bf16[576,2048]{1,0:T(8,128)(2,1)S(1)} %get-tuple-element.50.refs_1_) | copy-start | bytes 7077892
  124.7 52.8 %copy-start.4 = (bf16[768,768]{1,0:T(8,128)(2,1)}, bf16[768,768]{1,0:T(8,128)(2,1)S(1)}, u32[]{:S(2)}) copy-start(bf16[768,768]{1,0:T(8,128)(2,1)S(1)} %get-tuple-element.47.refs_5_.refs_9_) | copy-start | bytes 3538948
  124.7 55.0 %copy-start.3 = (bf16[768,3072]{1,0:T(8,128)(2,1)}, bf16[768,3072]{1,0:T(8,128)(2,1)S(1)}, u32[]{:S(2)}) copy-start(bf16[768,3072]{1,0:T(8,128)(2,1)S(1)} %get-tuple-element.48.refs_4_.refs_8_) | copy-start | bytes 14155780
  125.6 6.2 %copy-start.21 = (f32[512,768]{1,0:T(8,128)}, f32[512,768]{1,0:T(8,128)S(1)}, u32[]{:S(2)}) copy-start(f32[512,768]{1,0:T(8,128)S(1)} %get-tuple-element.82.refs_5_) | copy-start | bytes 4718596
  125.6 6.1 %slice-start = ((s8[4718592]{0:T(1024)(128)(4,1)}), s8[4194304]{0:T(1024)(128)(4,1)S(1)}, s32[]{:S(2)}) async-start(s8[4718592]{0:T(1024)(128)(4,1)} %bitcast.45), calls=%async_computation | async-start | bytes 8388608
  125.9 5.8 %slice-start.1 = ((s8[4718592]{0:T(1024)(128)(4,1)}), s8[524288]{0:T(1024)(128)(4,1)S(1)}, s32[]{:S(2)}) async-start(s8[4718592]{0:T(1024)(128)(4,1)} %bitcast.45), calls=%async_computation.1 | async-start | bytes 1048576
  131.8 3.1 copy-start.2
  134.5 43.0 %copy-start.18 = (f32[512,768]{1,0:T(8,128)}, f32[512,768]{1,0:T(8,128)S(1)}, u32[]{:S(2)}) copy-start(f32[512,768]{1,0:T(8,128)S(1)} %get-tuple-element.86.refs_2_) | copy-start | bytes 4718596
  179.4 6.1 %copy-start.22 = (f32[512,768]{1,0:T(8,128)}, f32[512,768]{1,0:T(8,128)S(1)}, u32[]{:S(2)}) copy-start(f32[512,768]{1,0:T(8,128)S(1)} %get-tuple-element.88.refs_1_) | copy-start | bytes 4718596
  185.5 3.5 copy-start.20
  410.8 9.7 %copy-start.10 = (bf16[96,2304]{1,0:T(8,128)(2,1)S(1)}, bf16[96,2304]{1,0:T(8,128)(2,1)}, u32[]{:S(2)}) copy-start(bf16[96,2304]{1,0:T(8,128)(2,1)} %refs_0_.1) | copy-start | bytes 1327108
  410.8 9.7 %copy-start.26 = (f32[96,2304]{1,0:T(8,128)S(1)}, f32[96,2304]{1,0:T(8,128)}, u32[]{:S(2)}) copy-start(f32[96,2304]{1,0:T(8,128)} %get-tuple-element.104) | copy-start | bytes 2654212
  410.8 9.9 %copy-start.33 = (bf16[96]{0:T(256)(128)(2,1)S(1)}, bf16[96]{0:T(256)(128)(2,1)}, u32[]{:S(2)}) copy-start(bf16[96]{0:T(256)(128)(2,1)} %param.14) | copy-start | bytes 580
  410.8 10.4 %copy-start.25 = (f32[96,3072]{1,0:T(8,128)S(1)}, f32[96,3072]{1,0:T(8,128)}, u32[]{:S(2)}) copy-start(f32[96,3072]{1,0:T(8,128)} %get-tuple-element.106) | copy-start | bytes 3538948
  (14 other events, 24.1 us)

commit v6 on v5

--- a/solution.py
+++ b/solution.py
@@ -11,8 +11,9 @@
 HEAD_DIM = 64
 CHUNK = 768
 EVERY = 3
-SLOTS = 5
+SLOTS = 6
 PAIRS = 2
+AHEAD = 2
 
 
 epsilon = 1e-05
@@ -522,8 +523,9 @@
             work.x_sum,
             work.finish,
         )
-        self.lags = (0, 1, 2, 1, 1, 1)
+        self.lags = (0, 1, 2, 2, 2, 1)
         self.done = [0] * len(self.calls)
+        self.extra = []
 
     def tick(self, limit):
         made = self.done[0]
@@ -542,6 +544,50 @@
     def run_out(self, limit):
         while self.done[-1] < limit:
             self.tick(limit)
+            if self.done[0] == limit and self.extra:
+                self.extra.pop(0)()
+        for task in self.extra:
+            task()
+
+
+def last_tasks(sources, scratch, d_packed, result):
+    weight_s, stream_s, base_s, gain_s, sems = scratch
+    weight, stream, base, gain = sources
+    width = weight_s.shape[1]
+    flying, total = {}, {}
+
+    def fetch(key, source, place, slot):
+        flying[key] = pltpu.make_async_copy(source, place, sems.at[slot])
+        flying[key].start()
+
+    def fetch_weight(part):
+        fetch(part, weight.at[:, pl.ds(part * width, width)], weight_s.at[part % 2], part)
+
+    def begin():
+        fetch_weight(0)
+        fetch_weight(1)
+        fetch("stream", stream, stream_s, 3)
+        fetch("base", base, base_s, 4)
+        fetch("gain", gain, gain_s, 5)
+
+    def multiply(part):
+        flying[part].wait()
+        term = nn(weight_s[part % 2], d_packed[part * width : (part + 1) * width, :])
+        if part == 0:
+            fetch_weight(2)
+        total["grad"] = term if part == 0 else total["grad"] + term
+
+    def end():
+        for key in ("stream", "base", "gain"):
+            flying[key].wait()
+        unit, inverse = norm_unit(stream_s[...].T)
+        grad = base_s[...] + norm_backward(unit, inverse, column(gain_s[...]), total["grad"])
+        stream_s[...] = grad.T
+        copy = pltpu.make_async_copy(stream_s, result, sems.at[6])
+        copy.start()
+        copy.wait()
+
+    return [begin] + [functools.partial(multiply, part) for part in range(3)] + [end]
 
 
 def causal_mask(size):
@@ -725,6 +771,7 @@
         (carry_in, small) = take(2)
         pairs = [take(2) for _ in range(7)]
         (second_packed,) = take(1)
+        last_in = take(4)
     (d_packed_out,) = take(1)
     carry_out = None if units else take(1)[0]
     grads_out = take(5) if units else []
@@ -733,6 +780,7 @@
     if units:
         carry_s, carry_sem = take(2)
         product_scratch = take(3)
+        last_s = take(5)
         work = Scatter(seq, dp, units, grads_out, refs)
         products = Products([small] + pairs + [second_packed], product_scratch, work, d_packed_in)
 
@@ -778,8 +826,8 @@
         )
 
     if units:
-        pipeline.tick(early)
-        pipeline.tick(early)
+        for _ in range(AHEAD):
+            pipeline.tick(early)
     mask = causal_mask(tokens)
     hook = 0
     for h in range(heads):
@@ -861,11 +909,13 @@
                 out_recv.at[h, peer],
                 {"seq": peer},
             ).wait_recv()
-    finished = pltpu.make_async_copy(d_packed_in, d_packed_out, out_sem.at[0])
-    finished.start()
     if units:
+        pipeline.extra = last_tasks(last_in, last_s, d_packed_in, d_packed_out)
         pipeline.run_out(len(units))
         work.drain()
+    else:
+        finished = pltpu.make_async_copy(d_packed_in, d_packed_out, out_sem.at[0])
+        finished.start()
     for copy in copies.values():
         copy.wait_send()
     for h in range(heads - 1):
@@ -877,7 +927,8 @@
         def _():
             outgoing(heads - 1, jnp.int32(j), j).wait_send()
 
-    finished.wait()
+    if not units:
+        finished.wait()
 
 
 def attend_backward(seq, dp, heads, d_mixed, packs, own, totals, extra, units, call_id):
@@ -890,6 +941,8 @@
     dma = pltpu.SemaphoreType.DMA
     f32 = jnp.float32
     out_shape = [jax.ShapeDtypeStruct((3 * width, tokens), jnp.bfloat16)]
+    if units:
+        out_shape = [jax.ShapeDtypeStruct((tokens, width), f32)]
     out_specs = [hbm]
     more = []
     if units:
@@ -902,7 +955,15 @@
         out_shape += [jax.ShapeDtypeStruct(shape, f32) for shape in zip(heights, widths)]
         out_specs += [hbm] * 5
         more = [pltpu.VMEM((2 * HEAD_DIM, length), f32), dma((heads,))]
-        more += Products.scratch(width, tokens) + Scatter.scratch(seq, dp, units)
+        more += Products.scratch(width, tokens)
+        more += [
+            pltpu.VMEM((2, width, width), jnp.bfloat16),
+            pltpu.VMEM((tokens, width), f32),
+            pltpu.VMEM((width, tokens), f32),
+            pltpu.VMEM((1, width), f32),
+            dma((8,)),
+        ]
+        more += Scatter.scratch(seq, dp, units)
     else:
         out_shape.append(jax.ShapeDtypeStruct((heads, 2 * HEAD_DIM, length), f32))
         out_specs.append(vmem)
@@ -960,7 +1021,7 @@
     return 0.5 * (1.0 + bend) + inner * (1.0 - bend * bend)
 
 
-def dense_kernel(first, mlp, chunks, *refs):
+def dense_kernel(first, chunks, *refs):
     refs = list(refs)
 
     def take(count):
@@ -968,21 +1029,37 @@
         del refs[:count]
         return taken
 
-    both = first * mlp
-    count = 5 * first + (1 - first) + 6 * mlp + both
+    count = 5 * first + (1 - first) + 6 + first
     sources = take(count)
-    results = take(1 - mlp + mlp * 5 + both * 4)
+    results = take(5 + first * 4)
     places = take(count)
     sems, out_sems = take(2)
-    fetched = [
-        pltpu.make_async_copy(source, place, sems.at[index])
-        for index, (source, place) in enumerate(zip(sources, places))
-    ]
-    for copy in fetched:
+    base = 5 * first + (1 - first)
+    middle, hidden, down_w, up_w, out_w, gain = range(base, base + 6)
+    width = places[middle].shape[1]
+
+    def span(part):
+        return pl.ds(part * width, width)
+
+    order = [(0, None)]
+    if first:
+        order = [(index, part) for part in range(3) for index in (1, 0)] + [(2, None), (4, None), (3, None)]
+    for part in range(chunks):
+        order += [(down_w, part), (hidden, part), (up_w, part)]
+    order += [(middle, None), (gain, None), (out_w, None)] + [(base + 6, None)] * first
+    by_columns = (up_w, 1) if first else (up_w,)
+    fetched = {}
+    for index, part in order:
+        source, place = sources[index], places[index]
+        if part is not None:
+            where = (slice(None), span(part)) if index in by_columns else (span(part),)
+            source, place = source.at[where], place.at[where]
+        copy = pltpu.make_async_copy(source, place, sems.at[index, part or 0])
         copy.start()
-
-    def get(index):
-        fetched[index].wait()
+        fetched[index, part] = copy
+
+    def get(index, part=None):
+        fetched[index, part].wait()
         return places[index]
 
     sent = []
@@ -993,96 +1070,84 @@
         sent.append(copy)
 
     if first:
-        grad = nn(get(1)[...], get(0)[...])
+        grad = None
+        for part in range(3):
+            term = nn(get(1, part)[:, span(part)], get(0, part)[span(part), :])
+            grad = term if grad is None else grad + term
         unit, inverse = norm_unit(get(2)[...].T)
         gain_a = column(get(4)[...])
         upstream = get(3)[...] + norm_backward(unit, inverse, gain_a, grad)
     else:
         upstream = get(0)[...].astype(jnp.float32)
-    if not mlp:
-        (out_s,) = refs
-        out_s[...] = upstream.T
-        put(out_s, results[0])
-    else:
-        base = 5 * first + (1 - first)
-        middle, hidden, down_w, up_w, out_w, gain = range(base, base + 6)
-        hidden_s, grad_s, middle_s, mixed_s, normed_s, up_s, rounded_s = refs[:7]
-        up_s[...] = upstream
-        rounded_s[...] = upstream.astype(jnp.bfloat16)
-        if first:
-            first_s, second_s = refs[7:]
-            rounded_out, sum_out, first_out, second_out = results[5:]
-            put(rounded_s, rounded_out)
-            sum_out[...] = jnp.sum(upstream, axis=1, keepdims=True)
-            second_s[...] = (unit * gain_a).astype(jnp.bfloat16)
-            put(second_s, second_out)
-        size = places[hidden].shape[0] // chunks
-        get(down_w)
-        get(hidden)
-        total = None
-        for chunk in range(chunks):
-            span = slice(chunk * size, (chunk + 1) * size)
-            d_active = nn(places[down_w][span, :], rounded_s[...])
-            hidden_s[span, :] = (d_active * gelu_slope(places[hidden][span, :])).astype(jnp.bfloat16)
-            put(hidden_s.at[span], results[0].at[span])
-            if chunk == 0:
-                get(up_w)
-            part = nn(places[up_w][:, span], hidden_s[span, :])
-            total = part if total is None else total + part
-        unit, inverse = norm_unit(get(middle)[...].T)
-        gain_b = column(get(gain)[...])
-        d_middle = up_s[...] + norm_backward(unit, inverse, gain_b, total)
-        grad_s[...] = d_middle
-        middle_s[...] = d_middle.astype(jnp.bfloat16)
-        normed_s[...] = (unit * gain_b).astype(jnp.bfloat16)
-        put(grad_s, results[1])
-        put(middle_s, results[2])
-        put(normed_s, results[4])
-        mixed_s[...] = nn(get(out_w)[...], middle_s[...]).astype(jnp.bfloat16)
-        put(mixed_s, results[3])
-        if first:
-            first_s[...] = (norm_unit(get(base + 6)[...].T)[0] * gain_a).astype(jnp.bfloat16)
-            put(first_s, first_out)
+    hidden_s, grad_s, middle_s, mixed_s, normed_s, up_s, rounded_s = refs[:7]
+    up_s[...] = upstream
+    rounded_s[...] = upstream.astype(jnp.bfloat16)
+    if first:
+        first_s, second_s = refs[7:]
+        rounded_out, sum_out, first_out, second_out = results[5:]
+        put(rounded_s, rounded_out)
+        sum_out[...] = jnp.sum(upstream, axis=1, keepdims=True)
+        second_s[...] = (unit * gain_a).astype(jnp.bfloat16)
+        put(second_s, second_out)
+    total = None
+    for part in range(chunks):
+        d_active = nn(get(down_w, part)[span(part), :], rounded_s[...])
+        slope = gelu_slope(get(hidden, part)[span(part), :])
+        hidden_s[span(part), :] = (d_active * slope).astype(jnp.bfloat16)
+        put(hidden_s.at[span(part)], results[0].at[span(part)])
+        term = nn(get(up_w, part)[:, span(part)], hidden_s[span(part), :])
+        total = term if total is None else total + term
+    unit, inverse = norm_unit(get(middle)[...].T)
+    gain_b = column(get(gain)[...])
+    d_middle = up_s[...] + norm_backward(unit, inverse, gain_b, total)
+    grad_s[...] = d_middle
+    middle_s[...] = d_middle.astype(jnp.bfloat16)
+    normed_s[...] = (unit * gain_b).astype(jnp.bfloat16)
+    put(grad_s, results[1])
+    put(middle_s, results[2])
+    put(normed_s, results[4])
+    mixed_s[...] = nn(get(out_w)[...], middle_s[...]).astype(jnp.bfloat16)
+    put(mixed_s, results[3])
+    if first:
+        first_s[...] = (norm_unit(get(base + 6)[...].T)[0] * gain_a).astype(jnp.bfloat16)
+        put(first_s, first_out)
     for copy in sent:
         copy.wait()
 
 
 def dense_backward(before, after):
-    first, mlp = int(len(before) > 1), int(len(after) > 0)
+    first = int(len(before) > 1)
     args = list(before) + list(after)
     width, tokens = (before[3] if first else before[0]).shape
     hbm = pl.BlockSpec(memory_space=pl.ANY)
     b, f32 = jnp.bfloat16, jnp.float32
-    chunks, outs, specs, more = 1, [jax.ShapeDtypeStruct((tokens, width), f32)], [hbm], []
-    flops = 6 * width * width * tokens * first
-    if mlp:
-        ff = after[1].shape[0]
-        chunks = ff // width
-        flops += 2 * tokens * width * (2 * ff + width)
-        flat = (width, tokens)
-        shapes = [((ff, tokens), b), (flat, f32), (flat, b), (flat, b), (flat, b)]
-        more = [pltpu.VMEM(shape, kind) for shape, kind in shapes]
-        more += [pltpu.VMEM(flat, f32), pltpu.VMEM(flat, b)]
-        outs = [jax.ShapeDtypeStruct(shape, kind) for shape, kind in shapes]
-        specs = [hbm] * 5
-        if first:
-            more += [pltpu.VMEM(flat, b)] * 2
-            outs += [jax.ShapeDtypeStruct(flat, b), jax.ShapeDtypeStruct((width, 1), f32)]
-            outs += [jax.ShapeDtypeStruct(flat, b)] * 2
-            specs += [hbm, pl.BlockSpec(memory_space=pltpu.VMEM), hbm, hbm]
-    else:
-        more = [pltpu.VMEM((tokens, width), f32)]
+    ff = after[1].shape[0]
+    flat = (width, tokens)
+    shapes = [((ff, tokens), b), (flat, f32), (flat, b), (flat, b), (flat, b)]
+    more = [pltpu.VMEM(shape, kind) for shape, kind in shapes]
+    more += [pltpu.VMEM(flat, f32), pltpu.VMEM(flat, b)]
+    outs = [jax.ShapeDtypeStruct(shape, kind) for shape, kind in shapes]
+    specs = [hbm] * 5
+    if first:
+        more += [pltpu.VMEM(flat, b)] * 2
+        outs += [jax.ShapeDtypeStruct(flat, b), jax.ShapeDtypeStruct((width, 1), f32)]
+        outs += [jax.ShapeDtypeStruct(flat, b)] * 2
+        specs += [hbm, pl.BlockSpec(memory_space=pltpu.VMEM), hbm, hbm]
+    flops = 2 * tokens * width * (2 * ff + width + 3 * width * first)
     return pl.pallas_call(
-        functools.partial(dense_kernel, first, mlp, chunks),
+        functools.partial(dense_kernel, first, ff // width),
         out_shape=tuple(outs),
         in_specs=[hbm] * len(args),
         out_specs=tuple(specs),
         scratch_shapes=[pltpu.VMEM(arg.shape, arg.dtype) for arg in args]
-        + [pltpu.SemaphoreType.DMA((len(args),)), pltpu.SemaphoreType.DMA((16,))]
+        + [
+            pltpu.SemaphoreType.DMA((len(args), max(3, ff // width))),
+            pltpu.SemaphoreType.DMA((16,)),
+        ]
         + more,
         compiler_params=pltpu.CompilerParams(vmem_limit_bytes=58 << 20),
         cost_estimate=pl.CostEstimate(flops=flops, bytes_accessed=24 << 20, transcendentals=0),
-        name=f"dense_backward_{first}{mlp}",
+        name=f"dense_backward_{first}",
     )(*args)
 
 
@@ -1139,7 +1204,7 @@
         extra = [passed, jnp.pad(embed, ((0, 0), (0, 7), (0, 256 - rows)))]
         for pair in zip(factors, second_factors):
             extra += pair
-        extra.append(second_packed)
+        extra += [second_packed, before[1], stream, d_middle, before[4]]
         ff = d_hidden.shape[0]
         units = [(0, 8, 256, 0, 0)]
         units += [(1, rows, width, 0, 0)]
@@ -1199,11 +1264,8 @@
     )
     second = (outs[1], factors, outs[0])
     before = (outs[0], qkv_w, stream, d_middle, gains[0])
-    (stream, d_middle), factors, outs = block_backward(
-        sizes, 4, before, first_kept, gains, weights, second
-    )
-    d_first = dense_backward((outs[0], qkv_w, stream, d_middle, gains[0]), ())[0]
-    packed, small, out_grad, up_grad, down_grad, qkv_grad = outs
+    _, _, outs = block_backward(sizes, 4, before, first_kept, gains, weights, second)
+    d_first, small, out_grad, up_grad, down_grad, qkv_grad = outs
     f32 = jnp.float32
     gain_a = jnp.sum(qkv_weight.astype(f32) * qkv_grad, axis=1) / norm_gain.astype(f32)
     gain_b = jnp.sum(up_weight.astype(f32) * up_grad, axis=1) / mlp_gain.astype(f32)

time: 423 us -> 417 us (0.986)
  Pallas kernels: 378 us -> 367 us
    pallas_call x3 -> x2, Pallas kernels: 46.1 us -> 37.6 us  [dense_backward(): pl.pallas_call(functools.partial(dense_kernel, first, ff // width), out_s...]
    unnamed x81 -> x84, local copies, waits for them, and re-layouts: 7.45 us -> 9.37 us
where the time goes in v6:
time: 417 us; the launch traced here: 419 us
  Pallas kernels  367 us (88%)
  matrix products  25.3 us (6%)
  local copies, waits for them, and re-layouts  13.7 us (3%)
  other arithmetic  11.6 us (3%)
    pallas_call x2, Pallas kernels, attend_backward(): pl.pallas_call(functools.partial(backward_kernel, seq, dp, sets, units, h...  179 us
    pallas_call x2, Pallas kernels, attend_forward(): pl.pallas_call(functools.partial(forward_kernel, seq, dp, sets, units, ar...  123 us
    pallas_call x2, Pallas kernels, dense_backward(): pl.pallas_call(functools.partial(dense_kernel, first, ff // width), out_s...  37.6 us
    pallas_call x1, Pallas kernels, gather_now(): pl.pallas_call(functools.partial(gather_kernel, seq, dp, units, arrays),...  27.5 us
    dot_general x8, matrix products, dots(): lax.dot_general(left, right, (((left_side,), (right_side,)), ((), ())), p...  25.3 us
    unnamed x84, local copies, waits for them, and re-layouts  9.37 us

profile of v6, /device:TPU:0, one launch (start us, length us, event | category | flops | bytes accessed | tf_op | source)
XLA Modules:
  0.0 418.8 jit_solution(12710216544430514815)
XLA Ops:
  0.8 1.4 convert_reduce_fusion
  2.2 1.5 multiply_reduce_fusion.3
  4.4 1.2 copy.23
  5.5 1.3 convert_bitcast_fusion.refs_11_.refs_22_
  6.8 27.5 %gather_first.1 = (bf16[768,2304]{1,0:T(8,128)(2,1)S(1)}, bf16[64,256]{1,0:T(8,128)(2,1)S(1)}) custom-call(bf16[96,2304]{1,0:T(8,128)(2,1)S(1)} %copy-done.9, bf16[8,256]{1,0:T(8,128)(2,1)S(1)} %fusion.40.refs_1_), custom_call_target="tpu_custom_call" | custom-call | tf_op jit(solution)/shard_map/gather_first/pallas_call | solution.py:225
  37.4 3.5 convolution_convert_fusion.1.refs_0_
  40.9 82.2 %attend_forward_1.1 = (bf16[576,2048]{1,0:T(8,128)(2,1)S(1)}, bf16[768,512]{1,0:T(8,128)(2,1)S(1)}, bf16[192,2048]{1,0:T(8,128)(2,1)S(1)}, f32[3,1,2048]{2,1,0:T...) custom-call(bf16[2304,512]{1,0:T(8,128)(2,1)S(1)} %convolution_convert_fusion.1., ...), custom_call_target="tpu_custom_call" | custom-call | tf_op jit(solution)/shard_map/attend_forward_1/pallas_call | solution.py:728
  125.9 5.8 %fusion.7 = (bf16[3072,512]{1,0:T(8,128)(2,1)S(1)}, f32[3072,512]{1,0:T(8,128)}) fusion(bf16[768,3072]{1,0:T(8,128)(2,1)S(1)} %get-tuple-element.48.refs_4_.refs_8_, f32[512,768]{1,0:T(8,128)S(1)} %get-tuple-element.82.refs_5_, f32[768]{0:T(1024)S(1)} %reshape.139, f32[512]{0:T(512)S(1)} %add_rsqrt_fusion.2, f32[512]{0:T(512)S(1)} %broadcast_multiply_fusion.2), kind=kOutput, calls=%fused_computation.9 | convolution fusion | flops 2431647744 | bytes 15735808 | tf_op jit(solution)/shard_map/dot_general | solution.py:1155
  131.7 2.7 fusion.45
  134.8 2.2 convolution_convert_fusion.refs_0_
  137.1 40.3 %attend_forward_2.1 = (bf16[576,2048]{1,0:T(8,128)(2,1)S(1)}, bf16[768,512]{1,0:T(8,128)(2,1)S(1)}, bf16[192,2048]{1,0:T(8,128)(2,1)S(1)}, f32[3,1,2048]{2,1,0:T(1,128)S(1)}) custom-call(bf16[2304,512]{1,0:T(8,128)(2,1)S(1)} %convolution_convert_fusion.refs_0_, bf16[576,2048]{1,0:T(8,128)(2,1)S(1)} %get-tuple-element.50.refs_1_), custom_call_target="tpu_custom_call" | custom-call | tf_op jit(solution)/shard_map/attend_forward_2/pallas_call | solution.py:728
  179.6 5.8 %fusion.15 = (bf16[3072,512]{1,0:T(8,128)(2,1)S(1)}, f32[3072,512]{1,0:T(8,128)}) fusion(bf16[768,3072]{1,0:T(8,128)(2,1)S(1)} %get-tuple-element.48.refs_4_.refs_8_, f32[512,768]{1,0:T(8,128)S(1)} %get-tuple-element.88.refs_1_, f32[512]{0:T(512)S(1)} %add_rsqrt_fusion, f32[512]{0:T(512)S(1)} %broadcast_multiply_fusion, f32[768]{0:T(1024)S(1)} %reshape.139), kind=kOutput, calls=%fused_computation.17 | convolution fusion | flops 2431647744 | bytes 15735808 | tf_op jit(solution)/shard_map/dot_general | solution.py:1155
  185.4 3.5 fusion.16
  189.0 15.5 %dense_backward_0.1 = (bf16[3072,512]{1,0:T(8,128)(2,1)}, f32[768,512]{1,0:T(8,128)}, bf16[768,512]{1,0:T(8,128)(2,1)}, bf16[768,512]{1,0:T(8,128)(2,1)}, bf16[768,512]{1,0:T(8,128)(2,1)}) custom-call(bf16[768,512]{1,0:T(8,128)(2,1)} %bitcast.49, f32[512,768]{1,0:T(8,128)} %copy-done.22, f32[3072,512]{1,0:T(8,128)} %get-tuple-element.90.refs_2_, ...), custom_call_target="tpu_custom_call" | custom-call | flops 5435817984 | bytes 25165824 | tf_op jit(solution)/shard_map/dense_backward_0/pallas_call | solution.py:1137
  204.4 60.4 %attend_backward_2.1 = (bf16[2304,512]{1,0:T(8,128)(2,1)}, f32[3,128,2048]{2,1,0:T(8,128)}) custom-call(bf16[768,512]{1,0:T(8,128)(2,1)} %get-tuple-element.52.refs_0_, bf16[576,2048]{1,0:T(8,128)(2,1)} %copy-done, bf16[576,2048]{1,0:T(8,128)(2,1)} %copy-done.6, bf16[192,2048]{1,0:T(8,128)(2,1)} %copy-done.11, f32[3,1,2048]{2,1,0:T(1,128)} %copy-done.17), custom_call_target="tpu_custom_call" | custom-call | tf_op jit(solution)/shard_map/attend_backward_2/pallas_call | solution.py:970
  264.8 22.1 %dense_backward_1.1 = (bf16[3072,512]{1,0:T(8,128)(2,1)}, f32[768,512]{1,0:T(8,128)}, bf16[768,512]{1,0:T(8,128)(2,1)}, bf16[768,512]{1,0:T(8,128)(2,1)}, bf16[7...) custom-call(bf16[2304,512]{1,0:T(8,128)(2,1)} %get-tuple-element.56., ...), custom_call_target="tpu_custom_call" | custom-call | flops 7247757312 | bytes 25165824 | tf_op jit(solution)/shard_map/dense_backward_1/pallas_call | solution.py:1137
  287.0 1.2 convert_reduce_fusion.1
  288.9 118.8 %attend_backward_1.1 = (f32[512,768]{1,0:T(8,128)}, f32[8,256]{1,0:T(8,128)}, f32[96,768]{1,0:T(8,128)}, f32[96,3072]{1,0:T(8,128)}, f32[384,768]{1,0:T(8,128)}, /*index=5*/f32[96,2304]{1,0:T(8,128)}) custom-call(bf16[768,512]{1,0:T(8,128)(2,1)} %get-tuple-element.58.refs_0_, bf16[576,2048]{1,0:T(8,128)(2,1)} %copy-done, bf16[192,2048]{1,0:T(8,128)(2,1)} %copy-done.13, ...), custom_call_target="tpu_custom_call" | custom-call | tf_op jit(solution)/shard_map/attend_backward_1/pallas_call | solution.py:970
  407.7 1.3 slice_bitcast_fusion
  409.0 1.4 multiply_reduce_fusion.5
  410.9 1.5 multiply_reduce_fusion.4
  413.0 1.1 copy.34
  416.5 1.0 copy.37
  417.6 1.0 copy.38
  (109 shorter events, 13.2 us)
Async XLA Ops:
  0.6 3.7 copy-start.35
  0.7 3.7 copy-start.33
  0.7 3.7 copy-start.29
  0.7 3.6 copy-start.32
  0.8 4.8 %copy-start.23 = (bf16[1,512,768]{2,1,0:T(8,128)(2,1)S(1)}, bf16[1,512,768]{2,1,0:T(8,128)(2,1)}, u32[]{:S(2)}) copy-start(bf16[1,512,768]{2,1,0:T(8,128)(2,1)} %param.9) | copy-start | bytes 2359300
  37.3 3.5 copy-start.7
  37.4 3.5 copy-start.14
  37.4 3.5 copy-start.15
  40.9 83.7 %copy-start.24 = (bf16[1,512,768]{2,1,0:T(8,128)(2,1)S(1)}, bf16[1,512,768]{2,1,0:T(8,128)(2,1)}, u32[]{:S(2)}) copy-start(bf16[1,512,768]{2,1,0:T(8,128)(2,1)} %param.9) | copy-start | bytes 2359300
  124.6 7.1 %copy-start.12 = (bf16[768,512]{1,0:T(8,128)(2,1)}, bf16[768,512]{1,0:T(8,128)(2,1)S(1)}, u32[]{:S(2)}) copy-start(bf16[768,512]{1,0:T(8,128)(2,1)S(1)} %get-tuple-element.46.refs_6_) | copy-start | bytes 2359300
  124.6 12.4 %copy-start = (bf16[576,2048]{1,0:T(8,128)(2,1)}, bf16[576,2048]{1,0:T(8,128)(2,1)S(1)}, u32[]{:S(2)}) copy-start(bf16[576,2048]{1,0:T(8,128)(2,1)S(1)} %get-tuple-element.50.refs_1_) | copy-start | bytes 7077892
  124.6 52.8 %copy-start.4 = (bf16[768,768]{1,0:T(8,128)(2,1)}, bf16[768,768]{1,0:T(8,128)(2,1)S(1)}, u32[]{:S(2)}) copy-start(bf16[768,768]{1,0:T(8,128)(2,1)S(1)} %get-tuple-element.47.refs_5_.refs_9_) | copy-start | bytes 3538948
  124.6 55.0 %copy-start.3 = (bf16[768,3072]{1,0:T(8,128)(2,1)}, bf16[768,3072]{1,0:T(8,128)(2,1)S(1)}, u32[]{:S(2)}) copy-start(bf16[768,3072]{1,0:T(8,128)(2,1)S(1)} %get-tuple-element.48.refs_4_.refs_8_) | copy-start | bytes 14155780
  125.5 6.2 %copy-start.21 = (f32[512,768]{1,0:T(8,128)}, f32[512,768]{1,0:T(8,128)S(1)}, u32[]{:S(2)}) copy-start(f32[512,768]{1,0:T(8,128)S(1)} %get-tuple-element.82.refs_5_) | copy-start | bytes 4718596
  125.5 6.1 %slice-start = ((s8[4718592]{0:T(1024)(128)(4,1)}), s8[4194304]{0:T(1024)(128)(4,1)S(1)}, s32[]{:S(2)}) async-start(s8[4718592]{0:T(1024)(128)(4,1)} %bitcast.45), calls=%async_computation | async-start | bytes 8388608
  125.9 5.8 %slice-start.1 = ((s8[4718592]{0:T(1024)(128)(4,1)}), s8[524288]{0:T(1024)(128)(4,1)S(1)}, s32[]{:S(2)}) async-start(s8[4718592]{0:T(1024)(128)(4,1)} %bitcast.45), calls=%async_computation.1 | async-start | bytes 1048576
  134.5 43.0 %copy-start.18 = (f32[512,768]{1,0:T(8,128)}, f32[512,768]{1,0:T(8,128)S(1)}, u32[]{:S(2)}) copy-start(f32[512,768]{1,0:T(8,128)S(1)} %get-tuple-element.86.refs_2_) | copy-start | bytes 4718596
  179.3 6.1 %copy-start.22 = (f32[512,768]{1,0:T(8,128)}, f32[512,768]{1,0:T(8,128)S(1)}, u32[]{:S(2)}) copy-start(f32[512,768]{1,0:T(8,128)S(1)} %get-tuple-element.88.refs_1_) | copy-start | bytes 4718596
  185.4 3.5 copy-start.20
  288.9 120.2 %copy-start.10 = (bf16[96,2304]{1,0:T(8,128)(2,1)S(1)}, bf16[96,2304]{1,0:T(8,128)(2,1)}, u32[]{:S(2)}) copy-start(bf16[96,2304]{1,0:T(8,128)(2,1)} %refs_0_.1) | copy-start | bytes 1327108
  288.9 121.5 %copy-start.34 = (bf16[96]{0:T(256)(128)(2,1)S(1)}, bf16[96]{0:T(256)(128)(2,1)}, u32[]{:S(2)}) copy-start(bf16[96]{0:T(256)(128)(2,1)} %param.14) | copy-start | bytes 580
  407.7 3.3 copy-start.8
  407.7 4.7 %copy-start.36 = (bf16[96]{0:T(256)(128)(2,1)S(1)}, bf16[96]{0:T(256)(128)(2,1)}, u32[]{:S(2)}) copy-start(bf16[96]{0:T(256)(128)(2,1)} %param.15) | copy-start | bytes 580
  407.7 5.3 %copy-start.27 = (f32[512,768]{1,0:T(8,128)S(1)}, f32[512,768]{1,0:T(8,128)}, u32[]{:S(2)}) copy-start(f32[512,768]{1,0:T(8,128)} %get-tuple-element.73) | copy-start | bytes 4718596
  (15 other events, 26.0 us)

commit v7 on v6

--- a/solution.py
+++ b/solution.py
@@ -880,7 +880,7 @@
                     d_query = part if d_query is None else d_query + part
                 dq_s[:, span] = d_query
                 hook += 1
-                if units and hook % EVERY == 0:
+                if units and hook % EVERY == 0 and hook < heads * seq * (seq + 1) // 2:
                     pipeline.tick(early)
             local_grad[c0 : c0 + HEAD_DIM, keys] = dq_s[:, keys].astype(jnp.bfloat16)
             local_grad[c0 + HEAD_DIM : c0 + group, keys] = dkv_s[sets - 1, :, keys].astype(
@@ -900,6 +900,8 @@
         d_packed_in[pl.ds(pl.multiple_of((me * heads + h) * group, group), group)] = local_grad[
             c0 : c0 + group, own_lanes
         ]
+    if units:
+        pipeline.tick(early)
     for h in range(heads):
         for peer in peers:
             remote(

time: 417 us -> 416 us (level)
  no operation moved by 1% of the time
where the time goes in v7:
time: 416 us; the launch traced here: 417 us
  Pallas kernels  365 us (88%)
  matrix products  25.3 us (6%)
  local copies, waits for them, and re-layouts  13.7 us (3%)
  other arithmetic  11.6 us (3%)
    pallas_call x2, Pallas kernels, attend_backward(): pl.pallas_call(functools.partial(backward_kernel, seq, dp, sets, units, h...  178 us
    pallas_call x2, Pallas kernels, attend_forward(): pl.pallas_call(functools.partial(forward_kernel, seq, dp, sets, units, ar...  123 us
    pallas_call x2, Pallas kernels, dense_backward(): pl.pallas_call(functools.partial(dense_kernel, first, ff // width), out_s...  37.6 us
    pallas_call x1, Pallas kernels, gather_now(): pl.pallas_call(functools.partial(gather_kernel, seq, dp, units, arrays),...  27.5 us
    dot_general x8, matrix products, dots(): lax.dot_general(left, right, (((left_side,), (right_side,)), ((), ())), p...  25.3 us
    unnamed x84, local copies, waits for them, and re-layouts  9.37 us

profile of v7, /device:TPU:0, one launch (start us, length us, event | category | flops | bytes accessed | tf_op | source)
XLA Modules:
  0.0 417.2 jit_solution(14404243548927949179)
XLA Ops:
  0.8 1.4 convert_reduce_fusion
  2.2 1.5 multiply_reduce_fusion.3
  4.4 1.2 copy.23
  5.5 1.3 convert_bitcast_fusion.refs_11_.refs_22_
  6.8 27.5 %gather_first.1 = (bf16[768,2304]{1,0:T(8,128)(2,1)S(1)}, bf16[64,256]{1,0:T(8,128)(2,1)S(1)}) custom-call(bf16[96,2304]{1,0:T(8,128)(2,1)S(1)} %copy-done.9, bf16[8,256]{1,0:T(8,128)(2,1)S(1)} %fusion.40.refs_1_), custom_call_target="tpu_custom_call" | custom-call | tf_op jit(solution)/shard_map/gather_first/pallas_call | solution.py:225
  37.4 3.5 convolution_convert_fusion.1.refs_0_
  40.9 82.2 %attend_forward_1.1 = (bf16[576,2048]{1,0:T(8,128)(2,1)S(1)}, bf16[768,512]{1,0:T(8,128)(2,1)S(1)}, bf16[192,2048]{1,0:T(8,128)(2,1)S(1)}, f32[3,1,2048]{2,1,0:T...) custom-call(bf16[2304,512]{1,0:T(8,128)(2,1)S(1)} %convolution_convert_fusion.1., ...), custom_call_target="tpu_custom_call" | custom-call | tf_op jit(solution)/shard_map/attend_forward_1/pallas_call | solution.py:728
  125.9 5.8 %fusion.7 = (bf16[3072,512]{1,0:T(8,128)(2,1)S(1)}, f32[3072,512]{1,0:T(8,128)}) fusion(bf16[768,3072]{1,0:T(8,128)(2,1)S(1)} %get-tuple-element.48.refs_4_.refs_8_, f32[512,768]{1,0:T(8,128)S(1)} %get-tuple-element.82.refs_5_, f32[768]{0:T(1024)S(1)} %reshape.139, f32[512]{0:T(512)S(1)} %add_rsqrt_fusion.2, f32[512]{0:T(512)S(1)} %broadcast_multiply_fusion.2), kind=kOutput, calls=%fused_computation.9 | convolution fusion | flops 2431647744 | bytes 15735808 | tf_op jit(solution)/shard_map/dot_general | solution.py:1157
  131.7 2.7 fusion.45
  134.8 2.2 convolution_convert_fusion.refs_0_
  137.1 40.3 %attend_forward_2.1 = (bf16[576,2048]{1,0:T(8,128)(2,1)S(1)}, bf16[768,512]{1,0:T(8,128)(2,1)S(1)}, bf16[192,2048]{1,0:T(8,128)(2,1)S(1)}, f32[3,1,2048]{2,1,0:T(1,128)S(1)}) custom-call(bf16[2304,512]{1,0:T(8,128)(2,1)S(1)} %convolution_convert_fusion.refs_0_, bf16[576,2048]{1,0:T(8,128)(2,1)S(1)} %get-tuple-element.50.refs_1_), custom_call_target="tpu_custom_call" | custom-call | tf_op jit(solution)/shard_map/attend_forward_2/pallas_call | solution.py:728
  179.6 5.8 %fusion.15 = (bf16[3072,512]{1,0:T(8,128)(2,1)S(1)}, f32[3072,512]{1,0:T(8,128)}) fusion(bf16[768,3072]{1,0:T(8,128)(2,1)S(1)} %get-tuple-element.48.refs_4_.refs_8_, f32[512,768]{1,0:T(8,128)S(1)} %get-tuple-element.88.refs_1_, f32[512]{0:T(512)S(1)} %add_rsqrt_fusion, f32[512]{0:T(512)S(1)} %broadcast_multiply_fusion, f32[768]{0:T(1024)S(1)} %reshape.139), kind=kOutput, calls=%fused_computation.17 | convolution fusion | flops 2431647744 | bytes 15735808 | tf_op jit(solution)/shard_map/dot_general | solution.py:1157
  185.4 3.5 fusion.16
  189.0 15.5 %dense_backward_0.1 = (bf16[3072,512]{1,0:T(8,128)(2,1)}, f32[768,512]{1,0:T(8,128)}, bf16[768,512]{1,0:T(8,128)(2,1)}, bf16[768,512]{1,0:T(8,128)(2,1)}, bf16[768,512]{1,0:T(8,128)(2,1)}) custom-call(bf16[768,512]{1,0:T(8,128)(2,1)} %bitcast.49, f32[512,768]{1,0:T(8,128)} %copy-done.22, f32[3072,512]{1,0:T(8,128)} %get-tuple-element.90.refs_2_, ...), custom_call_target="tpu_custom_call" | custom-call | flops 5435817984 | bytes 25165824 | tf_op jit(solution)/shard_map/dense_backward_0/pallas_call | solution.py:1139
  204.4 60.4 %attend_backward_2.1 = (bf16[2304,512]{1,0:T(8,128)(2,1)}, f32[3,128,2048]{2,1,0:T(8,128)}) custom-call(bf16[768,512]{1,0:T(8,128)(2,1)} %get-tuple-element.52.refs_0_, bf16[576,2048]{1,0:T(8,128)(2,1)} %copy-done, bf16[576,2048]{1,0:T(8,128)(2,1)} %copy-done.6, bf16[192,2048]{1,0:T(8,128)(2,1)} %copy-done.11, f32[3,1,2048]{2,1,0:T(1,128)} %copy-done.17), custom_call_target="tpu_custom_call" | custom-call | tf_op jit(solution)/shard_map/attend_backward_2/pallas_call | solution.py:972
  264.8 22.1 %dense_backward_1.1 = (bf16[3072,512]{1,0:T(8,128)(2,1)}, f32[768,512]{1,0:T(8,128)}, bf16[768,512]{1,0:T(8,128)(2,1)}, bf16[768,512]{1,0:T(8,128)(2,1)}, bf16[7...) custom-call(bf16[2304,512]{1,0:T(8,128)(2,1)} %get-tuple-element.56., ...), custom_call_target="tpu_custom_call" | custom-call | flops 7247757312 | bytes 25165824 | tf_op jit(solution)/shard_map/dense_backward_1/pallas_call | solution.py:1139
  287.0 1.2 convert_reduce_fusion.1
  288.9 117.3 %attend_backward_1.1 = (f32[512,768]{1,0:T(8,128)}, f32[8,256]{1,0:T(8,128)}, f32[96,768]{1,0:T(8,128)}, f32[96,3072]{1,0:T(8,128)}, f32[384,768]{1,0:T(8,128)}, /*index=5*/f32[96,2304]{1,0:T(8,128)}) custom-call(bf16[768,512]{1,0:T(8,128)(2,1)} %get-tuple-element.58.refs_0_, bf16[576,2048]{1,0:T(8,128)(2,1)} %copy-done, bf16[192,2048]{1,0:T(8,128)(2,1)} %copy-done.13, ...), custom_call_target="tpu_custom_call" | custom-call | tf_op jit(solution)/shard_map/attend_backward_1/pallas_call | solution.py:972
  406.2 1.3 slice_bitcast_fusion
  407.5 1.4 multiply_reduce_fusion.5
  409.4 1.5 multiply_reduce_fusion.4
  411.4 1.1 copy.34
  415.0 1.0 copy.37
  416.0 1.0 copy.38
  (109 shorter events, 13.2 us)
Async XLA Ops:
  0.6 3.7 copy-start.35
  0.7 3.7 copy-start.33
  0.7 3.7 copy-start.29
  0.7 3.6 copy-start.32
  0.8 4.8 %copy-start.23 = (bf16[1,512,768]{2,1,0:T(8,128)(2,1)S(1)}, bf16[1,512,768]{2,1,0:T(8,128)(2,1)}, u32[]{:S(2)}) copy-start(bf16[1,512,768]{2,1,0:T(8,128)(2,1)} %param.9) | copy-start | bytes 2359300
  37.3 3.5 copy-start.7
  37.4 3.5 copy-start.14
  37.4 3.5 copy-start.15
  40.9 83.7 %copy-start.24 = (bf16[1,512,768]{2,1,0:T(8,128)(2,1)S(1)}, bf16[1,512,768]{2,1,0:T(8,128)(2,1)}, u32[]{:S(2)}) copy-start(bf16[1,512,768]{2,1,0:T(8,128)(2,1)} %param.9) | copy-start | bytes 2359300
  124.6 7.1 %copy-start.12 = (bf16[768,512]{1,0:T(8,128)(2,1)}, bf16[768,512]{1,0:T(8,128)(2,1)S(1)}, u32[]{:S(2)}) copy-start(bf16[768,512]{1,0:T(8,128)(2,1)S(1)} %get-tuple-element.46.refs_6_) | copy-start | bytes 2359300
  124.6 12.4 %copy-start = (bf16[576,2048]{1,0:T(8,128)(2,1)}, bf16[576,2048]{1,0:T(8,128)(2,1)S(1)}, u32[]{:S(2)}) copy-start(bf16[576,2048]{1,0:T(8,128)(2,1)S(1)} %get-tuple-element.50.refs_1_) | copy-start | bytes 7077892
  124.6 52.8 %copy-start.4 = (bf16[768,768]{1,0:T(8,128)(2,1)}, bf16[768,768]{1,0:T(8,128)(2,1)S(1)}, u32[]{:S(2)}) copy-start(bf16[768,768]{1,0:T(8,128)(2,1)S(1)} %get-tuple-element.47.refs_5_.refs_9_) | copy-start | bytes 3538948
  124.6 55.0 %copy-start.3 = (bf16[768,3072]{1,0:T(8,128)(2,1)}, bf16[768,3072]{1,0:T(8,128)(2,1)S(1)}, u32[]{:S(2)}) copy-start(bf16[768,3072]{1,0:T(8,128)(2,1)S(1)} %get-tuple-element.48.refs_4_.refs_8_) | copy-start | bytes 14155780
  125.5 6.2 %copy-start.21 = (f32[512,768]{1,0:T(8,128)}, f32[512,768]{1,0:T(8,128)S(1)}, u32[]{:S(2)}) copy-start(f32[512,768]{1,0:T(8,128)S(1)} %get-tuple-element.82.refs_5_) | copy-start | bytes 4718596
  125.5 6.1 %slice-start = ((s8[4718592]{0:T(1024)(128)(4,1)}), s8[4194304]{0:T(1024)(128)(4,1)S(1)}, s32[]{:S(2)}) async-start(s8[4718592]{0:T(1024)(128)(4,1)} %bitcast.45), calls=%async_computation | async-start | bytes 8388608
  125.9 5.8 %slice-start.1 = ((s8[4718592]{0:T(1024)(128)(4,1)}), s8[524288]{0:T(1024)(128)(4,1)S(1)}, s32[]{:S(2)}) async-start(s8[4718592]{0:T(1024)(128)(4,1)} %bitcast.45), calls=%async_computation.1 | async-start | bytes 1048576
  134.5 43.0 %copy-start.18 = (f32[512,768]{1,0:T(8,128)}, f32[512,768]{1,0:T(8,128)S(1)}, u32[]{:S(2)}) copy-start(f32[512,768]{1,0:T(8,128)S(1)} %get-tuple-element.86.refs_2_) | copy-start | bytes 4718596
  179.3 6.1 %copy-start.22 = (f32[512,768]{1,0:T(8,128)}, f32[512,768]{1,0:T(8,128)S(1)}, u32[]{:S(2)}) copy-start(f32[512,768]{1,0:T(8,128)S(1)} %get-tuple-element.88.refs_1_) | copy-start | bytes 4718596
  185.4 3.5 copy-start.20
  288.9 118.7 %copy-start.10 = (bf16[96,2304]{1,0:T(8,128)(2,1)S(1)}, bf16[96,2304]{1,0:T(8,128)(2,1)}, u32[]{:S(2)}) copy-start(bf16[96,2304]{1,0:T(8,128)(2,1)} %refs_0_.1) | copy-start | bytes 1327108
  288.9 120.0 %copy-start.34 = (bf16[96]{0:T(256)(128)(2,1)S(1)}, bf16[96]{0:T(256)(128)(2,1)}, u32[]{:S(2)}) copy-start(bf16[96]{0:T(256)(128)(2,1)} %param.14) | copy-start | bytes 580
  406.1 3.3 copy-start.8
  406.2 4.7 %copy-start.36 = (bf16[96]{0:T(256)(128)(2,1)S(1)}, bf16[96]{0:T(256)(128)(2,1)}, u32[]{:S(2)}) copy-start(bf16[96]{0:T(256)(128)(2,1)} %param.15) | copy-start | bytes 580
  406.2 5.3 %copy-start.27 = (f32[512,768]{1,0:T(8,128)S(1)}, f32[512,768]{1,0:T(8,128)}, u32[]{:S(2)}) copy-start(f32[512,768]{1,0:T(8,128)} %get-tuple-element.73) | copy-start | bytes 4718596
  (15 other events, 26.0 us)
